TPU v7x, 512 devices: a whole 4x4x16 slice. The times are simulated.
512 devices in a mesh: seq: 32 (over z, core), dp: 16 (over x, y).
Axes of the slice: x: 4, y: 4, z: 16, core: 2. Of those that a mesh axis runs over, the one named last changes fastest.
Arguments:
- queries: bfloat16 [16, 4096, 2048], P('dp', 'seq'), may hold values from -6 to 6
- key_rows: bfloat16 [16, 4096, 256], P('dp', 'seq'), may hold values from -6 to 6
- value_matrix: bfloat16 [16, 4096, 256], P('dp', 'seq'), may hold values from -6 to 6
- head_sink_logits: float32 [32], replicated, may hold values from 2 to 6
- residual: bfloat16 [16, 4096, 2880], P('dp', 'seq'), may hold values from -6 to 6
- out_weight: bfloat16 [2048, 2880], P('dp'), may hold values from -0.125 to 0.125
- norm_gain: float32 [2880], replicated, may hold values from 0.25 to 1.75
- router: bfloat16 [2880, 128], replicated, may hold values from -0.109375 to 0.109375
- expert_gate: bfloat16 [2880, 4096], P('dp', 'seq'), may hold values from -0.109375 to 0.109375
- expert_up: bfloat16 [2880, 4096], P('dp', 'seq'), may hold values from -0.109375 to 0.109375
- expert_down: bfloat16 [2880, 4096], P('dp', 'seq'), may hold values from -0.125 to 0.125
- routes: int32 [16, 4096, 4], P('dp', 'seq'), may hold values from 0 to 127, as said below
- group_ids: int32 [16], P('dp'), may hold values from 0 to 3, never falling along the last dimension, each value on 1 to 8 neighbouring positions
- rewards: int32 [16], P('dp'), may hold values from 0 to 3
- response_mask: int32 [16, 4096], P('dp', 'seq'), may hold values from 0 to 1, as said below
- upstream: bfloat16 [16, 4096, 2880], P('dp', 'seq'), may hold values from -6 to 6
Outputs:
- grad_queries: bfloat16 [16, 4096, 2048], P('dp', 'seq')
- grad_keys: bfloat16 [16, 4096, 256], P('dp', 'seq')
- grad_values: bfloat16 [16, 4096, 256], P('dp', 'seq')
- grad_residual: bfloat16 [16, 4096, 2880], P('dp', 'seq')
- grad_sinks: float32 [32], replicated
Inputs may be any that keep to these rules, and one draw needn't show every extreme that they name: `routes`: each token names 4 different experts. Among the 128 positions of every aligned block of a rollout at most 4 tokens name a given expert below 2; the first block of the first rollout has exactly 4 for each of them. `group_ids`: the rollouts of one group are adjacent and every group has 1 to 8 rollouts. `response_mask`: in each rollout the ones form one run that starts within the first quarter of the positions and ends within the last quarter.
All inputs are finite; a program needn't handle non-finite values.
Results may differ from a plain program's by a relative error of at most 0.0095.
Values may be sent and summed in bfloat16 or wider, within the bound.
No kernel may reach another device: no remote copies, remote signals or barrier semaphores. Data moves between devices by JAX's collectives and lax.ppermute only.
A program may use at most 128 MiB of HBM per device.

v0:
```python
import jax
import jax.numpy as jnp
from jax import lax
from jax.sharding import PartitionSpec as P

D = 2880
HEAD_SIZE = 64
WINDOW = 128
EXPERTS = 128
QUERY_HEADS = 32
KEY_VALUE_HEADS = 4
EW = 2
CAP = 4


NORM_EPS = 1e-05
GLU_SLOPE = 1.702
HIGHEST = lax.Precision.HIGHEST
CONTRACT_LAST = (((1,), (1,)), ((), ()))


def passed_along(value, axis, steps):
    count = lax.axis_size(axis)
    initial, last = (max(0, -steps), min(count, count - steps))
    return lax.ppermute(value, axis, [(source, source + steps) for source in range(initial, last)])


def glu_forward(gate_pre, up_pre):
    return ((up_pre + 1.0) * gate_pre * jax.nn.sigmoid(GLU_SLOPE * gate_pre)).astype(jnp.bfloat16)


def glu_grads(grad_act, gate_pre, up_pre):
    sigmoid_gate = jax.nn.sigmoid(GLU_SLOPE * gate_pre)
    grad_up = grad_act * (gate_pre * sigmoid_gate)
    grad_gate = (
        grad_act
        * (up_pre + 1.0)
        * (sigmoid_gate + GLU_SLOPE * gate_pre * sigmoid_gate * (1.0 - sigmoid_gate))
    )
    return (grad_gate, grad_up)


def head_scores(query_tile_block, key_tile_block, head_sink_logits, allowed):
    query_total_count = query_tile_block.shape[0]
    key_total_count = key_tile_block.shape[0]
    query_head_rows = query_tile_block.reshape(
        query_total_count, KEY_VALUE_HEADS, QUERY_HEADS // KEY_VALUE_HEADS, HEAD_SIZE
    )
    key_head_rows = key_tile_block.reshape(key_total_count, KEY_VALUE_HEADS, HEAD_SIZE)
    attention_scores = jnp.einsum(
        "baqj,eaj->aqbe", query_head_rows, key_head_rows, preferred_element_type=jnp.float32
    ) * HEAD_SIZE ** (-0.5)
    attention_scores = jnp.where(allowed[None, None], attention_scores, -1e30)
    sink_logit_column = head_sink_logits.reshape(KEY_VALUE_HEADS, QUERY_HEADS // KEY_VALUE_HEADS)[
        :, :, None
    ]
    largest = jnp.maximum(jnp.max(attention_scores, axis=3), sink_logit_column)
    raised = jnp.where(allowed[None, None], jnp.exp(attention_scores - largest[..., None]), 0.0)
    sink_raised = jnp.exp(sink_logit_column - largest)
    denominator = jnp.sum(raised, axis=3) + sink_raised
    return (raised / denominator[..., None], sink_raised / denominator)


def head_mix(reduced_probabilities, value_tile_block):
    key_total_count = value_tile_block.shape[0]
    value_head_rows = value_tile_block.reshape(key_total_count, KEY_VALUE_HEADS, HEAD_SIZE)
    mixed_output = jnp.einsum(
        "amlh,hai->lami", reduced_probabilities, value_head_rows, preferred_element_type=jnp.float32
    )
    return mixed_output.reshape(mixed_output.shape[0], QUERY_HEADS * HEAD_SIZE).astype(jnp.bfloat16)


def head_grads(
    probs,
    reduced_probabilities,
    sink_probs,
    query_tile_block,
    key_tile_block,
    value_tile_block,
    mixed_gradient,
):
    query_total_count = query_tile_block.shape[0]
    key_total_count = key_tile_block.shape[0]
    query_head_rows = query_tile_block.reshape(
        query_total_count, KEY_VALUE_HEADS, QUERY_HEADS // KEY_VALUE_HEADS, HEAD_SIZE
    )
    key_head_rows = key_tile_block.reshape(key_total_count, KEY_VALUE_HEADS, HEAD_SIZE)
    value_head_rows = value_tile_block.reshape(key_total_count, KEY_VALUE_HEADS, HEAD_SIZE)
    heads_gradient = mixed_gradient.reshape(
        query_total_count, KEY_VALUE_HEADS, QUERY_HEADS // KEY_VALUE_HEADS, HEAD_SIZE
    )
    probability_gradient = jnp.einsum(
        "baqj,eaj->aqbe", heads_gradient, value_head_rows, preferred_element_type=jnp.float32
    )
    spread = jnp.sum(probs * probability_gradient, axis=3)
    score_gradient = (probs * (probability_gradient - spread[..., None])).astype(jnp.bfloat16)
    head_scaling = HEAD_SIZE ** (-0.5)
    query_gradient = (
        jnp.einsum(
            "amlh,hai->lami", score_gradient, key_head_rows, preferred_element_type=jnp.float32
        )
        * head_scaling
    )
    key_gradient = (
        jnp.einsum(
            "ujko,kujm->oum", score_gradient, query_head_rows, preferred_element_type=jnp.float32
        )
        * head_scaling
    )
    value_gradient = jnp.einsum(
        "ujko,kujm->oum", reduced_probabilities, heads_gradient, preferred_element_type=jnp.float32
    )
    sink_gradient = -jnp.sum(sink_probs * spread, axis=2).reshape(QUERY_HEADS)
    return (
        query_gradient.reshape(query_total_count, QUERY_HEADS * HEAD_SIZE).astype(jnp.bfloat16),
        key_gradient.reshape(key_total_count, KEY_VALUE_HEADS * HEAD_SIZE),
        value_gradient.reshape(key_total_count, KEY_VALUE_HEADS * HEAD_SIZE),
        sink_gradient,
    )


def block_backward(grad_flat, gate_pre, up_pre, gate_full, up_full, down_full):
    grad_act = jnp.dot(grad_flat, down_full, preferred_element_type=jnp.float32)
    grad_gate, grad_up = glu_grads(grad_act, gate_pre, up_pre)
    grad_pair = jnp.concatenate([grad_gate, grad_up], axis=1).astype(jnp.bfloat16)
    weight_pair = jnp.concatenate([gate_full, up_full], axis=1)
    return lax.dot_general(
        grad_pair, weight_pair, CONTRACT_LAST, preferred_element_type=jnp.float32
    ).astype(jnp.bfloat16)


def shards(
    queries,
    key_rows,
    value_matrix,
    head_sink_logits,
    residual,
    out_weight,
    norm_gain,
    router,
    expert_gate,
    expert_up,
    expert_down,
    routes,
    group_ids,
    rewards,
    response_mask,
    upstream,
):
    seq_count = lax.axis_size("seq")
    dp_count = lax.axis_size("dp")
    seq_index = lax.axis_index("seq")
    query_rows = queries[0]
    own_keys = key_rows[0]
    own_values = value_matrix[0]
    tokens_here = query_rows.shape[0]
    pieces = seq_count // EW
    group_count = max(dp_count // 4, 1)
    all_tokens = dp_count * seq_count * tokens_here
    group_hot = (group_ids[0] == jnp.arange(group_count, dtype=jnp.int32)).astype(jnp.float32)
    reward = rewards[0].astype(jnp.float32)
    group_terms = (
        group_hot[:, None] * jnp.stack([jnp.ones_like(reward), reward, reward * reward])[None, :]
    )
    mask_wide = response_mask[0].astype(jnp.float32)
    local_count = jnp.sum(mask_wide)
    group_totals = lax.psum(group_terms, "dp")
    token_total = lax.psum(local_count, ("seq", "dp"))
    group_sizes = group_totals[:, 0]
    group_means = group_totals[:, 1] / group_sizes
    group_spread = group_totals[:, 2] / group_sizes - group_means * group_means
    own_mean = jnp.sum(group_hot * group_means)
    own_spread = jnp.sum(group_hot * group_spread)
    advantage = (reward - own_mean) / jnp.sqrt(jnp.maximum(own_spread, 1.0))
    token_scale = -advantage * all_tokens / token_total
    loss_weight = token_scale * mask_wide
    halo_keys, halo_values = passed_along((own_keys, own_values), "seq", 1)
    key_tile_block = jnp.concatenate([halo_keys, own_keys], axis=0)
    value_tile_block = jnp.concatenate([halo_values, own_values], axis=0)
    row_index = jnp.arange(tokens_here, dtype=jnp.int32)[:, None]
    col_index = jnp.arange(WINDOW + tokens_here, dtype=jnp.int32)[None, :]
    allowed = (
        (col_index >= row_index + 1)
        & (col_index <= row_index + WINDOW)
        & ((col_index >= WINDOW) | (seq_index > 0))
    )
    probs, sink_probs = head_scores(query_rows, key_tile_block, head_sink_logits, allowed)
    reduced_probabilities = probs.astype(jnp.bfloat16)
    attended = head_mix(reduced_probabilities, value_tile_block)
    out_full = lax.all_gather(out_weight, "dp", axis=0, tiled=True)
    projected = jnp.dot(attended, out_full, preferred_element_type=jnp.float32)
    mid_rows = lax.optimization_barrier(
        (residual[0].astype(jnp.float32) + projected).astype(jnp.bfloat16)
    )
    mid_wide = mid_rows.astype(jnp.float32)
    inv_rms = lax.rsqrt(jnp.mean(mid_wide * mid_wide, axis=1, keepdims=True) + NORM_EPS)
    unit_rows = mid_wide * inv_rms
    normed = (unit_rows * norm_gain[None, :]).astype(jnp.bfloat16)
    logits = jnp.dot(normed, router, preferred_element_type=jnp.float32)
    route_hot = routes[0][:, :, None] == jnp.arange(EXPERTS, dtype=jnp.int32)[None, None, :]
    route_logits = jnp.sum(jnp.where(route_hot, logits[:, None, :], 0.0), axis=2)
    raised = jnp.exp(route_logits)
    route_weights = raised / jnp.sum(raised, axis=1, keepdims=True)
    member = route_hot[:, :, :EW]
    expert_share = jnp.sum(jnp.where(member, route_weights[:, :, None], 0.0), axis=1)
    chosen = jnp.any(member, axis=1)
    slot_rank = jnp.cumsum(chosen.astype(jnp.int32), axis=0) - 1
    slot_hot = chosen[:, :, None] & (
        slot_rank[:, :, None] == jnp.arange(CAP, dtype=jnp.int32)[None, None, :]
    )
    slot_low = slot_hot.astype(jnp.bfloat16)
    slot_wide = slot_hot.astype(jnp.float32)
    slot_rows = jnp.einsum(
        "tec,td->ecd", slot_low, normed, preferred_element_type=jnp.float32
    ).astype(jnp.bfloat16)
    outgoing = jnp.broadcast_to(slot_rows[:, None], (EW, pieces, CAP, D)).reshape(seq_count, CAP, D)
    upstream_slots = jnp.einsum(
        "tec,td->ecd", slot_low, upstream[0], preferred_element_type=jnp.float32
    )
    weight_slots = jnp.einsum("tec,t->ec", slot_wide, loss_weight, precision=HIGHEST)
    share_slots = jnp.einsum("tec,te->ec", slot_wide, expert_share, precision=HIGHEST)
    cot_slots = weight_slots[:, :, None] * upstream_slots
    grad_out = (share_slots[:, :, None] * cot_slots).astype(jnp.bfloat16)
    grad_outgoing = jnp.broadcast_to(grad_out[:, None], (EW, pieces, CAP, D)).reshape(
        seq_count, CAP, D
    )
    gate_full, up_full, down_full = (
        lax.all_gather(expert_gate, "dp", axis=0, tiled=True),
        lax.all_gather(expert_up, "dp", axis=0, tiled=True),
        lax.all_gather(expert_down, "dp", axis=0, tiled=True),
    )
    arrived = lax.all_to_all(outgoing, "seq", split_axis=0, concat_axis=0, tiled=True)
    senders = arrived.shape[0]
    items = arrived.shape[1]
    block_senders = arrived.shape[0]
    block_items = arrived.shape[1]
    flat_rows = arrived.reshape(block_senders * block_items, D)
    gate_pre = jnp.dot(flat_rows, gate_full, preferred_element_type=jnp.float32)
    up_pre = jnp.dot(flat_rows, up_full, preferred_element_type=jnp.float32)
    activation = glu_forward(gate_pre, up_pre)
    partial_out = lax.dot_general(
        activation, down_full, CONTRACT_LAST, preferred_element_type=jnp.float32
    ).astype(jnp.bfloat16)
    partial_out, gate_pre, up_pre = (
        partial_out.reshape(block_senders, block_items, D),
        gate_pre,
        up_pre,
    )
    back_out = lax.all_to_all(partial_out, "seq", split_axis=0, concat_axis=0, tiled=True)
    gate_held = gate_pre.reshape(senders, items, -1)
    up_held = up_pre.reshape(senders, items, -1)
    grad_arrived = lax.all_to_all(grad_outgoing, "seq", split_axis=0, concat_axis=0, tiled=True)
    grad_piece = block_backward(
        grad_arrived.reshape(seq_count * CAP, D),
        gate_held.reshape(seq_count * CAP, -1),
        up_held.reshape(seq_count * CAP, -1),
        gate_full,
        up_full,
        down_full,
    )
    grad_back = lax.all_to_all(
        grad_piece.reshape(seq_count, CAP, D), "seq", split_axis=0, concat_axis=0, tiled=True
    )
    expert_out = jnp.sum(back_out.reshape(EW, pieces, CAP, D).astype(jnp.float32), axis=1)
    grad_share_slots = jnp.sum(cot_slots * expert_out, axis=2)
    grad_rows = jnp.sum(grad_back.reshape(EW, pieces, CAP, D).astype(jnp.float32), axis=1)
    grad_normed_moe = jnp.einsum("tec,ecd->td", slot_wide, grad_rows, precision=HIGHEST)
    grad_share = jnp.einsum("tec,ec->te", slot_wide, grad_share_slots, precision=HIGHEST)
    grad_weights = jnp.sum(jnp.where(member, grad_share[:, None, :], 0.0), axis=2)
    grad_route = route_weights * (
        grad_weights - jnp.sum(route_weights * grad_weights, axis=1, keepdims=True)
    )
    grad_logits = jnp.sum(jnp.where(route_hot, grad_route[:, :, None], 0.0), axis=1).astype(
        jnp.bfloat16
    )
    grad_normed = (
        lax.dot_general(grad_logits, router, CONTRACT_LAST, preferred_element_type=jnp.float32)
        + grad_normed_moe
    )
    grad_unit = grad_normed * norm_gain[None, :]
    grad_mid = loss_weight[:, None] * upstream[0].astype(jnp.float32) + inv_rms * (
        grad_unit - unit_rows * jnp.mean(grad_unit * unit_rows, axis=1, keepdims=True)
    )
    grad_residual = grad_mid.astype(jnp.bfloat16)
    grad_attended = lax.dot_general(
        grad_residual, out_full, CONTRACT_LAST, preferred_element_type=jnp.float32
    ).astype(jnp.bfloat16)
    query_gradient, key_gradient, value_gradient, sink_gradient = head_grads(
        probs,
        reduced_probabilities,
        sink_probs,
        query_rows,
        key_tile_block,
        value_tile_block,
        grad_attended,
    )
    next_keys, next_values = (
        passed_along(key_gradient[:WINDOW].astype(jnp.bfloat16), "seq", -1).astype(jnp.float32),
        passed_along(value_gradient[:WINDOW].astype(jnp.bfloat16), "seq", -1).astype(jnp.float32),
    )
    own_key_grad = key_gradient[WINDOW:]
    own_value_grad = value_gradient[WINDOW:]
    split_at = tokens_here - WINDOW
    grad_key_rows = jnp.concatenate(
        [own_key_grad[:split_at], own_key_grad + next_keys], axis=0
    ).astype(jnp.bfloat16)
    grad_value_rows = jnp.concatenate(
        [own_value_grad[:split_at], own_value_grad + next_values], axis=0
    ).astype(jnp.bfloat16)
    grad_sinks = lax.psum(sink_gradient, ("seq", "dp"))
    return (
        query_gradient[None],
        grad_key_rows[None],
        grad_value_rows[None],
        grad_residual[None],
        grad_sinks,
    )


def solution(mesh):
    return jax.shard_map(
        shards,
        mesh=mesh,
        in_specs=(
            P("dp", "seq", None),
            P("dp", "seq", None),
            P("dp", "seq", None),
            P(),
            P("dp", "seq", None),
            P("dp", None),
            P(),
            P(),
            P("dp", "seq"),
            P("dp", "seq"),
            P("dp", "seq"),
            P("dp", "seq", None),
            P("dp"),
            P("dp"),
            P("dp", "seq"),
            P("dp", "seq", None),
        ),
        out_specs=(
            P("dp", "seq", None),
            P("dp", "seq", None),
            P("dp", "seq", None),
            P("dp", "seq", None),
            P(),
        ),
        check_vma=False,
    )
```

profile of v0, /device:TPU:1, one launch (start us, length us, event | category | flops | bytes accessed | tf_op | source)
XLA Modules:
  0.0 638.6 jit_solution(8633226536649746921)
XLA Ops:
  7.9 4.9 collective-permute-start
  12.8 1.9 collective-permute-start.1
  25.1 99.6 %all-gather.5.cloned.1.call-done = bf16[2048,2880]{0,1:T(8,128)(2,1)} async-done(((bf16[128,2880]{0,1:T(8,128)(2,1)}), bf16[2048,2880]{0,1:T(8,128)(2,1)}) %all-gather.5.cloned.1.call-update) | async-done | bytes 11796496 | tf_op jit(solution)/shard_map/all_gather | solution.py:190
  124.7 7.6 %fusion.5 = bf16[128,2880]{0,1:T(8,128)(2,1)S(1)} fusion(bf16[2048,2880]{0,1:T(8,128)(2,1)} %all-gather.5.cloned.1.call-done, bf16[128,2048]{0,1:T(8,128)(2,1)S(1)} %bitcast.208, bf16[1,128,2880]{1,2,0:T(8,128)(2,1)S(1)} %copy-done.35), kind=kOutput, calls=%fused_computation.14 | convolution fusion | flops 1511055360 | bytes 13795328 | tf_op jit(solution)/shard_map/dot_general | solution.py:191
  134.4 14.4 %all-to-all-start = ((bf16[32,4,2880]{2,1,0:T(4,128)(2,1)}), bf16[32,4,2880]{2,1,0:T(4,128)(2,1)}, u32[]{:S(2)}, u32[]{:S(2)}) async-start(bf16[32,4,2880]{2,1,0:T(4,128)(2,1)} %bitcast.30), calls=%async_computation | async-start | bytes 1507328 | tf_op jit(solution)/shard_map/all_to_all | solution.py:232
  148.8 20.4 %all-gather = bf16[16,180,128]{2,1,0:T(8,128)(2,1)S(1)} all-gather(bf16[1,180,128]{2,1,0:T(8,128)(2,1)S(1)} %bitcast.197), channel_id=1, replica_groups=mesh['seq'=32,'dp'=16] {'dp'}, dimensions={0}, use_global_device_ids=true | all-gather | bytes 783360 | tf_op jit(solution)/shard_map/all_gather | solution.py:229
  170.2 17.8 %all-gather.1 = bf16[16,180,128]{2,1,0:T(8,128)(2,1)S(1)} all-gather(bf16[1,180,128]{2,1,0:T(8,128)(2,1)S(1)} %bitcast.198), channel_id=1, replica_groups=mesh['seq'=32,'dp'=16] {'dp'}, dimensions={0}, use_global_device_ids=true | all-gather | bytes 783360 | tf_op jit(solution)/shard_map/all_gather | solution.py:228
  189.0 18.4 %all-gather.2 = bf16[16,180,128]{2,1,0:T(8,128)(2,1)S(1)} all-gather(bf16[1,180,128]{2,1,0:T(8,128)(2,1)} %bitcast.199), channel_id=1, replica_groups=mesh['seq'=32,'dp'=16] {'dp'}, dimensions={0}, use_global_device_ids=true | all-gather | bytes 783360 | tf_op jit(solution)/shard_map/all_gather | solution.py:230
  207.5 1.6 reshape.259
  216.7 25.3 %all-to-all-start.1 = ((bf16[32,4,2880]{2,1,0:T(4,128)(2,1)}), bf16[32,4,2880]{2,1,0:T(4,128)(2,1)S(1)}, u32[]{:S(2)}, u32[]{:S(2)}) async-start(bf16[32,4,2880]{2,1,0:T(4,128)(2,1)} %reshape.260), calls=%async_computation.1 | async-start | bytes 1507328 | tf_op jit(solution)/shard_map/all_to_all | solution.py:249
  245.3 103.4 %psum.22 = f32[]{:T(128)} all-reduce(f32[]{:T(128)} %convert_reduce_fusion.2), channel_id=1, replica_groups=mesh['seq'=32,'dp'=16] {'seq','dp'}, use_global_device_ids=true, to_apply=%region_6.7 | all-reduce | flops 1 | bytes 8 | tf_op jit(solution)/shard_map/psum | solution.py:168
  348.7 30.5 %psum.21 = f32[4,3]{0,1:T(4,128)} all-reduce(f32[4,3]{0,1:T(4,128)} %broadcast_multiply_fusion), channel_id=1, replica_groups=mesh['seq'=32,'dp'=16] {'dp'}, use_global_device_ids=true, to_apply=%region_2.0 | all-reduce | flops 12 | bytes 96 | tf_op jit(solution)/shard_map/psum | solution.py:167
  384.0 1.6 fusion.29
  393.0 59.8 %all_to_all.20 = bf16[32,4,2880]{2,1,0:T(4,128)(2,1)} all-to-all(bf16[32,4,2880]{2,1,0:T(4,128)(2,1)S(1)} %bitcast.179), channel_id=1, replica_groups=mesh['seq'=32,'dp'=16] {'seq'}, dimensions={0} | all-to-all | bytes 1474560 | tf_op jit(solution)/shard_map/all_to_all | solution.py:252
  455.7 1.9 convolution_convert_fusion.1
  459.0 4.2 all-to-all-start.3
  468.7 37.8 %all-to-all-done.3 = bf16[32,4,2880]{2,1,0:T(4,128)(2,1)S(1)} async-done(((bf16[32,4,2880]{2,1,0:T(4,128)(2,1)}), bf16[32,4,2880]{2,1,0:T(4,128)(2,1)S(1)}, u32[]{:S(2)}, u32[]{:S(2)}) %all-to-all-start.3) | async-done | bytes 737312 | tf_op jit(solution)/shard_map/all_to_all | solution.py:261
  506.8 2.0 convolution_bitcast_fusion
  510.7 6.5 %convolution_convert_fusion.3 = bf16[128,2048]{1,0:T(8,128)(2,1)S(1)} fusion(bf16[128,2880]{0,1:T(8,128)(2,1)S(1)} %fusion.16, bf16[2048,2880]{0,1:T(8,128)(2,1)} %all-gather.5.cloned.1.call-done), kind=kOutput, calls=%fused_computation.19 | convolution fusion | flops 1510211584 | bytes 13058048 | tf_op jit(solution)/shard_map/dot_general | solution.py:285
  517.5 3.8 fusion
  521.4 1.7 fusion.2
  526.7 2.8 collective-permute-start.2
  529.9 1.9 collective-permute-start.3
  531.9 98.3 %psum.23 = f32[32]{0:T(128)} all-reduce(f32[32]{0:T(128)S(1)} %neg.16), channel_id=1, replica_groups=mesh['seq'=32,'dp'=16] {'seq','dp'}, use_global_device_ids=true, to_apply=%region_22.23 | all-reduce | flops 32 | bytes 256 | tf_op jit(solution)/shard_map/psum | solution.py:310
  (161 shorter events, 52.6 us)
Async XLA Ops:
  7.2 376.8 %copy-start = (bf16[2880,128]{1,0:T(8,128)(2,1)S(1)}, bf16[2880,128]{1,0:T(8,128)(2,1)}, u32[]{:S(2)}) copy-start(bf16[2880,128]{1,0:T(8,128)(2,1)} %param.23) | copy-start | bytes 2211844
  7.2 117.5 %all-gather.5.cloned.1.call-start = ((), (), s32[]{:S(2)}) async-start(), calls=%async_computation.4 | async-start | bytes 12533760 | tf_op jit(solution)/shard_map/all_gather | solution.py:190
  7.9 12.8 %collective-permute-start = (bf16[128,256]{1,0:T(8,128)(2,1)}, bf16[128,256]{1,0:T(8,128)(2,1)S(1)}, u32[]{:S(2)}, u32[]{:S(2)}) collective-permute-start(bf16[128,256]{1,0:T(8,128)(2,1)} %bitcast.191), channel_id=1, source_target_pairs={{0,16},{16,32},{32,48},{48,64},{64,80},{80,96},{96,112},{112,128},... | collective-permute-start | bytes 196616 | tf_op jit(solution)/shard_map/ppermute | solution.py:25
  12.8 8.0 %collective-permute-start.1 = (bf16[128,256]{1,0:T(8,128)(2,1)}, bf16[128,256]{1,0:T(8,128)(2,1)S(1)}, u32[]{:S(2)}, u32[]{:S(2)}) collective-permute-start(bf16[128,256]{1,0:T(8,128)(2,1)} %bitcast.192), channel_id=1, source_target_pairs={{0,16},{16,32},{32,48},{48,64},{64,80},{80,96},{96,112},{112,128},... | collective-permute-start | bytes 196616 | tf_op jit(solution)/shard_map/ppermute | solution.py:25
  16.7 6.4 copy-start.9
  16.7 116.0 %copy-start.30 = (pred[128,2,4]{0,2,1:T(4,128)(4,1)}, pred[128,2,4]{0,2,1:T(4,128)(4,1)S(1)}, u32[]{:S(2)}) copy-start(pred[128,2,4]{0,2,1:T(4,128)(4,1)S(1)} %fusion.44) | copy-start | bytes 3076
  23.8 100.9 %copy-start.35 = (bf16[1,128,2880]{1,2,0:T(8,128)(2,1)S(1)}, bf16[1,128,2880]{1,2,0:T(8,128)(2,1)}, u32[]{:S(2)}) copy-start(bf16[1,128,2880]{1,2,0:T(8,128)(2,1)} %param.20) | copy-start | bytes 2211844
  124.7 8.0 %copy-start.29 = (f32[2880]{0:T(1024)S(1)}, f32[2880]{0:T(1024)}, u32[]{:S(2)}) copy-start(f32[2880]{0:T(1024)} %param.22) | copy-start | bytes 34564
  132.3 16.5 %copy-start.25 = (bf16[180,128]{1,0:T(8,128)(2,1)S(1)}, bf16[180,128]{1,0:T(8,128)(2,1)}, u32[]{:S(2)}) copy-start(bf16[180,128]{1,0:T(8,128)(2,1)} %param.25) | copy-start | bytes 138244
  132.3 37.9 %copy-start.26 = (bf16[180,128]{1,0:T(8,128)(2,1)S(1)}, bf16[180,128]{1,0:T(8,128)(2,1)}, u32[]{:S(2)}) copy-start(bf16[180,128]{1,0:T(8,128)(2,1)} %param.24) | copy-start | bytes 138244
  132.7 56.2 %copy-start.32 = (f32[128]{0:T(128)}, f32[128]{0:T(128)S(1)}, u32[]{:S(2)}) copy-start(f32[128]{0:T(128)S(1)} %add_rsqrt_fusion) | copy-start | bytes 1540
  134.4 73.1 %all-to-all-start = ((bf16[32,4,2880]{2,1,0:T(4,128)(2,1)}), bf16[32,4,2880]{2,1,0:T(4,128)(2,1)}, u32[]{:S(2)}, u32[]{:S(2)}) async-start(bf16[32,4,2880]{2,1,0:T(4,128)(2,1)} %bitcast.30), calls=%async_computation | async-start | bytes 1507328 | tf_op jit(solution)/shard_map/all_to_all | solution.py:232
  216.7 171.4 %all-to-all-start.1 = ((bf16[32,4,2880]{2,1,0:T(4,128)(2,1)}), bf16[32,4,2880]{2,1,0:T(4,128)(2,1)S(1)}, u32[]{:S(2)}, u32[]{:S(2)}) async-start(bf16[32,4,2880]{2,1,0:T(4,128)(2,1)} %reshape.260), calls=%async_computation.1 | async-start | bytes 1507328 | tf_op jit(solution)/shard_map/all_to_all | solution.py:249
  459.0 51.2 %copy-start.4 = (bf16[1,128,2880]{1,2,0:T(8,128)(2,1)S(1)}, bf16[1,128,2880]{1,2,0:T(8,128)(2,1)}, u32[]{:S(2)}) copy-start(bf16[1,128,2880]{1,2,0:T(8,128)(2,1)} %param.31) | copy-start | bytes 2211844
  459.0 47.5 %all-to-all-start.3 = ((bf16[32,4,2880]{2,1,0:T(4,128)(2,1)}), bf16[32,4,2880]{2,1,0:T(4,128)(2,1)S(1)}, u32[]{:S(2)}, u32[]{:S(2)}) async-start(bf16[32,4,2880]{2,1,0:T(4,128)(2,1)} %reshape.263), calls=%async_computation.3 | async-start | bytes 1507328 | tf_op jit(solution)/shard_map/all_to_all | solution.py:261
  510.6 6.6 %copy-start.3 = (bf16[128,2880]{0,1:T(8,128)(2,1)}, bf16[128,2880]{0,1:T(8,128)(2,1)S(1)}, u32[]{:S(2)}) copy-start(bf16[128,2880]{0,1:T(8,128)(2,1)S(1)} %fusion.16) | copy-start | bytes 2211844
  510.6 6.8 %copy-start.10 = (pred[128,256]{0,1:T(8,128)(4,1)S(1)}, pred[128,256]{0,1:T(8,128)(4,1)}, u32[]{:S(2)}) copy-start(pred[128,256]{0,1:T(8,128)(4,1)} %copy-done.9) | copy-start | bytes 98308
  510.7 6.8 %copy-start.14 = (f32[4,8,128]{2,1,0:T(8,128)S(1)}, f32[4,8,128]{2,1,0:T(8,128)}, u32[]{:S(2)}) copy-start(f32[4,8,128]{2,1,0:T(8,128)} %copy-done.13) | copy-start | bytes 49156
  510.7 6.8 %copy-start.19 = (f32[4,8,128]{2,1,0:T(8,128)S(1)}, f32[4,8,128]{2,1,0:T(8,128)}, u32[]{:S(2)}) copy-start(f32[4,8,128]{2,1,0:T(8,128)} %copy-done.18) | copy-start | bytes 49156
  510.7 6.8 %copy-start.21 = (bf16[1,128,256]{1,2,0:T(8,128)(2,1)S(1)}, bf16[1,128,256]{1,2,0:T(8,128)(2,1)}, u32[]{:S(2)}) copy-start(bf16[1,128,256]{1,2,0:T(8,128)(2,1)} %copy-done.20) | copy-start | bytes 196612
  510.7 6.8 %copy-start.23 = (bf16[128,256]{0,1:T(8,128)(2,1)S(1)}, bf16[128,256]{0,1:T(8,128)(2,1)}, u32[]{:S(2)}) copy-start(bf16[128,256]{0,1:T(8,128)(2,1)} %copy-done.22) | copy-start | bytes 196612
  524.3 5.4 copy-start.16
  526.7 103.7 %collective-permute-start.2 = (bf16[128,256]{1,0:T(8,128)(2,1)S(1)}, bf16[128,256]{1,0:T(8,128)(2,1)S(1)}, u32[]{:S(2)}, u32[]{:S(2)}) collective-permute-start(bf16[128,256]{1,0:T(8,128)(2,1)S(1)} %copy.97), channel_id=1, source_target_pairs={{16,0},{32,16},{48,32},{64,48},{80,64},{96,80},{112,96},{128,112},... | collective-permute-start | bytes 196616 | tf_op jit(solution)/shard_map/ppermute | solution.py:25
  529.9 101.1 %collective-permute-start.3 = (bf16[128,256]{1,0:T(8,128)(2,1)S(1)}, bf16[128,256]{1,0:T(8,128)(2,1)S(1)}, u32[]{:S(2)}, u32[]{:S(2)}) collective-permute-start(bf16[128,256]{1,0:T(8,128)(2,1)S(1)} %copy.100), channel_id=1, source_target_pairs={{16,0},{32,16},{48,32},{64,48},{80,64},{96,80},{112,96},{128,112},... | collective-permute-start | bytes 196616 | tf_op jit(solution)/shard_map/ppermute | solution.py:25
  (20 other events, 51.2 us)
Sparse Core Ops, SparseCore 0:
  11.0 113.6 all-gather.4
where the time goes:
time: 640 us; the launch traced here: 639 us
  blocking collectives  349 us (55%)
  waiting for transfers between devices  138 us (22%)
  starting transfers between devices  55.6 us (9%)
  matrix products  39.8 us (6%)
  local copies, waits for them, and re-layouts  21.4 us (3%)
  between operations  18.1 us (3%)
  other arithmetic  17.2 us (3%)
    psum x1, blocking collectives, shards(): token_total = lax.psum(local_count, ('seq', 'dp'))  103 us
    all_gather x1, waiting for transfers between devices, shards(): out_full = lax.all_gather(out_weight, 'dp', axis=0, tiled=True)  99.6 us
    psum x1, blocking collectives, shards(): grad_sinks = lax.psum(sink_gradient, ('seq', 'dp'))  98.3 us
    all_to_all x1, blocking collectives, shards(): lax.all_to_all(grad_outgoing, 'seq', split_axis=0, concat_axis=0, tiled=T...  59.8 us
    all_to_all x1, waiting for transfers between devices, shards(): lax.all_to_all(grad_piece.reshape(seq_count, CAP, D), 'seq', split_axis=0...  37.8 us
    psum x1, blocking collectives, shards(): group_totals = lax.psum(group_terms, 'dp')  30.5 us
    all_to_all x1, starting transfers between devices, shards(): lax.all_to_all(partial_out, 'seq', split_axis=0, concat_axis=0, tiled=True)  25.3 us
    all_gather x1, blocking collectives, shards(): lax.all_gather(expert_up, 'dp', axis=0, tiled=True)  20.4 us
  transfers between devices with their start and end apart: 8, of which 2 were waited for; matrix products, arithmetic and copies ran while one was open for 4% of the time, Pallas kernels for 0%

commit v1 on v0

v1 whole, which is shorter than its diff:
```python
import jax
import jax.numpy as jnp
from jax import lax
from jax.sharding import Mesh, PartitionSpec as P

D = 2880
PADDED = 2944
HEAD_SIZE = 64
WINDOW = 128
EXPERTS = 128
QUERY_HEADS = 32
KEY_VALUE_HEADS = 4
EW = 2
CAP = 4
SLOTS = EW * CAP

NORM_EPS = 1e-05
GLU_SLOPE = 1.702
HIGHEST = lax.Precision.HIGHEST
CONTRACT_LAST = (((1,), (1,)), ((), ()))
F32 = jnp.float32
BF16 = jnp.bfloat16


def dot32(a, b, **kw):
    return jnp.dot(a, b, preferred_element_type=F32, **kw)


def dot_last(a, b):
    return lax.dot_general(a, b, CONTRACT_LAST, preferred_element_type=F32)


def exchange(value, axis):
    return lax.all_to_all(value, axis, split_axis=0, concat_axis=0, tiled=True)


def to_all(value, axis):
    count = lax.axis_size(axis)
    return exchange(jnp.broadcast_to(value[None], (count, *value.shape)), axis)


def swap_cores(value):
    return lax.ppermute(value, "core", [(0, 1), (1, 0)])


def along_seq(value, steps):
    chips, cores = lax.axis_size("z"), lax.axis_size("core")
    count = chips * cores
    first, last = max(0, -steps), min(count, count - steps)
    return lax.ppermute(value, ("z", "core"), [(i, i + steps) for i in range(first, last)])


def head_scores(query_rows, key_rows, sinks, allowed):
    tokens, keys = query_rows.shape[0], key_rows.shape[0]
    per_group = QUERY_HEADS // KEY_VALUE_HEADS
    q = query_rows.reshape(tokens, KEY_VALUE_HEADS, per_group, HEAD_SIZE)
    k = key_rows.reshape(keys, KEY_VALUE_HEADS, HEAD_SIZE)
    scores = jnp.einsum("baqj,eaj->aqbe", q, k, preferred_element_type=F32) * HEAD_SIZE**-0.5
    scores = jnp.where(allowed[None, None], scores, -1e30)
    sink_column = sinks.reshape(KEY_VALUE_HEADS, per_group)[:, :, None]
    largest = jnp.maximum(jnp.max(scores, axis=3), sink_column)
    raised = jnp.where(allowed[None, None], jnp.exp(scores - largest[..., None]), 0.0)
    sink_raised = jnp.exp(sink_column - largest)
    denominator = jnp.sum(raised, axis=3) + sink_raised
    return raised / denominator[..., None], sink_raised / denominator


def head_mix(probs_low, value_rows):
    v = value_rows.reshape(value_rows.shape[0], KEY_VALUE_HEADS, HEAD_SIZE)
    mixed = jnp.einsum("amlh,hai->lami", probs_low, v, preferred_element_type=F32)
    return mixed.reshape(mixed.shape[0], QUERY_HEADS * HEAD_SIZE).astype(BF16)


def head_grads(probs, probs_low, sink_probs, query_rows, key_rows, value_rows, grad_attended):
    tokens, keys = query_rows.shape[0], key_rows.shape[0]
    per_group = QUERY_HEADS // KEY_VALUE_HEADS
    q = query_rows.reshape(tokens, KEY_VALUE_HEADS, per_group, HEAD_SIZE)
    k = key_rows.reshape(keys, KEY_VALUE_HEADS, HEAD_SIZE)
    v = value_rows.reshape(keys, KEY_VALUE_HEADS, HEAD_SIZE)
    g = grad_attended.reshape(tokens, KEY_VALUE_HEADS, per_group, HEAD_SIZE)
    grad_prob = jnp.einsum("baqj,eaj->aqbe", g, v, preferred_element_type=F32)
    spread = jnp.sum(probs * grad_prob, axis=3)
    grad_score = (probs * (grad_prob - spread[..., None])).astype(BF16)
    scaling = HEAD_SIZE**-0.5
    grad_q = jnp.einsum("amlh,hai->lami", grad_score, k, preferred_element_type=F32) * scaling
    grad_k = jnp.einsum("ujko,kujm->oum", grad_score, q, preferred_element_type=F32) * scaling
    grad_v = jnp.einsum("ujko,kujm->oum", probs_low, g, preferred_element_type=F32)
    grad_sinks = -jnp.sum(sink_probs * spread, axis=2).reshape(QUERY_HEADS)
    return (
        grad_q.reshape(tokens, QUERY_HEADS * HEAD_SIZE).astype(BF16),
        grad_k.reshape(keys, KEY_VALUE_HEADS * HEAD_SIZE),
        grad_v.reshape(keys, KEY_VALUE_HEADS * HEAD_SIZE),
        grad_sinks,
    )


def shards(
    queries,
    key_rows,
    value_matrix,
    head_sink_logits,
    residual,
    out_weight,
    norm_gain,
    router,
    expert_gate,
    expert_up,
    expert_down,
    routes,
    group_ids,
    rewards,
    response_mask,
    upstream,
):
    chips, cores, dp_count = lax.axis_size("z"), lax.axis_size("core"), lax.axis_size("dp")
    core = lax.axis_index("core")
    seq_index = lax.axis_index("z") * cores + core
    query_rows = queries[0]
    tokens = query_rows.shape[0]
    group_count = max(dp_count // 4, 1)
    all_tokens = dp_count * chips * cores * tokens
    half = D // 2
    lanes = out_weight.shape[0]

    route_rows = routes[0]
    window = jnp.arange(EW, dtype=jnp.int32)
    chosen = jnp.any(route_rows[:, :, None] == window, axis=1)
    below = jnp.arange(tokens)[:, None] >= jnp.arange(tokens)[None, :]
    rank = dot32(below.astype(BF16), chosen.astype(BF16)) - 1.0
    slot_hot = chosen.T[:, None, :] & (
        rank.T[:, None, :] == jnp.arange(CAP, dtype=F32)[None, :, None]
    )
    pick = slot_hot.reshape(SLOTS, tokens)
    pick_low = pick.astype(BF16)
    slot_expert = jnp.repeat(window, CAP)
    upstream_slots = dot32(pick_low, upstream[0]).astype(BF16)
    residual_slots = dot32(pick_low, residual[0])

    shard = jnp.stack([expert_gate, expert_up, expert_down])
    gathered = to_all(shard, "dp")
    own_block = jnp.concatenate([gathered[:, i].reshape(D, -1) for i in range(3)], axis=1)
    other_block = swap_cores(own_block)
    hid = expert_gate.shape[1]

    by_expert = upstream_slots.reshape(EW, 1, CAP, D)
    outgoing = jnp.broadcast_to(by_expert, (EW, chips // EW, CAP, D)).reshape(chips, CAP, D)
    up_rows = exchange(outgoing, "z").reshape(chips * CAP, D)

    halo = along_seq(jnp.concatenate([key_rows[0], value_matrix[0]], axis=1), 1)
    kv_width = key_rows.shape[2]
    keys_here = jnp.concatenate([halo[:, :kv_width], key_rows[0]], axis=0)
    values_here = jnp.concatenate([halo[:, kv_width:], value_matrix[0]], axis=0)
    row_index = jnp.arange(tokens, dtype=jnp.int32)[:, None]
    col_index = jnp.arange(WINDOW + tokens, dtype=jnp.int32)[None, :]
    allowed = (
        (col_index >= row_index + 1)
        & (col_index <= row_index + WINDOW)
        & ((col_index >= WINDOW) | (seq_index > 0))
    )
    probs, sink_probs = head_scores(query_rows, keys_here, head_sink_logits, allowed)
    probs_low = probs.astype(BF16)
    attended = head_mix(probs_low, values_here)
    attended_slots = dot32(pick_low, attended).astype(BF16)

    mask_wide = response_mask[0].astype(F32)
    facts = jnp.stack(
        [
            jnp.sum(mask_wide),
            rewards[0].astype(F32),
            group_ids[0].astype(F32),
        ]
    )
    facts_row = jnp.pad(facts, (0, lanes - 3))[None].astype(BF16)
    columns = attended_slots.reshape(SLOTS, dp_count, lanes).transpose(1, 0, 2)
    sent = jnp.concatenate(
        [columns, jnp.broadcast_to(facts_row[None], (dp_count, 1, lanes))], axis=1
    )
    sent = jnp.pad(sent, ((0, 0), (0, 2 * SLOTS - SLOTS - 1), (0, 0)))
    arrived = exchange(sent, "dp")
    facts_all = arrived[:, SLOTS, :3].astype(F32)
    partial = dot32(arrived[:, :SLOTS].reshape(dp_count * SLOTS, lanes), out_weight)
    partial = exchange(partial.astype(BF16).reshape(dp_count, SLOTS, D), "dp")
    projected = jnp.sum(partial.astype(F32), axis=0)

    own_half = lax.dynamic_slice_in_dim(out_weight, core * half, half, axis=1)
    own_out = to_all(own_half, "dp").reshape(dp_count * lanes, half)
    other_out = swap_cores(own_out)

    mid = (residual_slots + projected).astype(BF16)
    mid_wide = lax.optimization_barrier(mid).astype(F32)
    inv_rms = lax.rsqrt(jnp.mean(mid_wide * mid_wide, axis=1, keepdims=True) + NORM_EPS)
    unit_rows = mid_wide * inv_rms
    normed = (unit_rows * norm_gain[None, :]).astype(BF16)

    counts_here = jnp.sum(facts_all[:, 0])
    group_hot = (facts_all[:, 2][:, None] == jnp.arange(group_count, dtype=F32)).astype(F32)
    reward_all = facts_all[:, 1]
    group_sizes = jnp.sum(group_hot, axis=0)
    group_sums = jnp.sum(group_hot * reward_all[:, None], axis=0)
    group_squares = jnp.sum(group_hot * (reward_all * reward_all)[:, None], axis=0)
    own_hot = (group_ids[0] == jnp.arange(group_count, dtype=jnp.int32)).astype(F32)
    means = group_sums / group_sizes
    spreads = group_squares / group_sizes - means * means
    own_mean = jnp.sum(jnp.where(own_hot > 0, means, 0.0))
    own_spread = jnp.sum(jnp.where(own_hot > 0, spreads, 0.0))
    advantage = (rewards[0].astype(F32) - own_mean) / jnp.sqrt(jnp.maximum(own_spread, 1.0))

    count_high = jnp.floor(counts_here / 64.0)
    count_tail = jnp.stack([count_high, counts_here - 64.0 * count_high])
    count_tail = jnp.pad(count_tail, (0, PADDED - D - 2)).astype(BF16)
    with_tail = jnp.concatenate(
        [normed, jnp.broadcast_to(count_tail[None], (SLOTS, PADDED - D))], axis=1
    )
    by_expert = with_tail.reshape(EW, 1, CAP, PADDED)
    outgoing = jnp.broadcast_to(by_expert, (EW, chips // EW, CAP, PADDED))
    came = exchange(outgoing.reshape(chips, CAP, PADDED), "z")
    count_parts = jnp.sum(came[:, 0, D : D + 2].astype(F32), axis=0)
    core_count = count_parts[0] * 64.0 + count_parts[1]
    token_total = core_count + swap_cores(jnp.full((8, 128), core_count))[0, 0]
    token_scale = -advantage * all_tokens / token_total
    loss_weight = token_scale * mask_wide

    rows = came.reshape(chips * CAP, PADDED)[:, :D]
    pieces = []
    shares = 0.0
    grads = []
    for block in (own_block, other_block):
        pre = dot32(rows, block[:, : 2 * hid])
        up_down = dot32(up_rows, block[:, 2 * hid :])
        gate_pre, up_pre = pre[:, :hid], pre[:, hid:]
        sigmoid_gate = jax.nn.sigmoid(GLU_SLOPE * gate_pre)
        activation = ((up_pre + 1.0) * gate_pre * sigmoid_gate).astype(BF16)
        shares = shares + jnp.sum(activation.astype(F32) * up_down, axis=1)
        grad_up = up_down * (gate_pre * sigmoid_gate)
        grad_gate = (
            up_down
            * (up_pre + 1.0)
            * (sigmoid_gate + GLU_SLOPE * gate_pre * sigmoid_gate * (1.0 - sigmoid_gate))
        )
        grads.append(jnp.concatenate([grad_gate, grad_up], axis=1).astype(BF16))
    piece = dot_last(grads[0], own_block[:, : 2 * hid]) + dot_last(grads[1], other_block[:, : 2 * hid])
    share_1 = shares.astype(BF16).astype(F32)
    share_2 = (shares - share_1).astype(BF16).astype(F32)
    share_3 = shares - share_1 - share_2
    tail = jnp.pad(jnp.stack([share_1, share_2, share_3], axis=1), ((0, 0), (0, PADDED - D - 3)))
    back = jnp.concatenate([piece, tail], axis=1).astype(BF16)
    back = exchange(back.reshape(chips, CAP, PADDED), "z")
    summed = jnp.sum(back.reshape(EW, chips // EW, CAP, PADDED).astype(F32), axis=1)
    summed = summed.reshape(SLOTS, PADDED)
    share_slots = jnp.sum(summed[:, D : D + 3], axis=1)

    logits = dot32(normed, router)
    route_slots = dot32(pick_low, route_rows.astype(BF16)).astype(jnp.int32)
    route_hot = route_slots[:, :, None] == jnp.arange(EXPERTS, dtype=jnp.int32)
    route_logits = jnp.sum(jnp.where(route_hot, logits[:, None, :], 0.0), axis=2)
    raised = jnp.exp(route_logits)
    route_weights = raised / jnp.sum(raised, axis=1, keepdims=True)
    weight_slots = jnp.sum(
        jnp.where(route_slots == slot_expert[:, None], route_weights, 0.0), axis=1
    )
    loss_slots = jnp.sum(jnp.where(pick, loss_weight[None, :], 0.0), axis=1)
    same = dot_last(pick_low, pick_low)
    grad_rows = (weight_slots * loss_slots)[:, None] * summed[:, :D]
    grad_rows = dot32(same, grad_rows, precision=HIGHEST)
    grad_share = loss_slots * share_slots
    token_share = jnp.sum(
        same[:, :, None] * (grad_share[:, None] * (slot_expert[:, None] == window))[None], axis=1
    )
    grad_weights = jnp.sum(
        jnp.where(route_slots[:, :, None] == window, token_share[:, None, :], 0.0), axis=2
    )
    grad_route = route_weights * (
        grad_weights - jnp.sum(route_weights * grad_weights, axis=1, keepdims=True)
    )
    grad_logits = jnp.sum(jnp.where(route_hot, grad_route[:, :, None], 0.0), axis=1).astype(BF16)
    grad_normed = dot_last(grad_logits, router) + grad_rows
    grad_unit = grad_normed * norm_gain[None, :]
    norm_grad = inv_rms * (
        grad_unit - unit_rows * jnp.mean(grad_unit * unit_rows, axis=1, keepdims=True)
    )
    earlier = jnp.tril(same, -1)
    primary = jnp.sum(earlier, axis=1) == 0
    place = jnp.where(primary[:, None], pick.astype(F32), 0.0)
    norm_part = lax.dot_general(
        place, norm_grad, (((0,), (0,)), ((), ())), precision=HIGHEST, preferred_element_type=F32
    )
    grad_residual = (loss_weight[:, None] * upstream[0].astype(F32) + norm_part).astype(BF16)

    grad_own = lax.dynamic_slice_in_dim(grad_residual, core * half, half, axis=1)
    grad_other = lax.dynamic_slice_in_dim(grad_residual, (1 - core) * half, half, axis=1)
    grad_attended = (dot_last(grad_own, own_out) + dot_last(grad_other, other_out)).astype(BF16)
    grad_q, grad_k, grad_v, grad_sinks = head_grads(
        probs, probs_low, sink_probs, query_rows, keys_here, values_here, grad_attended
    )
    sinks = jnp.pad(grad_sinks, (0, 128 - QUERY_HEADS))[None]
    sinks = jnp.sum(to_all(sinks, "dp"), axis=0)
    sinks = jnp.sum(to_all(sinks, "z"), axis=0)
    sinks = sinks + swap_cores(sinks)
    onward = jnp.concatenate([grad_k[:WINDOW], grad_v[:WINDOW]], axis=1).astype(BF16)
    onward = along_seq(onward, -1).astype(F32)
    grad_key_rows = (grad_k[WINDOW:] + onward[:, :kv_width]).astype(BF16)
    grad_value_rows = (grad_v[WINDOW:] + onward[:, kv_width:]).astype(BF16)
    return (
        grad_q[None],
        grad_key_rows[None],
        grad_value_rows[None],
        grad_residual[None],
        sinks[0, :QUERY_HEADS],
    )


def solution(mesh):
    seq, dp = mesh.shape["seq"], mesh.shape["dp"]
    split = Mesh(mesh.devices.reshape(seq // 2, 2, dp), ("z", "core", "dp"))
    whole = ("z", "core")
    return jax.shard_map(
        shards,
        mesh=split,
        in_specs=(
            P("dp", whole, None),
            P("dp", whole, None),
            P("dp", whole, None),
            P(),
            P("dp", whole, None),
            P("dp", None),
            P(),
            P(),
            P("dp", whole),
            P("dp", whole),
            P("dp", whole),
            P("dp", whole, None),
            P("dp"),
            P("dp"),
            P("dp", whole),
            P("dp", whole, None),
        ),
        out_specs=(
            P("dp", whole, None),
            P("dp", whole, None),
            P("dp", whole, None),
            P("dp", whole, None),
            P(),
        ),
        check_vma=False,
    )
```

time: 640 us -> 371 us (0.58)
  blocking collectives: 349 us -> 13.2 us
  starting transfers between devices: 55.6 us -> 130 us
  local copies, waits for them, and re-layouts: 21.4 us -> 47 us
  waiting for transfers between devices: 138 us -> 119 us
  between operations: 18.1 us -> 7.91 us
    psum x3 -> x0, blocking collectives: 232 us -> none  [the longest x1 103 us: shards(): token_total = lax.psum(local_count, ('seq', 'dp'))]
    all_gather x1 -> x0, waiting for transfers between devices: 99.6 us -> none  [shards(): out_full = lax.all_gather(out_weight, 'dp', axis=0, tiled=True)]
    all_to_all x3 -> x8, waiting for transfers between devices: 37.8 us -> 115 us  [exchange(): return lax.all_to_all(value, axis, split_axis=0, concat_axis=0, tiled=True)]
    all_gather x3 -> x0, blocking collectives: 56.5 us -> none  [the longest x1 20.4 us: shards(): lax.all_gather(expert_up, 'dp', axis=0, tiled=True)]
    all_to_all x3 -> x8, starting transfers between devices: 43.9 us -> 99.2 us  [exchange(): return lax.all_to_all(value, axis, split_axis=0, concat_axis=0, tiled=True)]
    all_to_all x1, blocking collectives: 59.8 us -> 13.2 us  [exchange(): return lax.all_to_all(value, axis, split_axis=0, concat_axis=0, tiled=True)]
    ppermute x4 -> x6, starting transfers between devices: 11.6 us -> 30.3 us  [the longest x4 23.4 us: swap_cores(): return lax.ppermute(value, 'core', [(0, 1), (1, 0)])]
    broadcast_in_dim x2 -> x11, local copies, waits for them, and re-layouts: 1.28 us -> 11.1 us  [the longest x4 7.2 us: to_all(): return exchange(jnp.broadcast_to(value[None], (count, *value.shape)), axis)]
  transfers between devices with their start and end apart: 8 -> 14, of which waited for: 2 -> 10; matrix products, arithmetic and copies ran while one was open for 4% -> 19% of each run, Pallas kernels for 0% -> 0%
where the time goes in v1:
time: 371 us; the launch traced here: 369 us
  starting transfers between devices  130 us (35%)
  waiting for transfers between devices  119 us (32%)
  local copies, waits for them, and re-layouts  47 us (13%)
  matrix products  34.2 us (9%)
  other arithmetic  17.8 us (5%)
  blocking collectives  13.2 us (4%)
  between operations  7.91 us (2%)
    all_to_all x8, waiting for transfers between devices, exchange(): return lax.all_to_all(value, axis, split_axis=0, concat_axis=0, tiled=True)  115 us
    all_to_all x8, starting transfers between devices, exchange(): return lax.all_to_all(value, axis, split_axis=0, concat_axis=0, tiled=True)  99.2 us
    ppermute x4, starting transfers between devices, swap_cores(): return lax.ppermute(value, 'core', [(0, 1), (1, 0)])  23.4 us
    all_to_all x1, blocking collectives, exchange(): return lax.all_to_all(value, axis, split_axis=0, concat_axis=0, tiled=True)  13.2 us
    dot_general x6, matrix products, dot_last(): return lax.dot_general(a, b, CONTRACT_LAST, preferred_element_type=F32)  12 us
    dot_general x12, matrix products, dot32(): return jnp.dot(a, b, preferred_element_type=F32, **kw)  8.97 us
    unnamed x125, local copies, waits for them, and re-layouts  7.72 us
  transfers between devices with their start and end apart: 14, of which 10 were waited for; matrix products, arithmetic and copies ran while one was open for 19% of the time, Pallas kernels for 0%

profile of v1, /device:TPU:1, one launch (start us, length us, event | category | flops | bytes accessed | tf_op | source)
XLA Modules:
  0.0 368.8 jit_solution(12856634317959720086)
XLA Ops:
  1.6 4.9 %collective-permute-start = (bf16[128,512]{1,0:T(8,128)(2,1)S(1)}, bf16[128,512]{1,0:T(8,128)(2,1)S(1)}, u32[]{:S(2)}, u32[]{:S(2)}) collective-permute-start(bf16[128,512]{1,0:T(8,128)(2,1)S(1)} %pad_maximum_fusion.3), channel_id=1, source_target_pairs={{0,16},{16,32},{32,48},{48,64},{64,80},{80,96},{96,112},{112,128},... | collective-permute-start | bytes 393224 | tf_op jit(solution)/shard_map/ppermute | solution.py:50
  19.0 13.2 %all_to_all.45 = bf16[16,16,128]{2,1,0:T(8,128)(2,1)S(1)} all-to-all(bf16[16,16,128]{2,1,0:T(8,128)(2,1)S(1)} %pad.24), channel_id=1, replica_groups=mesh['z'=16,'core'=2,'dp'=16] {'dp'}, dimensions={0} | all-to-all | bytes 131072 | tf_op jit(solution)/shard_map/all_to_all | solution.py:34
  39.7 10.6 %all-to-all-done.1 = bf16[16,8,2880]{2,1,0:T(8,128)(2,1)S(1)} async-done(((bf16[16,8,2880]{2,1,0:T(8,128)(2,1)}), bf16[16,8,2880]{2,1,0:T(8,128)(2,1)S(1)}, u32[]{:S(2)}, u32[]{:S(2)}) %all-to-all-start.1) | async-done | bytes 737312 | tf_op jit(solution)/shard_map/all_to_all | solution.py:34
  51.1 14.8 %all-to-all-start.3 = ((bf16[16,4,2880]{2,1,0:T(4,128)(2,1)}), bf16[16,4,2880]{2,1,0:T(4,128)(2,1)S(1)}, u32[]{:S(2)}, u32[]{:S(2)}) async-start(bf16[16,4,2880]{2,1,0:T(4,128)(2,1)} %bitcast.40), calls=%async_computation.3 | async-start | bytes 753664 | tf_op jit(solution)/shard_map/all_to_all | solution.py:34
  72.0 10.5 %all-to-all-done.3 = bf16[16,4,2880]{2,1,0:T(4,128)(2,1)S(1)} async-done(((bf16[16,4,2880]{2,1,0:T(4,128)(2,1)}), bf16[16,4,2880]{2,1,0:T(4,128)(2,1)S(1)}, u32[]{:S(2)}, u32[]{:S(2)}) %all-to-all-start.3) | async-done | bytes 368672 | tf_op jit(solution)/shard_map/all_to_all | solution.py:34
  94.9 14.5 %all-to-all-done.4 = bf16[16,3,180,128]{3,2,1,0:T(8,128)(2,1)S(1)} async-done(((bf16[16,3,180,128]{3,2,1,0:T(8,128)(2,1)}), bf16[16,3,180,128]{3,2,1,0:T(8,128)(2,1)S(1)}, u32[]{:S(2)}, u32[]{:S(2)}) %all-to-all-start.4) | async-done | bytes 2211872 | tf_op jit(solution)/shard_map/all_to_all | solution.py:34
  109.4 19.4 %all-to-all-start.2 = ((bf16[16,4,2944]{2,1,0:T(4,128)(2,1)}), bf16[16,4,2944]{2,1,0:T(4,128)(2,1)}, u32[]{:S(2)}, u32[]{:S(2)}) async-start(bf16[16,4,2944]{2,1,0:T(4,128)(2,1)} %copy.255), calls=%async_computation.2 | async-start | bytes 753664 | tf_op jit(solution)/shard_map/all_to_all | solution.py:34
  129.6 13.4 %all-to-all-done.2 = bf16[16,4,2944]{2,1,0:T(4,128)(2,1)} async-done(((bf16[16,4,2944]{2,1,0:T(4,128)(2,1)}), bf16[16,4,2944]{2,1,0:T(4,128)(2,1)}, u32[]{:S(2)}, u32[]{:S(2)}) %all-to-all-start.2) | async-done | bytes 376864 | tf_op jit(solution)/shard_map/all_to_all | solution.py:34
  143.0 4.3 %broadcast_in_dim.214 = bf16[16,128,1440]{1,2,0:T(8,128)(2,1)} broadcast(bf16[128,1440]{0,1:T(8,128)(2,1)} %constant_dynamic-slice_fusion), dimensions={1,2} | broadcast | bytes 6266880 | tf_op jit(solution)/shard_map/broadcast_in_dim | solution.py:39
  147.4 6.5 %all-to-all-start.6 = ((bf16[16,128,1440]{1,2,0:T(8,128)(2,1)}), bf16[16,128,1440]{1,2,0:T(8,128)(2,1)}, u32[]{:S(2)}, u32[]{:S(2)}) async-start(bf16[16,128,1440]{1,2,0:T(8,128)(2,1)} %broadcast_in_dim.214), calls=%async_computation.6 | async-start | bytes 11796480 | tf_op jit(solution)/shard_map/all_to_all | solution.py:34
  165.4 10.3 %collective-permute-start.2 = (bf16[2880,384]{1,0:T(8,128)(2,1)}, bf16[2880,384]{1,0:T(8,128)(2,1)}, u32[]{:S(2)}, u32[]{:S(2)}) collective-permute-start(bf16[2880,384]{1,0:T(8,128)(2,1)} %pad_maximum_fusion), channel_id=1, source_target_pairs={{0,16},{16,0},{1,17},{17,1},{2,18},{18,2},{3,19},{19,3},{4,20},{20... | collective-permute-start | bytes 6635528 | tf_op jit(solution)/shard_map/ppermute | solution.py:43
  180.6 44.1 %all-to-all-done.6 = bf16[16,128,1440]{1,2,0:T(8,128)(2,1)} async-done(((bf16[16,128,1440]{1,2,0:T(8,128)(2,1)}), bf16[16,128,1440]{1,2,0:T(8,128)(2,1)}, u32[]{:S(2)}, u32[]{:S(2)}) %all-to-all-start.6) | async-done | bytes 5898272 | tf_op jit(solution)/shard_map/all_to_all | solution.py:34
  224.7 6.1 %copy_bitcast_fusion = bf16[2048,1440]{0,1:T(8,128)(2,1)} fusion(bf16[16,128,1440]{1,2,0:T(8,128)(2,1)} %all-to-all-done.6), kind=kLoop, calls=%fused_computation | loop fusion | bytes 11796480 | tf_op jit(solution)/shard_map/reshape | solution.py:186
  230.7 5.7 %collective-permute-start.3 = (bf16[2048,1440]{0,1:T(8,128)(2,1)}, bf16[2048,1440]{0,1:T(8,128)(2,1)}, u32[]{:S(2)}, u32[]{:S(2)}) collective-permute-start(bf16[2048,1440]{0,1:T(8,128)(2,1)} %copy_bitcast_fusion), channel_id=1, source_target_pairs={{0,16},{16,0},{1,17},{17,1},{2,18},{18,2},{3,19},{19,3},{4,20},{20... | collective-permute-start | bytes 17694728 | tf_op jit(solution)/shard_map/ppermute | solution.py:43
  245.6 33.0 %all-to-all-start.5 = ((bf16[16,4,2944]{2,1,0:T(4,128)(2,1)}), bf16[16,4,2944]{2,1,0:T(4,128)(2,1)S(1)}, u32[]{:S(2)}, u32[]{:S(2)}) async-start(bf16[16,4,2944]{2,1,0:T(4,128)(2,1)} %pad_maximum_fusion.1), calls=%async_computation.5 | async-start | bytes 753664 | tf_op jit(solution)/shard_map/all_to_all | solution.py:34
  288.7 8.8 %all-to-all-done.5 = bf16[16,4,2944]{2,1,0:T(4,128)(2,1)S(1)} async-done(((bf16[16,4,2944]{2,1,0:T(4,128)(2,1)}), bf16[16,4,2944]{2,1,0:T(4,128)(2,1)S(1)}, u32[]{:S(2)}, u32[]{:S(2)}) %all-to-all-start.5) | async-done | bytes 376864 | tf_op jit(solution)/shard_map/all_to_all | solution.py:34
  301.6 4.0 %fusion.25 = f32[128,2048]{1,0:T(8,128)S(1)} fusion(bf16[128,2880]{0,1:T(8,128)(2,1)S(1)} %fusion.4, s32[]{:T(128)S(6)} %select_n.61, bf16[16,128,1440]{1,2,0:T(8,128)(2,1)} %all-to-all-done.6), kind=kOutput, calls=%fused_computation.48 | convolution fusion | flops 754974720 | bytes 7315460 | tf_op jit(solution)/shard_map/dot_general | solution.py:30
  309.6 4.3 %convolution_bitcast_fusion = f32[256,4,64]{0,2,1:T(8,128)} fusion(bf16[128,4,8,64]{0,3,2,1:T(8,128)(2,1)S(1)} %bitcast.203, f32[4,256,128,8]{2,1,3,0:T(8,128)} %copy-done.2, f32[4,8,128]{2,1,0:T(8,128)S(1)} %copy-done.28, f32[4,8,128]{2,1,0:T(8,128)S(1)} %copy-done.24, pred[128,256]{0,1:T(8,128)(4,1)S(1)} %fusion.33), kind=kOutput, calls=%fused_computation.32 | convolution fusion | flops 140509184 | bytes 5046272 | tf_op jit(solution)/shard_map/ujko,kujm->oum/dot_general | solution.py:87
  318.0 7.7 %all-to-all-start.7 = ((f32[16,1,128]{2,1,0:T(1,128)}), f32[16,1,128]{2,1,0:T(1,128)S(1)}, u32[]{:S(2)}, u32[]{:S(2)}) async-start(f32[16,1,128]{2,1,0:T(1,128)} %broadcast_in_dim.218), calls=%async_computation.7 | async-start | bytes 16384 | tf_op jit(solution)/shard_map/all_to_all | solution.py:34
  327.2 4.9 %all-to-all-done.7 = f32[16,1,128]{2,1,0:T(1,128)S(1)} async-done(((f32[16,1,128]{2,1,0:T(1,128)}), f32[16,1,128]{2,1,0:T(1,128)S(1)}, u32[]{:S(2)}, u32[]{:S(2)}) %all-to-all-start.7) | async-done | bytes 8224 | tf_op jit(solution)/shard_map/all_to_all | solution.py:34
  332.7 10.4 %all-to-all-start.8 = ((f32[16,1,128]{2,1,0:T(1,128)}), f32[16,1,128]{2,1,0:T(1,128)S(1)}, u32[]{:S(2)}, u32[]{:S(2)}) async-start(f32[16,1,128]{2,1,0:T(1,128)} %broadcast_in_dim.219), calls=%async_computation.8 | async-start | bytes 16384 | tf_op jit(solution)/shard_map/all_to_all | solution.py:34
  346.6 7.8 %all-to-all-done.8 = f32[16,1,128]{2,1,0:T(1,128)S(1)} async-done(((f32[16,1,128]{2,1,0:T(1,128)}), f32[16,1,128]{2,1,0:T(1,128)S(1)}, u32[]{:S(2)}, u32[]{:S(2)}) %all-to-all-start.8) | async-done | bytes 8224 | tf_op jit(solution)/shard_map/all_to_all | solution.py:34
  354.4 5.2 %collective-permute-start.5 = (f32[1,128]{1,0:T(1,128)S(1)}, f32[1,128]{1,0:T(1,128)S(1)}, u32[]{:S(2)}, u32[]{:S(2)}) collective-permute-start(f32[1,128]{1,0:T(1,128)S(1)} %bitcast.234), channel_id=1, source_target_pairs={{0,16},{16,0},{1,17},{17,1},{2,18},{18,2},{3,19},{19,3},{4,20},{20... | collective-permute-start | bytes 1544 | tf_op jit(solution)/shard_map/ppermute | solution.py:43
  364.3 3.8 %collective-permute-done.4 = bf16[128,512]{1,0:T(8,128)(2,1)S(1)} collective-permute-done((bf16[128,512]{1,0:T(8,128)(2,1)S(1)}, bf16[128,512]{1,0:T(8,128)(2,1)S(1)}, u32[]{:S(2)}, u32[]{:S(2)}) %collective-permute-start.4) | collective-permute-done | bytes 131104 | tf_op jit(solution)/shard_map/ppermute | solution.py:50
  (267 shorter events, 92.6 us)
Async XLA Ops:
  1.6 13.3 %collective-permute-start = (bf16[128,512]{1,0:T(8,128)(2,1)S(1)}, bf16[128,512]{1,0:T(8,128)(2,1)S(1)}, u32[]{:S(2)}, u32[]{:S(2)}) collective-permute-start(bf16[128,512]{1,0:T(8,128)(2,1)S(1)} %pad_maximum_fusion.3), channel_id=1, source_target_pairs={{0,16},{16,32},{32,48},{48,64},{64,80},{80,96},{96,112},{112,128},... | collective-permute-start | bytes 393224 | tf_op jit(solution)/shard_map/ppermute | solution.py:50
  18.8 52.2 %copy-start.15 = (bf16[1,128,2880]{1,2,0:T(8,128)(2,1)S(1)}, bf16[1,128,2880]{1,2,0:T(8,128)(2,1)}, u32[]{:S(2)}) copy-start(bf16[1,128,2880]{1,2,0:T(8,128)(2,1)} %param.20) | copy-start | bytes 2211844
  34.3 16.0 %all-to-all-start.1 = ((bf16[16,8,2880]{2,1,0:T(8,128)(2,1)}), bf16[16,8,2880]{2,1,0:T(8,128)(2,1)S(1)}, u32[]{:S(2)}, u32[]{:S(2)}) async-start(bf16[16,8,2880]{2,1,0:T(8,128)(2,1)} %bitcast.29), calls=%async_computation.1 | async-start | bytes 1507328 | tf_op jit(solution)/shard_map/all_to_all | solution.py:34
  51.1 31.3 %all-to-all-start.3 = ((bf16[16,4,2880]{2,1,0:T(4,128)(2,1)}), bf16[16,4,2880]{2,1,0:T(4,128)(2,1)S(1)}, u32[]{:S(2)}, u32[]{:S(2)}) async-start(bf16[16,4,2880]{2,1,0:T(4,128)(2,1)} %bitcast.40), calls=%async_computation.3 | async-start | bytes 753664 | tf_op jit(solution)/shard_map/all_to_all | solution.py:34
  84.1 25.3 %all-to-all-start.4 = ((bf16[16,3,180,128]{3,2,1,0:T(8,128)(2,1)}), bf16[16,3,180,128]{3,2,1,0:T(8,128)(2,1)S(1)}, u32[]{:S(2)}, u32[]{:S(2)}) async-start(bf16[16,3,180,128]{3,2,1,0:T(8,128)(2,1)} %broadcast_in_dim.209), calls=%async_computation.4 | async-start | bytes 4521984 | tf_op jit(solution)/shard_map/all_to_all | solution.py:34
  109.4 33.6 %all-to-all-start.2 = ((bf16[16,4,2944]{2,1,0:T(4,128)(2,1)}), bf16[16,4,2944]{2,1,0:T(4,128)(2,1)}, u32[]{:S(2)}, u32[]{:S(2)}) async-start(bf16[16,4,2944]{2,1,0:T(4,128)(2,1)} %copy.255), calls=%async_computation.2 | async-start | bytes 753664 | tf_op jit(solution)/shard_map/all_to_all | solution.py:34
  147.4 77.3 %all-to-all-start.6 = ((bf16[16,128,1440]{1,2,0:T(8,128)(2,1)}), bf16[16,128,1440]{1,2,0:T(8,128)(2,1)}, u32[]{:S(2)}, u32[]{:S(2)}) async-start(bf16[16,128,1440]{1,2,0:T(8,128)(2,1)} %broadcast_in_dim.214), calls=%async_computation.6 | async-start | bytes 11796480 | tf_op jit(solution)/shard_map/all_to_all | solution.py:34
  165.4 71.7 %collective-permute-start.2 = (bf16[2880,384]{1,0:T(8,128)(2,1)}, bf16[2880,384]{1,0:T(8,128)(2,1)}, u32[]{:S(2)}, u32[]{:S(2)}) collective-permute-start(bf16[2880,384]{1,0:T(8,128)(2,1)} %pad_maximum_fusion), channel_id=1, source_target_pairs={{0,16},{16,0},{1,17},{17,1},{2,18},{18,2},{3,19},{19,3},{4,20},{20... | collective-permute-start | bytes 6635528 | tf_op jit(solution)/shard_map/ppermute | solution.py:43
  178.3 52.4 %copy-start.12 = (bf16[64,2944]{1,0:T(8,128)(2,1)}, bf16[64,2944]{1,0:T(8,128)(2,1)S(1)}, u32[]{:S(2)}) copy-start(bf16[64,2944]{1,0:T(8,128)(2,1)S(1)} %reshape.535) | copy-start | bytes 1130500
  230.7 74.9 %collective-permute-start.3 = (bf16[2048,1440]{0,1:T(8,128)(2,1)}, bf16[2048,1440]{0,1:T(8,128)(2,1)}, u32[]{:S(2)}, u32[]{:S(2)}) collective-permute-start(bf16[2048,1440]{0,1:T(8,128)(2,1)} %copy_bitcast_fusion), channel_id=1, source_target_pairs={{0,16},{16,0},{1,17},{17,1},{2,18},{18,2},{3,19},{19,3},{4,20},{20... | collective-permute-start | bytes 17694728 | tf_op jit(solution)/shard_map/ppermute | solution.py:43
  239.0 58.9 %copy-start.51 = (s32[8]{0:T(128)S(1)}, s32[8]{0:T(128)}, u32[]{:S(2)}) copy-start(s32[8]{0:T(128)} %eq.175) | copy-start | bytes 100
  239.1 58.9 %copy-start.42 = (f32[8,8]{1,0:T(8,128)S(1)}, f32[8,8]{1,0:T(8,128)}, u32[]{:S(2)}) copy-start(f32[8,8]{1,0:T(8,128)} %copy.257) | copy-start | bytes 772
  239.1 59.4 %copy-start.14 = (bf16[8,2880]{1,0:T(8,128)(2,1)S(1)}, bf16[8,2880]{1,0:T(8,128)(2,1)}, u32[]{:S(2)}) copy-start(bf16[8,2880]{1,0:T(8,128)(2,1)} %copy-done.13) | copy-start | bytes 138244
  239.1 59.4 %copy-start.34 = (f32[2880]{0:T(1024)S(1)}, f32[2880]{0:T(1024)}, u32[]{:S(2)}) copy-start(f32[2880]{0:T(1024)} %param.22) | copy-start | bytes 34564
  239.1 59.4 %copy-start.41 = (f32[8,8]{0,1:T(8,128)S(1)}, f32[8,8]{0,1:T(8,128)}, u32[]{:S(2)}) copy-start(f32[8,8]{0,1:T(8,128)} %copy-done.40) | copy-start | bytes 772
  239.1 59.4 %copy-start.47 = (f32[8]{0:T(128)S(1)}, f32[8]{0:T(128)}, u32[]{:S(2)}) copy-start(f32[8]{0:T(128)} %copy-done.46) | copy-start | bytes 100
  240.6 58.4 %copy-start.7 = (bf16[1,128,2880]{1,2,0:T(8,128)(2,1)S(1)}, bf16[1,128,2880]{1,2,0:T(8,128)(2,1)}, u32[]{:S(2)}) copy-start(bf16[1,128,2880]{1,2,0:T(8,128)(2,1)} %param.31) | copy-start | bytes 2211844
  240.6 58.4 %copy-start.55 = (f32[8]{0:T(128)S(1)}, f32[8]{0:T(128)}, u32[]{:S(2)}) copy-start(f32[8]{0:T(128)} %eq.166) | copy-start | bytes 100
  245.6 51.8 %all-to-all-start.5 = ((bf16[16,4,2944]{2,1,0:T(4,128)(2,1)}), bf16[16,4,2944]{2,1,0:T(4,128)(2,1)S(1)}, u32[]{:S(2)}, u32[]{:S(2)}) async-start(bf16[16,4,2944]{2,1,0:T(4,128)(2,1)} %pad_maximum_fusion.1), calls=%async_computation.5 | async-start | bytes 753664 | tf_op jit(solution)/shard_map/all_to_all | solution.py:34
  284.2 3.1 collective-permute-start.1
  318.0 14.1 %all-to-all-start.7 = ((f32[16,1,128]{2,1,0:T(1,128)}), f32[16,1,128]{2,1,0:T(1,128)S(1)}, u32[]{:S(2)}, u32[]{:S(2)}) async-start(f32[16,1,128]{2,1,0:T(1,128)} %broadcast_in_dim.218), calls=%async_computation.7 | async-start | bytes 16384 | tf_op jit(solution)/shard_map/all_to_all | solution.py:34
  332.7 21.7 %all-to-all-start.8 = ((f32[16,1,128]{2,1,0:T(1,128)}), f32[16,1,128]{2,1,0:T(1,128)S(1)}, u32[]{:S(2)}, u32[]{:S(2)}) async-start(f32[16,1,128]{2,1,0:T(1,128)} %broadcast_in_dim.219), calls=%async_computation.8 | async-start | bytes 16384 | tf_op jit(solution)/shard_map/all_to_all | solution.py:34
  354.4 9.3 %collective-permute-start.5 = (f32[1,128]{1,0:T(1,128)S(1)}, f32[1,128]{1,0:T(1,128)S(1)}, u32[]{:S(2)}, u32[]{:S(2)}) collective-permute-start(f32[1,128]{1,0:T(1,128)S(1)} %bitcast.234), channel_id=1, source_target_pairs={{0,16},{16,0},{1,17},{17,1},{2,18},{18,2},{3,19},{19,3},{4,20},{20... | collective-permute-start | bytes 1544 | tf_op jit(solution)/shard_map/ppermute | solution.py:43
  361.8 6.3 %collective-permute-start.4 = (bf16[128,512]{1,0:T(8,128)(2,1)S(1)}, bf16[128,512]{1,0:T(8,128)(2,1)S(1)}, u32[]{:S(2)}, u32[]{:S(2)}) collective-permute-start(bf16[128,512]{1,0:T(8,128)(2,1)S(1)} %pad_maximum_fusion.4), channel_id=1, source_target_pairs={{16,0},{32,16},{48,32},{64,48},{80,64},{96,80},{112,96},{128,112},... | collective-permute-start | bytes 393224 | tf_op jit(solution)/shard_map/ppermute | solution.py:50
  (49 other events, 759.7 us)

commit v2 on v1

--- a/solution.py
+++ b/solution.py
@@ -35,7 +35,7 @@
 
 
 def to_all(value, axis):
-    count = lax.axis_size(axis)
+    count = lax.psum(1, axis)
     return exchange(jnp.broadcast_to(value[None], (count, *value.shape)), axis)
 
 
@@ -113,13 +113,11 @@
     upstream,
 ):
     chips, cores, dp_count = lax.axis_size("z"), lax.axis_size("core"), lax.axis_size("dp")
-    core = lax.axis_index("core")
-    seq_index = lax.axis_index("z") * cores + core
+    seq_index = lax.axis_index("z") * cores + lax.axis_index("core")
     query_rows = queries[0]
     tokens = query_rows.shape[0]
     group_count = max(dp_count // 4, 1)
     all_tokens = dp_count * chips * cores * tokens
-    half = D // 2
     lanes = out_weight.shape[0]
 
     route_rows = routes[0]
@@ -133,18 +131,15 @@
     pick = slot_hot.reshape(SLOTS, tokens)
     pick_low = pick.astype(BF16)
     slot_expert = jnp.repeat(window, CAP)
-    upstream_slots = dot32(pick_low, upstream[0]).astype(BF16)
-    residual_slots = dot32(pick_low, residual[0])
+    same = dot_last(pick_low, pick_low)
+    primary = jnp.sum(jnp.tril(same, -1), axis=1) == 0
+    place = jnp.where(primary[:, None], pick, False)
+    taken = jnp.any(pick, axis=0)
 
     shard = jnp.stack([expert_gate, expert_up, expert_down])
     gathered = to_all(shard, "dp")
-    own_block = jnp.concatenate([gathered[:, i].reshape(D, -1) for i in range(3)], axis=1)
-    other_block = swap_cores(own_block)
+    out_full = lax.all_gather(out_weight, "dp", axis=0, tiled=True)
     hid = expert_gate.shape[1]
-
-    by_expert = upstream_slots.reshape(EW, 1, CAP, D)
-    outgoing = jnp.broadcast_to(by_expert, (EW, chips // EW, CAP, D)).reshape(chips, CAP, D)
-    up_rows = exchange(outgoing, "z").reshape(chips * CAP, D)
 
     halo = along_seq(jnp.concatenate([key_rows[0], value_matrix[0]], axis=1), 1)
     kv_width = key_rows.shape[2]
@@ -152,15 +147,21 @@
     values_here = jnp.concatenate([halo[:, kv_width:], value_matrix[0]], axis=0)
     row_index = jnp.arange(tokens, dtype=jnp.int32)[:, None]
     col_index = jnp.arange(WINDOW + tokens, dtype=jnp.int32)[None, :]
-    allowed = (
-        (col_index >= row_index + 1)
-        & (col_index <= row_index + WINDOW)
-        & ((col_index >= WINDOW) | (seq_index > 0))
-    )
-    probs, sink_probs = head_scores(query_rows, keys_here, head_sink_logits, allowed)
-    probs_low = probs.astype(BF16)
-    attended = head_mix(probs_low, values_here)
-    attended_slots = dot32(pick_low, attended).astype(BF16)
+
+    def visible(rows):
+        return (
+            (col_index >= rows + 1)
+            & (col_index <= rows + WINDOW)
+            & ((col_index >= WINDOW) | (seq_index > 0))
+        )
+
+    slot_rows = jnp.sum(jnp.where(pick, row_index[:, 0][None, :], 0), axis=1, keepdims=True)
+    query_slots = dot32(pick_low, query_rows).astype(BF16)
+    probs_slots, sink_slots = head_scores(
+        query_slots, keys_here, head_sink_logits, visible(slot_rows)
+    )
+    probs_slots_low = probs_slots.astype(BF16)
+    attended_slots = head_mix(probs_slots_low, values_here)
 
     mask_wide = response_mask[0].astype(F32)
     facts = jnp.stack(
@@ -176,16 +177,17 @@
         [columns, jnp.broadcast_to(facts_row[None], (dp_count, 1, lanes))], axis=1
     )
     sent = jnp.pad(sent, ((0, 0), (0, 2 * SLOTS - SLOTS - 1), (0, 0)))
+    sent, gathered = lax.optimization_barrier((sent, gathered))
     arrived = exchange(sent, "dp")
     facts_all = arrived[:, SLOTS, :3].astype(F32)
     partial = dot32(arrived[:, :SLOTS].reshape(dp_count * SLOTS, lanes), out_weight)
     partial = exchange(partial.astype(BF16).reshape(dp_count, SLOTS, D), "dp")
     projected = jnp.sum(partial.astype(F32), axis=0)
-
-    own_half = lax.dynamic_slice_in_dim(out_weight, core * half, half, axis=1)
-    own_out = to_all(own_half, "dp").reshape(dp_count * lanes, half)
-    other_out = swap_cores(own_out)
-
+    own_block = jnp.concatenate([gathered[:, i].reshape(D, -1) for i in range(3)], axis=1)
+    other_block = swap_cores(own_block)
+
+    residual_slots = dot32(pick_low, residual[0])
+    upstream_slots = dot32(pick_low, upstream[0]).astype(BF16)
     mid = (residual_slots + projected).astype(BF16)
     mid_wide = lax.optimization_barrier(mid).astype(F32)
     inv_rms = lax.rsqrt(jnp.mean(mid_wide * mid_wide, axis=1, keepdims=True) + NORM_EPS)
@@ -198,36 +200,38 @@
     group_sizes = jnp.sum(group_hot, axis=0)
     group_sums = jnp.sum(group_hot * reward_all[:, None], axis=0)
     group_squares = jnp.sum(group_hot * (reward_all * reward_all)[:, None], axis=0)
-    own_hot = (group_ids[0] == jnp.arange(group_count, dtype=jnp.int32)).astype(F32)
+    own_hot = group_ids[0] == jnp.arange(group_count, dtype=jnp.int32)
     means = group_sums / group_sizes
     spreads = group_squares / group_sizes - means * means
-    own_mean = jnp.sum(jnp.where(own_hot > 0, means, 0.0))
-    own_spread = jnp.sum(jnp.where(own_hot > 0, spreads, 0.0))
+    own_mean = jnp.sum(jnp.where(own_hot, means, 0.0))
+    own_spread = jnp.sum(jnp.where(own_hot, spreads, 0.0))
     advantage = (rewards[0].astype(F32) - own_mean) / jnp.sqrt(jnp.maximum(own_spread, 1.0))
 
     count_high = jnp.floor(counts_here / 64.0)
     count_tail = jnp.stack([count_high, counts_here - 64.0 * count_high])
     count_tail = jnp.pad(count_tail, (0, PADDED - D - 2)).astype(BF16)
-    with_tail = jnp.concatenate(
-        [normed, jnp.broadcast_to(count_tail[None], (SLOTS, PADDED - D))], axis=1
-    )
-    by_expert = with_tail.reshape(EW, 1, CAP, PADDED)
-    outgoing = jnp.broadcast_to(by_expert, (EW, chips // EW, CAP, PADDED))
-    came = exchange(outgoing.reshape(chips, CAP, PADDED), "z")
+    tails = jnp.broadcast_to(count_tail[None], (2 * SLOTS, PADDED - D))
+    both = jnp.concatenate([jnp.concatenate([normed, upstream_slots], axis=0), tails], axis=1)
+    at = jnp.arange(2 * SLOTS)
+    source = (at // SLOTS) * CAP + at % CAP + jnp.where(at % SLOTS >= CAP, SLOTS, 0)
+    arrange = (source[:, None] == at[None, :]).astype(BF16)
+    by_expert = dot32(arrange, both).astype(BF16).reshape(EW, 1, 2 * CAP, PADDED)
+    outgoing = jnp.broadcast_to(by_expert, (EW, chips // EW, 2 * CAP, PADDED))
+    came = exchange(outgoing.reshape(chips, 2 * CAP, PADDED), "z")
     count_parts = jnp.sum(came[:, 0, D : D + 2].astype(F32), axis=0)
     core_count = count_parts[0] * 64.0 + count_parts[1]
     token_total = core_count + swap_cores(jnp.full((8, 128), core_count))[0, 0]
     token_scale = -advantage * all_tokens / token_total
     loss_weight = token_scale * mask_wide
 
-    rows = came.reshape(chips * CAP, PADDED)[:, :D]
-    pieces = []
+    rows = came.reshape(chips * 2 * CAP, PADDED)[:, :D]
     shares = 0.0
     grads = []
     for block in (own_block, other_block):
-        pre = dot32(rows, block[:, : 2 * hid])
-        up_down = dot32(up_rows, block[:, 2 * hid :])
-        gate_pre, up_pre = pre[:, :hid], pre[:, hid:]
+        pre = dot32(rows, block).reshape(chips, 2 * CAP, 3 * hid)
+        up_down = pre[:, CAP:, 2 * hid :].reshape(chips * CAP, hid)
+        gate_pre = pre[:, :CAP, :hid].reshape(chips * CAP, hid)
+        up_pre = pre[:, :CAP, hid : 2 * hid].reshape(chips * CAP, hid)
         sigmoid_gate = jax.nn.sigmoid(GLU_SLOPE * gate_pre)
         activation = ((up_pre + 1.0) * gate_pre * sigmoid_gate).astype(BF16)
         shares = shares + jnp.sum(activation.astype(F32) * up_down, axis=1)
@@ -238,13 +242,24 @@
             * (sigmoid_gate + GLU_SLOPE * gate_pre * sigmoid_gate * (1.0 - sigmoid_gate))
         )
         grads.append(jnp.concatenate([grad_gate, grad_up], axis=1).astype(BF16))
-    piece = dot_last(grads[0], own_block[:, : 2 * hid]) + dot_last(grads[1], other_block[:, : 2 * hid])
+    piece = dot_last(grads[0], own_block[:, : 2 * hid]) + dot_last(
+        grads[1], other_block[:, : 2 * hid]
+    )
     share_1 = shares.astype(BF16).astype(F32)
     share_2 = (shares - share_1).astype(BF16).astype(F32)
     share_3 = shares - share_1 - share_2
     tail = jnp.pad(jnp.stack([share_1, share_2, share_3], axis=1), ((0, 0), (0, PADDED - D - 3)))
     back = jnp.concatenate([piece, tail], axis=1).astype(BF16)
     back = exchange(back.reshape(chips, CAP, PADDED), "z")
+    cot_rows = (loss_weight[:, None] * upstream[0].astype(F32)).astype(BF16)
+    probs, sink_probs = head_scores(query_rows, keys_here, head_sink_logits, visible(row_index))
+    grad_attended = jnp.where(taken[:, None], 0.0, dot_last(cot_rows, out_full)).astype(BF16)
+    grad_q, grad_k, grad_v, grad_sinks = head_grads(
+        probs, probs.astype(BF16), sink_probs, query_rows, keys_here, values_here, grad_attended
+    )
+    back, grad_q, grad_k, grad_v, grad_sinks = lax.optimization_barrier(
+        (back, grad_q, grad_k, grad_v, grad_sinks)
+    )
     summed = jnp.sum(back.reshape(EW, chips // EW, CAP, PADDED).astype(F32), axis=1)
     summed = summed.reshape(SLOTS, PADDED)
     share_slots = jnp.sum(summed[:, D : D + 3], axis=1)
@@ -259,7 +274,7 @@
         jnp.where(route_slots == slot_expert[:, None], route_weights, 0.0), axis=1
     )
     loss_slots = jnp.sum(jnp.where(pick, loss_weight[None, :], 0.0), axis=1)
-    same = dot_last(pick_low, pick_low)
+    cot_slots = loss_slots[:, None] * upstream_slots.astype(F32)
     grad_rows = (weight_slots * loss_slots)[:, None] * summed[:, :D]
     grad_rows = dot32(same, grad_rows, precision=HIGHEST)
     grad_share = loss_slots * share_slots
@@ -275,31 +290,42 @@
     grad_logits = jnp.sum(jnp.where(route_hot, grad_route[:, :, None], 0.0), axis=1).astype(BF16)
     grad_normed = dot_last(grad_logits, router) + grad_rows
     grad_unit = grad_normed * norm_gain[None, :]
-    norm_grad = inv_rms * (
+    grad_slots = cot_slots + inv_rms * (
         grad_unit - unit_rows * jnp.mean(grad_unit * unit_rows, axis=1, keepdims=True)
     )
-    earlier = jnp.tril(same, -1)
-    primary = jnp.sum(earlier, axis=1) == 0
-    place = jnp.where(primary[:, None], pick.astype(F32), 0.0)
-    norm_part = lax.dot_general(
-        place, norm_grad, (((0,), (0,)), ((), ())), precision=HIGHEST, preferred_element_type=F32
-    )
-    grad_residual = (loss_weight[:, None] * upstream[0].astype(F32) + norm_part).astype(BF16)
-
-    grad_own = lax.dynamic_slice_in_dim(grad_residual, core * half, half, axis=1)
-    grad_other = lax.dynamic_slice_in_dim(grad_residual, (1 - core) * half, half, axis=1)
-    grad_attended = (dot_last(grad_own, own_out) + dot_last(grad_other, other_out)).astype(BF16)
-    grad_q, grad_k, grad_v, grad_sinks = head_grads(
-        probs, probs_low, sink_probs, query_rows, keys_here, values_here, grad_attended
-    )
-    sinks = jnp.pad(grad_sinks, (0, 128 - QUERY_HEADS))[None]
-    sinks = jnp.sum(to_all(sinks, "dp"), axis=0)
+    grad_slots = jnp.where(primary[:, None], grad_slots, 0.0).astype(BF16)
+
+    attended_grad_slots = dot_last(grad_slots, out_full).astype(BF16)
+    slot_q, slot_k, slot_v, slot_sinks = head_grads(
+        probs_slots,
+        probs_slots_low,
+        sink_slots,
+        query_slots,
+        keys_here,
+        values_here,
+        attended_grad_slots,
+    )
+    sinks = jnp.pad(grad_sinks + slot_sinks, (0, 128 - QUERY_HEADS))[None]
+    sinks = jnp.sum(to_all(sinks, ("core", "dp")), axis=0)
     sinks = jnp.sum(to_all(sinks, "z"), axis=0)
-    sinks = sinks + swap_cores(sinks)
+    grad_k = grad_k + slot_k
+    grad_v = grad_v + slot_v
     onward = jnp.concatenate([grad_k[:WINDOW], grad_v[:WINDOW]], axis=1).astype(BF16)
     onward = along_seq(onward, -1).astype(F32)
     grad_key_rows = (grad_k[WINDOW:] + onward[:, :kv_width]).astype(BF16)
     grad_value_rows = (grad_v[WINDOW:] + onward[:, kv_width:]).astype(BF16)
+    put = place.astype(BF16)
+    by_token = (((0,), (0,)), ((), ()))
+    grad_residual = jnp.where(
+        taken[:, None],
+        lax.dot_general(put, grad_slots, by_token, preferred_element_type=F32).astype(BF16),
+        cot_rows,
+    )
+    grad_q = jnp.where(
+        taken[:, None],
+        lax.dot_general(put, slot_q, by_token, preferred_element_type=F32).astype(BF16),
+        grad_q,
+    )
     return (
         grad_q[None],
         grad_key_rows[None],

time: 371 us -> 276 us (0.74)
  waiting for transfers between devices: 119 us -> 39.2 us
  starting transfers between devices: 130 us -> 90 us
  matrix products: 34.2 us -> 47.9 us
  between operations: 7.91 us -> 21.6 us
  blocking collectives: 13.2 us -> 0 us
  other arithmetic: 17.8 us -> 29.6 us
    all_to_all x8 -> x7, waiting for transfers between devices: 115 us -> 38.5 us  [exchange(): return lax.all_to_all(value, axis, split_axis=0, concat_axis=0, tiled=True)]
    all_to_all x8 -> x7, starting transfers between devices: 99.2 us -> 68 us  [exchange(): return lax.all_to_all(value, axis, split_axis=0, concat_axis=0, tiled=True)]
    all_to_all x1 -> x0, blocking collectives: 13.2 us -> none  [exchange(): return lax.all_to_all(value, axis, split_axis=0, concat_axis=0, tiled=True)]
    ppermute x4 -> x2, starting transfers between devices: 23.4 us -> 15 us  [swap_cores(): return lax.ppermute(value, 'core', [(0, 1), (1, 0)])]
    reshape x5 -> x4, local copies, waits for them, and re-layouts: 8.97 us -> 1.27 us  [the longest x1 0.89 us: head_scores(): q = query_rows.reshape(tokens, KEY_VALUE_HEADS, per_group, HEAD_SIZE)]
    dot_general x12 -> x11, matrix products: 8.97 us -> 14 us  [dot32(): return jnp.dot(a, b, preferred_element_type=F32, **kw)]
    dot_general x6, matrix products: 12 us -> 16.8 us  [dot_last(): return lax.dot_general(a, b, CONTRACT_LAST, preferred_element_type=F32)]
    dot_general x1 -> x2, matrix products: 0.75 us -> 5.1 us  [head_scores(): jnp.einsum('baqj,eaj->aqbe', q, k, preferred_element_type=F32)]
  transfers between devices with their start and end apart: 14 -> 12, of which waited for: 10 -> 5; matrix products, arithmetic and copies ran while one was open for 19% -> 40% of each run, Pallas kernels for 0% -> 0%
where the time goes in v2:
time: 276 us; the launch traced here: 274 us
  starting transfers between devices  90 us (33%)
  matrix products  47.9 us (17%)
  local copies, waits for them, and re-layouts  45.7 us (17%)
  waiting for transfers between devices  39.2 us (14%)
  other arithmetic  29.6 us (11%)
  between operations  21.6 us (8%)
    all_to_all x7, starting transfers between devices, exchange(): return lax.all_to_all(value, axis, split_axis=0, concat_axis=0, tiled=True)  68 us
    all_to_all x7, waiting for transfers between devices, exchange(): return lax.all_to_all(value, axis, split_axis=0, concat_axis=0, tiled=True)  38.5 us
    dot_general x6, matrix products, dot_last(): return lax.dot_general(a, b, CONTRACT_LAST, preferred_element_type=F32)  16.8 us
    ppermute x2, starting transfers between devices, swap_cores(): return lax.ppermute(value, 'core', [(0, 1), (1, 0)])  15 us
    dot_general x11, matrix products, dot32(): return jnp.dot(a, b, preferred_element_type=F32, **kw)  14 us
    unnamed x172, local copies, waits for them, and re-layouts  10.5 us
    ppermute x2, starting transfers between devices, along_seq(): lax.ppermute(value, ('z', 'core'), [(i, i + steps) for i in range(first,...  7.05 us
  transfers between devices with their start and end apart: 12, of which 5 were waited for; matrix products, arithmetic and copies ran while one was open for 40% of the time, Pallas kernels for 0%

profile of v2, /device:TPU:1, one launch (start us, length us, event | category | flops | bytes accessed | tf_op | source)
XLA Modules:
  0.0 273.9 jit_solution(13181503627911838090)
XLA Ops:
  9.5 4.9 %collective-permute-start = (bf16[128,512]{1,0:T(8,128)(2,1)}, bf16[128,512]{1,0:T(8,128)(2,1)}, u32[]{:S(2)}, u32[]{:S(2)}) collective-permute-start(bf16[128,512]{1,0:T(8,128)(2,1)} %pad_maximum_fusion.2), channel_id=1, source_target_pairs={{0,16},{16,32},{32,48},{48,64},{64,80},{80,96},{96,112},{112,128},... | collective-permute-start | bytes 393224 | tf_op jit(solution)/shard_map/ppermute | solution.py:50
  16.9 6.8 %all-to-all-start = ((bf16[16,3,180,128]{3,2,1,0:T(8,128)(2,1)}), bf16[16,3,180,128]{3,2,1,0:T(8,128)(2,1)S(1)}, u32[]{:S(2)}, u32[]{:S(2)}) async-start(bf16[16,3,180,128]{3,2,1,0:T(8,128)(2,1)} %broadcast_in_dim.284), calls=%async_computation | async-start | bytes 4521984 | tf_op jit(solution)/shard_map/all_to_all | solution.py:34
  28.8 2.0 convolution_convert_fusion.3
  43.7 13.9 %all-to-all-done = bf16[16,3,180,128]{3,2,1,0:T(8,128)(2,1)S(1)} async-done(((bf16[16,3,180,128]{3,2,1,0:T(8,128)(2,1)}), bf16[16,3,180,128]{3,2,1,0:T(8,128)(2,1)S(1)}, u32[]{:S(2)}, u32[]{:S(2)}) %all-to-all-start) | async-done | bytes 2211872 | tf_op jit(solution)/shard_map/all_to_all | solution.py:34
  58.2 5.5 %all-to-all-start.1 = ((bf16[16,16,128]{2,1,0:T(8,128)(2,1)}), bf16[16,16,128]{2,1,0:T(8,128)(2,1)S(1)}, u32[]{:S(2)}, u32[]{:S(2)}) async-start(bf16[16,16,128]{2,1,0:T(8,128)(2,1)} %copy.213), calls=%async_computation.1 | async-start | bytes 131072 | tf_op jit(solution)/shard_map/all_to_all | solution.py:34
  65.0 5.2 %all-to-all-done.1 = bf16[16,16,128]{2,1,0:T(8,128)(2,1)S(1)} async-done(((bf16[16,16,128]{2,1,0:T(8,128)(2,1)}), bf16[16,16,128]{2,1,0:T(8,128)(2,1)S(1)}, u32[]{:S(2)}, u32[]{:S(2)}) %all-to-all-start.1) | async-done | bytes 65568 | tf_op jit(solution)/shard_map/all_to_all | solution.py:34
  70.2 2.3 convolution_convert_fusion.1
  72.5 2.3 copy.215
  74.8 4.3 %all-to-all-start.2 = ((bf16[16,8,2880]{2,1,0:T(8,128)(2,1)}), bf16[16,8,2880]{2,1,0:T(8,128)(2,1)}, u32[]{:S(2)}, u32[]{:S(2)}) async-start(bf16[16,8,2880]{2,1,0:T(8,128)(2,1)} %bitcast.212), calls=%async_computation.2 | async-start | bytes 1507328 | tf_op jit(solution)/shard_map/all_to_all | solution.py:34
  86.1 4.2 %fusion.3 = (f32[4,8,128]{2,1,0:T(8,128)}, f32[4,256,128,8]{2,1,3,0:T(8,128)}) fusion(pred[128,256]{0,1:T(8,128)(4,1)S(1)} %fusion.47, bf16[128,4,8,64]{0,3,2,1:T(8,128)(2,1)S(1)} %bitcast.209, bf16[128,4,64]{0,2,1:T(8,128)(2,1)} %bitcast.218, bf16[128,4,64]{0,2,1:T(8,128)(2,1)} %bitcast.222), kind=kOutput, calls=%fused_computation.7 | convolution fusion | flops 137621504 | bytes 4898816 | tf_op jit(solution)/shard_map/baqj,eaj->aqbe/dot_general | solution.py:58
  103.6 24.6 %all-to-all-start.3 = ((bf16[16,8,2944]{2,1,0:T(8,128)(2,1)}), bf16[16,8,2944]{2,1,0:T(8,128)(2,1)}, u32[]{:S(2)}, u32[]{:S(2)}) async-start(bf16[16,8,2944]{2,1,0:T(8,128)(2,1)} %bitcast.211), calls=%async_computation.3 | async-start | bytes 1507328 | tf_op jit(solution)/shard_map/all_to_all | solution.py:34
  138.1 5.3 %collective-permute-start.2 = (bf16[2880,384]{1,0:T(8,128)(2,1)}, bf16[2880,384]{1,0:T(8,128)(2,1)S(1)}, u32[]{:S(2)}, u32[]{:S(2)}) collective-permute-start(bf16[2880,384]{1,0:T(8,128)(2,1)} %constant_dynamic-update-slice_fusion), channel_id=1, source_target_pairs={{0,16},{16,0},{1,17},{17,1},{2,18},{18,2},{3,19},{19,3},{4,20},{20... | collective-permute-start | bytes 6635528 | tf_op jit(solution)/shard_map/ppermute | solution.py:43
  150.4 8.0 %all-to-all-done.3 = bf16[16,8,2944]{2,1,0:T(8,128)(2,1)} async-done(((bf16[16,8,2944]{2,1,0:T(8,128)(2,1)}), bf16[16,8,2944]{2,1,0:T(8,128)(2,1)}, u32[]{:S(2)}, u32[]{:S(2)}) %all-to-all-start.3) | async-done | bytes 753696 | tf_op jit(solution)/shard_map/all_to_all | solution.py:34
  164.4 9.6 %collective-permute-start.1 = (f32[8,128]{1,0:T(8,128)}, f32[8,128]{1,0:T(8,128)}, u32[]{:S(2)}, u32[]{:S(2)}) collective-permute-start(f32[8,128]{1,0:T(8,128)} %broadcast_in_dim.289), channel_id=1, source_target_pairs={{0,16},{16,0},{1,17},{17,1},{2,18},{18,2},{3,19},{19,3},{4,20},{20... | collective-permute-start | bytes 12296 | tf_op jit(solution)/shard_map/ppermute | solution.py:43
  174.0 2.4 convolution_bitcast_fusion.4
  185.9 8.1 %all-to-all-start.4 = ((bf16[16,4,2944]{2,1,0:T(4,128)(2,1)}), bf16[16,4,2944]{2,1,0:T(4,128)(2,1)}, u32[]{:S(2)}, u32[]{:S(2)}) async-start(bf16[16,4,2944]{2,1,0:T(4,128)(2,1)} %pad_maximum_fusion), calls=%async_computation.4 | async-start | bytes 753664 | tf_op jit(solution)/shard_map/all_to_all | solution.py:34
  198.0 6.3 %fusion.12 = bf16[128,2048]{1,0:T(8,128)(2,1)S(1)} fusion(bf16[2048,2880]{0,1:T(8,128)(2,1)} %all-gather.2.cloned.1.call-done, bf16[1,128,2880]{1,2,0:T(8,128)(2,1)} %param.31, f32[128]{0:T(128)S(1)} %multiply_bitcast_fusion, pred[128]{0:T(512)(128)(4,1)} %get-tuple-element.26), kind=kOutput, calls=%fused_computation.24 | convolution fusion | flops 1511579648 | bytes 13058688 | tf_op jit(solution)/shard_map/dot_general | solution.py:30
  204.7 3.8 %fusion = (f32[4,8,128]{2,1,0:T(8,128)S(1)}, f32[4,256,128,8]{2,1,3,0:T(8,128)S(1)}) fusion(f32[4,8,128]{2,1,0:T(8,128)S(1)} %copy-done.45, f32[4,8,128]{2,1,0:T(8,128)S(1)} %copy-done.32, f32[4,256,128,8]{2,1,3,0:T(8,128)} %get-tuple-element.61, pred[128,256]{0,1:T(8,128)(4,1)S(1)} %fusion.47, bf16[128,4,8,64]{0,3,2,1:T(8,128)(2,1)S(1)} %bitcast.225, ...), kind=kOutput, calls=%fused_computation.2 | convolution fusion | flops 141815808 | bytes 9125888 | tf_op jit(solution)/shard_map/baqj,eaj->aqbe/dot_general | solution.py:81
  215.2 2.0 fusion.15
  219.8 6.2 %convolution_convert_fusion.6 = bf16[8,2048]{1,0:T(8,128)(2,1)S(1)} fusion(bf16[2048,2880]{0,1:T(8,128)(2,1)} %all-gather.2.cloned.1.call-done, f32[8,2880]{1,0:T(8,128)S(1)} %get-tuple-element.67, bf16[8,2880]{1,0:T(8,128)(2,1)S(1)} %copy-done.12, bf16[8,2880]{1,0:T(8,128)(2,1)S(1)} %copy-done.24, f32[8]{0:T(128)S(1)} %broadcast_multiply_fusion, ...), kind=kOutput, calls=%fused_computation.29 | convolution fusion | flops 94618624 | bytes 12013672 | tf_op jit(solution)/shard_map/dot_general | solution.py:30
  228.4 8.0 %all-to-all-start.5 = ((f32[32,1,128]{2,1,0:T(1,128)}), f32[32,1,128]{2,1,0:T(1,128)S(1)}, u32[]{:S(2)}, u32[]{:S(2)}) async-start(f32[32,1,128]{2,1,0:T(1,128)} %broadcast_in_dim.312), calls=%async_computation.5 | async-start | bytes 32768 | tf_op jit(solution)/shard_map/all_to_all | solution.py:34
  237.9 2.1 collective-permute-start.3
  243.9 10.7 %all-to-all-start.6 = ((f32[16,1,128]{2,1,0:T(1,128)}), f32[16,1,128]{2,1,0:T(1,128)S(1)}, u32[]{:S(2)}, u32[]{:S(2)}) async-start(f32[16,1,128]{2,1,0:T(1,128)} %broadcast_in_dim.313), calls=%async_computation.6 | async-start | bytes 16384 | tf_op jit(solution)/shard_map/all_to_all | solution.py:34
  255.7 10.1 %all-to-all-done.6 = f32[16,1,128]{2,1,0:T(1,128)S(1)} async-done(((f32[16,1,128]{2,1,0:T(1,128)}), f32[16,1,128]{2,1,0:T(1,128)S(1)}, u32[]{:S(2)}, u32[]{:S(2)}) %all-to-all-start.6) | async-done | bytes 8224 | tf_op jit(solution)/shard_map/all_to_all | solution.py:34
  (329 shorter events, 93.7 us)
Async XLA Ops:
  7.2 140.3 %copy-start = (bf16[2880,128]{1,0:T(8,128)(2,1)S(1)}, bf16[2880,128]{1,0:T(8,128)(2,1)}, u32[]{:S(2)}) copy-start(bf16[2880,128]{1,0:T(8,128)(2,1)} %param.23) | copy-start | bytes 2211844
  7.2 16.5 %copy-start.62 = (s32[1,128,4]{1,2,0:T(4,128)S(1)}, s32[1,128,4]{1,2,0:T(4,128)}, u32[]{:S(2)}) copy-start(s32[1,128,4]{1,2,0:T(4,128)} %param.27) | copy-start | bytes 6148
  7.2 20.8 %copy-start.9 = (bf16[1,128,2048]{2,1,0:T(8,128)(2,1)S(1)}, bf16[1,128,2048]{2,1,0:T(8,128)(2,1)}, u32[]{:S(2)}) copy-start(bf16[1,128,2048]{2,1,0:T(8,128)(2,1)} %param.16) | copy-start | bytes 1572868
  7.2 190.7 %all-gather.2.cloned.1.call-start = ((), (), s32[]{:S(2)}) async-start(), calls=%async_computation.7 | async-start | bytes 12533760 | tf_op jit(solution)/shard_map/all_gather | solution.py:141
  9.5 29.3 %collective-permute-start = (bf16[128,512]{1,0:T(8,128)(2,1)}, bf16[128,512]{1,0:T(8,128)(2,1)}, u32[]{:S(2)}, u32[]{:S(2)}) collective-permute-start(bf16[128,512]{1,0:T(8,128)(2,1)} %pad_maximum_fusion.2), channel_id=1, source_target_pairs={{0,16},{16,32},{32,48},{48,64},{64,80},{80,96},{96,112},{112,128},... | collective-permute-start | bytes 393224 | tf_op jit(solution)/shard_map/ppermute | solution.py:50
  16.9 40.6 %all-to-all-start = ((bf16[16,3,180,128]{3,2,1,0:T(8,128)(2,1)}), bf16[16,3,180,128]{3,2,1,0:T(8,128)(2,1)S(1)}, u32[]{:S(2)}, u32[]{:S(2)}) async-start(bf16[16,3,180,128]{3,2,1,0:T(8,128)(2,1)} %broadcast_in_dim.284), calls=%async_computation | async-start | bytes 4521984 | tf_op jit(solution)/shard_map/all_to_all | solution.py:34
  33.3 45.8 %copy-start.14 = (bf16[1,128,256]{1,2,0:T(8,128)(2,1)}, bf16[1,128,256]{1,2,0:T(8,128)(2,1)S(1)}, u32[]{:S(2)}) copy-start(bf16[1,128,256]{1,2,0:T(8,128)(2,1)S(1)} %copy.207) | copy-start | bytes 196612
  39.8 39.3 %copy-start.52 = (bf16[128,256]{0,1:T(8,128)(2,1)}, bf16[128,256]{0,1:T(8,128)(2,1)S(1)}, u32[]{:S(2)}) copy-start(bf16[128,256]{0,1:T(8,128)(2,1)S(1)} %copy.209) | copy-start | bytes 196612
  39.9 39.2 %copy-start.17 = (bf16[128,256]{0,1:T(8,128)(2,1)}, bf16[128,256]{0,1:T(8,128)(2,1)S(1)}, u32[]{:S(2)}) copy-start(bf16[128,256]{0,1:T(8,128)(2,1)S(1)} %copy.206) | copy-start | bytes 196612
  43.3 35.8 %copy-start.20 = (bf16[4,8,8,256]{3,1,2,0:T(8,128)(2,1)}, bf16[4,8,8,256]{3,1,2,0:T(8,128)(2,1)S(1)}, u32[]{:S(2)}) copy-start(bf16[4,8,8,256]{3,1,2,0:T(8,128)(2,1)S(1)} %fusion.111) | copy-start | bytes 393220
  58.2 12.0 %all-to-all-start.1 = ((bf16[16,16,128]{2,1,0:T(8,128)(2,1)}), bf16[16,16,128]{2,1,0:T(8,128)(2,1)S(1)}, u32[]{:S(2)}, u32[]{:S(2)}) async-start(bf16[16,16,128]{2,1,0:T(8,128)(2,1)} %copy.213), calls=%async_computation.1 | async-start | bytes 131072 | tf_op jit(solution)/shard_map/all_to_all | solution.py:34
  74.8 22.1 %all-to-all-start.2 = ((bf16[16,8,2880]{2,1,0:T(8,128)(2,1)}), bf16[16,8,2880]{2,1,0:T(8,128)(2,1)}, u32[]{:S(2)}, u32[]{:S(2)}) async-start(bf16[16,8,2880]{2,1,0:T(8,128)(2,1)} %bitcast.212), calls=%async_computation.2 | async-start | bytes 1507328 | tf_op jit(solution)/shard_map/all_to_all | solution.py:34
  103.6 54.8 %all-to-all-start.3 = ((bf16[16,8,2944]{2,1,0:T(8,128)(2,1)}), bf16[16,8,2944]{2,1,0:T(8,128)(2,1)}, u32[]{:S(2)}, u32[]{:S(2)}) async-start(bf16[16,8,2944]{2,1,0:T(8,128)(2,1)} %bitcast.211), calls=%async_computation.3 | async-start | bytes 1507328 | tf_op jit(solution)/shard_map/all_to_all | solution.py:34
  138.1 41.0 %collective-permute-start.2 = (bf16[2880,384]{1,0:T(8,128)(2,1)}, bf16[2880,384]{1,0:T(8,128)(2,1)S(1)}, u32[]{:S(2)}, u32[]{:S(2)}) collective-permute-start(bf16[2880,384]{1,0:T(8,128)(2,1)} %constant_dynamic-update-slice_fusion), channel_id=1, source_target_pairs={{0,16},{16,0},{1,17},{17,1},{2,18},{18,2},{3,19},{19,3},{4,20},{20... | collective-permute-start | bytes 6635528 | tf_op jit(solution)/shard_map/ppermute | solution.py:43
  144.6 36.2 %copy-start.33 = (f32[4,8,128]{2,1,0:T(8,128)}, f32[4,8,128]{2,1,0:T(8,128)S(1)}, u32[]{:S(2)}) copy-start(f32[4,8,128]{2,1,0:T(8,128)S(1)} %fusion.11) | copy-start | bytes 49156
  164.4 29.7 %collective-permute-start.1 = (f32[8,128]{1,0:T(8,128)}, f32[8,128]{1,0:T(8,128)}, u32[]{:S(2)}, u32[]{:S(2)}) collective-permute-start(f32[8,128]{1,0:T(8,128)} %broadcast_in_dim.289), channel_id=1, source_target_pairs={{0,16},{16,0},{1,17},{17,1},{2,18},{18,2},{3,19},{19,3},{4,20},{20... | collective-permute-start | bytes 12296 | tf_op jit(solution)/shard_map/ppermute | solution.py:43
  185.9 31.3 %all-to-all-start.4 = ((bf16[16,4,2944]{2,1,0:T(4,128)(2,1)}), bf16[16,4,2944]{2,1,0:T(4,128)(2,1)}, u32[]{:S(2)}, u32[]{:S(2)}) async-start(bf16[16,4,2944]{2,1,0:T(4,128)(2,1)} %pad_maximum_fusion), calls=%async_computation.4 | async-start | bytes 753664 | tf_op jit(solution)/shard_map/all_to_all | solution.py:34
  226.1 14.1 %copy-start.4 = (bf16[1,128,2880]{1,2,0:T(8,128)(2,1)S(1)}, bf16[1,128,2880]{1,2,0:T(8,128)(2,1)}, u32[]{:S(2)}) copy-start(bf16[1,128,2880]{1,2,0:T(8,128)(2,1)} %param.31) | copy-start | bytes 2211844
  226.1 14.1 %copy-start.66 = (f32[128]{0:T(128)S(1)}, f32[128]{0:T(128)}, u32[]{:S(2)}) copy-start(f32[128]{0:T(128)} %copy-done.65) | copy-start | bytes 1540
  226.8 14.9 %copy-start.10 = (bf16[4,64,8,128]{3,1,2,0:T(8,128)(2,1)S(1)}, bf16[4,64,8,128]{3,1,2,0:T(8,128)(2,1)}, u32[]{:S(2)}) copy-start(bf16[4,64,8,128]{3,1,2,0:T(8,128)(2,1)} %fusion.22) | copy-start | bytes 1572868
  227.1 27.5 %copy-start.69 = (pred[2,4,128]{2,1,0:T(4,128)(4,1)S(1)}, pred[2,4,128]{2,1,0:T(4,128)(4,1)}, u32[]{:S(2)}) copy-start(pred[2,4,128]{2,1,0:T(4,128)(4,1)} %broadcast_select_fusion) | copy-start | bytes 3076
  228.4 14.9 %all-to-all-start.5 = ((f32[32,1,128]{2,1,0:T(1,128)}), f32[32,1,128]{2,1,0:T(1,128)S(1)}, u32[]{:S(2)}, u32[]{:S(2)}) async-start(f32[32,1,128]{2,1,0:T(1,128)} %broadcast_in_dim.312), calls=%async_computation.5 | async-start | bytes 32768 | tf_op jit(solution)/shard_map/all_to_all | solution.py:34
  237.9 28.4 %collective-permute-start.3 = (bf16[128,512]{1,0:T(8,128)(2,1)S(1)}, bf16[128,512]{1,0:T(8,128)(2,1)S(1)}, u32[]{:S(2)}, u32[]{:S(2)}) collective-permute-start(bf16[128,512]{1,0:T(8,128)(2,1)S(1)} %pad_maximum_fusion.3), channel_id=1, source_target_pairs={{16,0},{32,16},{48,32},{64,48},{80,64},{96,80},{112,96},{128,112},... | collective-permute-start | bytes 393224 | tf_op jit(solution)/shard_map/ppermute | solution.py:50
  243.9 22.0 %all-to-all-start.6 = ((f32[16,1,128]{2,1,0:T(1,128)}), f32[16,1,128]{2,1,0:T(1,128)S(1)}, u32[]{:S(2)}, u32[]{:S(2)}) async-start(f32[16,1,128]{2,1,0:T(1,128)} %broadcast_in_dim.313), calls=%async_computation.6 | async-start | bytes 16384 | tf_op jit(solution)/shard_map/all_to_all | solution.py:34
  (70 other events, 380.6 us)
Sparse Core Ops, SparseCore 0:
  11.0 132.6 all-gather.1

commit v3 on v2

--- a/solution.py
+++ b/solution.py
@@ -71,7 +71,9 @@
     return mixed.reshape(mixed.shape[0], QUERY_HEADS * HEAD_SIZE).astype(BF16)
 
 
-def head_grads(probs, probs_low, sink_probs, query_rows, key_rows, value_rows, grad_attended):
+def head_grads(
+    probs, probs_low, sink_probs, query_rows, key_rows, value_rows, grad_attended, scale
+):
     tokens, keys = query_rows.shape[0], key_rows.shape[0]
     per_group = QUERY_HEADS // KEY_VALUE_HEADS
     q = query_rows.reshape(tokens, KEY_VALUE_HEADS, per_group, HEAD_SIZE)
@@ -81,11 +83,11 @@
     grad_prob = jnp.einsum("baqj,eaj->aqbe", g, v, preferred_element_type=F32)
     spread = jnp.sum(probs * grad_prob, axis=3)
     grad_score = (probs * (grad_prob - spread[..., None])).astype(BF16)
-    scaling = HEAD_SIZE**-0.5
+    scaling = HEAD_SIZE**-0.5 * scale
     grad_q = jnp.einsum("amlh,hai->lami", grad_score, k, preferred_element_type=F32) * scaling
     grad_k = jnp.einsum("ujko,kujm->oum", grad_score, q, preferred_element_type=F32) * scaling
-    grad_v = jnp.einsum("ujko,kujm->oum", probs_low, g, preferred_element_type=F32)
-    grad_sinks = -jnp.sum(sink_probs * spread, axis=2).reshape(QUERY_HEADS)
+    grad_v = jnp.einsum("ujko,kujm->oum", probs_low, g, preferred_element_type=F32) * scale
+    grad_sinks = -jnp.sum(sink_probs * spread, axis=2).reshape(QUERY_HEADS) * scale
     return (
         grad_q.reshape(tokens, QUERY_HEADS * HEAD_SIZE).astype(BF16),
         grad_k.reshape(keys, KEY_VALUE_HEADS * HEAD_SIZE),
@@ -131,14 +133,9 @@
     pick = slot_hot.reshape(SLOTS, tokens)
     pick_low = pick.astype(BF16)
     slot_expert = jnp.repeat(window, CAP)
-    same = dot_last(pick_low, pick_low)
-    primary = jnp.sum(jnp.tril(same, -1), axis=1) == 0
-    place = jnp.where(primary[:, None], pick, False)
-    taken = jnp.any(pick, axis=0)
 
     shard = jnp.stack([expert_gate, expert_up, expert_down])
     gathered = to_all(shard, "dp")
-    out_full = lax.all_gather(out_weight, "dp", axis=0, tiled=True)
     hid = expert_gate.shape[1]
 
     halo = along_seq(jnp.concatenate([key_rows[0], value_matrix[0]], axis=1), 1)
@@ -177,17 +174,22 @@
         [columns, jnp.broadcast_to(facts_row[None], (dp_count, 1, lanes))], axis=1
     )
     sent = jnp.pad(sent, ((0, 0), (0, 2 * SLOTS - SLOTS - 1), (0, 0)))
-    sent, gathered = lax.optimization_barrier((sent, gathered))
+    sent, gathered, late_weight = lax.optimization_barrier((sent, gathered, out_weight))
+    out_full = lax.all_gather(late_weight, "dp", axis=0, tiled=True)
     arrived = exchange(sent, "dp")
     facts_all = arrived[:, SLOTS, :3].astype(F32)
     partial = dot32(arrived[:, :SLOTS].reshape(dp_count * SLOTS, lanes), out_weight)
-    partial = exchange(partial.astype(BF16).reshape(dp_count, SLOTS, D), "dp")
+    partial, residual_rows, upstream_rows, pick_low = lax.optimization_barrier(
+        (partial.astype(BF16).reshape(dp_count, SLOTS, D), residual[0], upstream[0], pick_low)
+    )
+    partial = exchange(partial, "dp")
+    pick = pick_low > 0
     projected = jnp.sum(partial.astype(F32), axis=0)
     own_block = jnp.concatenate([gathered[:, i].reshape(D, -1) for i in range(3)], axis=1)
     other_block = swap_cores(own_block)
 
-    residual_slots = dot32(pick_low, residual[0])
-    upstream_slots = dot32(pick_low, upstream[0]).astype(BF16)
+    residual_slots = dot32(pick_low, residual_rows)
+    upstream_slots = dot32(pick_low, upstream_rows).astype(BF16)
     mid = (residual_slots + projected).astype(BF16)
     mid_wide = lax.optimization_barrier(mid).astype(F32)
     inv_rms = lax.rsqrt(jnp.mean(mid_wide * mid_wide, axis=1, keepdims=True) + NORM_EPS)
@@ -216,13 +218,18 @@
     source = (at // SLOTS) * CAP + at % CAP + jnp.where(at % SLOTS >= CAP, SLOTS, 0)
     arrange = (source[:, None] == at[None, :]).astype(BF16)
     by_expert = dot32(arrange, both).astype(BF16).reshape(EW, 1, 2 * CAP, PADDED)
+    query_late, normed_late, route_late, upstream_rows, pick_low, by_expert = (
+        lax.optimization_barrier(
+            (query_rows, normed, route_rows, upstream_rows, pick_low, by_expert)
+        )
+    )
+    pick = pick_low > 0
+    same = dot_last(pick_low, pick_low)
+    primary = jnp.sum(jnp.tril(same, -1), axis=1) == 0
+    place = jnp.where(primary[:, None], pick, False)
+    taken = jnp.any(pick, axis=0)
     outgoing = jnp.broadcast_to(by_expert, (EW, chips // EW, 2 * CAP, PADDED))
     came = exchange(outgoing.reshape(chips, 2 * CAP, PADDED), "z")
-    count_parts = jnp.sum(came[:, 0, D : D + 2].astype(F32), axis=0)
-    core_count = count_parts[0] * 64.0 + count_parts[1]
-    token_total = core_count + swap_cores(jnp.full((8, 128), core_count))[0, 0]
-    token_scale = -advantage * all_tokens / token_total
-    loss_weight = token_scale * mask_wide
 
     rows = came.reshape(chips * 2 * CAP, PADDED)[:, :D]
     shares = 0.0
@@ -250,12 +257,27 @@
     share_3 = shares - share_1 - share_2
     tail = jnp.pad(jnp.stack([share_1, share_2, share_3], axis=1), ((0, 0), (0, PADDED - D - 3)))
     back = jnp.concatenate([piece, tail], axis=1).astype(BF16)
-    back = exchange(back.reshape(chips, CAP, PADDED), "z")
-    cot_rows = (loss_weight[:, None] * upstream[0].astype(F32)).astype(BF16)
-    probs, sink_probs = head_scores(query_rows, keys_here, head_sink_logits, visible(row_index))
-    grad_attended = jnp.where(taken[:, None], 0.0, dot_last(cot_rows, out_full)).astype(BF16)
+    masked = jnp.where(mask_wide[:, None] > 0.0, upstream_rows, jnp.zeros_like(upstream_rows))
+    back, masked = lax.optimization_barrier((back.reshape(chips, CAP, PADDED), masked))
+    back = exchange(back, "z")
+
+    grad_attended = jnp.where(taken[:, None], 0.0, dot_last(masked, out_full)).astype(BF16)
+    came, grad_attended = lax.optimization_barrier((came, grad_attended))
+    count_parts = jnp.sum(came[:, 0, D : D + 2].astype(F32), axis=0)
+    core_count = count_parts[0] * 64.0 + count_parts[1]
+    token_total = core_count + swap_cores(jnp.full((8, 128), core_count))[0, 0]
+    token_scale = -advantage * all_tokens / token_total
+    loss_weight = token_scale * mask_wide
+    probs, sink_probs = head_scores(query_late, keys_here, head_sink_logits, visible(row_index))
     grad_q, grad_k, grad_v, grad_sinks = head_grads(
-        probs, probs.astype(BF16), sink_probs, query_rows, keys_here, values_here, grad_attended
+        probs,
+        probs.astype(BF16),
+        sink_probs,
+        query_late,
+        keys_here,
+        values_here,
+        grad_attended,
+        token_scale,
     )
     back, grad_q, grad_k, grad_v, grad_sinks = lax.optimization_barrier(
         (back, grad_q, grad_k, grad_v, grad_sinks)
@@ -264,8 +286,8 @@
     summed = summed.reshape(SLOTS, PADDED)
     share_slots = jnp.sum(summed[:, D : D + 3], axis=1)
 
-    logits = dot32(normed, router)
-    route_slots = dot32(pick_low, route_rows.astype(BF16)).astype(jnp.int32)
+    logits = dot32(normed_late, router)
+    route_slots = dot32(pick_low, route_late.astype(BF16)).astype(jnp.int32)
     route_hot = route_slots[:, :, None] == jnp.arange(EXPERTS, dtype=jnp.int32)
     route_logits = jnp.sum(jnp.where(route_hot, logits[:, None, :], 0.0), axis=2)
     raised = jnp.exp(route_logits)
@@ -304,6 +326,7 @@
         keys_here,
         values_here,
         attended_grad_slots,
+        1.0,
     )
     sinks = jnp.pad(grad_sinks + slot_sinks, (0, 128 - QUERY_HEADS))[None]
     sinks = jnp.sum(to_all(sinks, ("core", "dp")), axis=0)
@@ -314,6 +337,7 @@
     onward = along_seq(onward, -1).astype(F32)
     grad_key_rows = (grad_k[WINDOW:] + onward[:, :kv_width]).astype(BF16)
     grad_value_rows = (grad_v[WINDOW:] + onward[:, kv_width:]).astype(BF16)
+    cot_rows = (loss_weight[:, None] * upstream_rows.astype(F32)).astype(BF16)
     put = place.astype(BF16)
     by_token = (((0,), (0,)), ((), ()))
     grad_residual = jnp.where(

time: 276 us -> 268 us (0.971)
  waiting for transfers between devices: 39.2 us -> 55.1 us
  starting transfers between devices: 90 us -> 78.2 us
  local copies, waits for them, and re-layouts: 45.7 us -> 36.6 us
  matrix products: 47.9 us -> 43.5 us
    all_to_all x7, waiting for transfers between devices: 38.5 us -> 55.1 us  [exchange(): return lax.all_to_all(value, axis, split_axis=0, concat_axis=0, tiled=True)]
    ppermute x2, starting transfers between devices: 15 us -> 7.61 us  [swap_cores(): return lax.ppermute(value, 'core', [(0, 1), (1, 0)])]
    all_to_all x7, starting transfers between devices: 68 us -> 63.5 us  [exchange(): return lax.all_to_all(value, axis, split_axis=0, concat_axis=0, tiled=True)]
    unnamed x172 -> x186, local copies, waits for them, and re-layouts: 10.5 us -> 8.33 us
  transfers between devices with their start and end apart: 12 -> 12, of which waited for: 5 -> 5; matrix products, arithmetic and copies ran while one was open for 40% -> 35% of each run, Pallas kernels for 0% -> 0%
where the time goes in v3:
time: 268 us; the launch traced here: 266 us
  starting transfers between devices  78.2 us (29%)
  waiting for transfers between devices  55.1 us (21%)
  matrix products  43.5 us (16%)
  local copies, waits for them, and re-layouts  36.6 us (14%)
  other arithmetic  31.1 us (12%)
  between operations  21.5 us (8%)
    all_to_all x7, starting transfers between devices, exchange(): return lax.all_to_all(value, axis, split_axis=0, concat_axis=0, tiled=True)  63.5 us
    all_to_all x7, waiting for transfers between devices, exchange(): return lax.all_to_all(value, axis, split_axis=0, concat_axis=0, tiled=True)  55.1 us
    dot_general x6, matrix products, dot_last(): return lax.dot_general(a, b, CONTRACT_LAST, preferred_element_type=F32)  16.7 us
    dot_general x11, matrix products, dot32(): return jnp.dot(a, b, preferred_element_type=F32, **kw)  11.4 us
    unnamed x186, local copies, waits for them, and re-layouts  8.33 us
    ppermute x2, starting transfers between devices, swap_cores(): return lax.ppermute(value, 'core', [(0, 1), (1, 0)])  7.61 us
    ppermute x2, starting transfers between devices, along_seq(): lax.ppermute(value, ('z', 'core'), [(i, i + steps) for i in range(first,...  7.05 us
  transfers between devices with their start and end apart: 12, of which 5 were waited for; matrix products, arithmetic and copies ran while one was open for 35% of the time, Pallas kernels for 0%

profile of v3, /device:TPU:1, one launch (start us, length us, event | category | flops | bytes accessed | tf_op | source)
XLA Modules:
  0.0 266.0 jit_solution(5118661761922873861)
XLA Ops:
  8.8 4.9 %collective-permute-start = (bf16[128,512]{1,0:T(8,128)(2,1)}, bf16[128,512]{1,0:T(8,128)(2,1)}, u32[]{:S(2)}, u32[]{:S(2)}) collective-permute-start(bf16[128,512]{1,0:T(8,128)(2,1)} %pad_maximum_fusion.2), channel_id=1, source_target_pairs={{0,16},{16,32},{32,48},{48,64},{64,80},{80,96},{96,112},{112,128},... | collective-permute-start | bytes 393224 | tf_op jit(solution)/shard_map/ppermute | solution.py:50
  16.3 6.8 %all-to-all-start = ((bf16[16,3,180,128]{3,2,1,0:T(8,128)(2,1)}), bf16[16,3,180,128]{3,2,1,0:T(8,128)(2,1)S(1)}, u32[]{:S(2)}, u32[]{:S(2)}) async-start(bf16[16,3,180,128]{3,2,1,0:T(8,128)(2,1)} %broadcast_in_dim.284), calls=%async_computation | async-start | bytes 4521984 | tf_op jit(solution)/shard_map/all_to_all | solution.py:34
  38.0 16.0 %all-to-all-done = bf16[16,3,180,128]{3,2,1,0:T(8,128)(2,1)S(1)} async-done(((bf16[16,3,180,128]{3,2,1,0:T(8,128)(2,1)}), bf16[16,3,180,128]{3,2,1,0:T(8,128)(2,1)S(1)}, u32[]{:S(2)}, u32[]{:S(2)}) %all-to-all-start) | async-done | bytes 2211872 | tf_op jit(solution)/shard_map/all_to_all | solution.py:34
  61.5 4.5 %all-to-all-start.1 = ((bf16[16,16,128]{2,1,0:T(8,128)(2,1)}), bf16[16,16,128]{2,1,0:T(8,128)(2,1)}, u32[]{:S(2)}, u32[]{:S(2)}) async-start(bf16[16,16,128]{2,1,0:T(8,128)(2,1)} %copy.214), calls=%async_computation.1 | async-start | bytes 131072 | tf_op jit(solution)/shard_map/all_to_all | solution.py:34
  70.3 2.3 reshape_squeeze.11
  76.6 4.4 %collective-permute-start.1 = (bf16[2880,384]{1,0:T(8,128)(2,1)}, bf16[2880,384]{1,0:T(8,128)(2,1)}, u32[]{:S(2)}, u32[]{:S(2)}) collective-permute-start(bf16[2880,384]{1,0:T(8,128)(2,1)} %constant_dynamic-update-slice_fusion), channel_id=1, source_target_pairs={{0,16},{16,0},{1,17},{17,1},{2,18},{18,2},{3,19},{19,3},{4,20},{20... | collective-permute-start | bytes 6635528 | tf_op jit(solution)/shard_map/ppermute | solution.py:43
  83.1 2.3 copy.215
  85.4 6.9 %all-to-all-start.2 = ((bf16[16,8,2880]{2,1,0:T(8,128)(2,1)}), bf16[16,8,2880]{2,1,0:T(8,128)(2,1)S(1)}, u32[]{:S(2)}, u32[]{:S(2)}) async-start(bf16[16,8,2880]{2,1,0:T(8,128)(2,1)} %bitcast.24), calls=%async_computation.2 | async-start | bytes 1507328 | tf_op jit(solution)/shard_map/all_to_all | solution.py:34
  98.8 6.5 %all-to-all-done.2 = bf16[16,8,2880]{2,1,0:T(8,128)(2,1)S(1)} async-done(((bf16[16,8,2880]{2,1,0:T(8,128)(2,1)}), bf16[16,8,2880]{2,1,0:T(8,128)(2,1)S(1)}, u32[]{:S(2)}, u32[]{:S(2)}) %all-to-all-start.2) | async-done | bytes 737312 | tf_op jit(solution)/shard_map/all_to_all | solution.py:34
  108.4 15.8 %all-to-all-start.3 = ((bf16[16,8,2944]{2,1,0:T(8,128)(2,1)}), bf16[16,8,2944]{2,1,0:T(8,128)(2,1)S(1)}, u32[]{:S(2)}, u32[]{:S(2)}) async-start(bf16[16,8,2944]{2,1,0:T(8,128)(2,1)} %bitcast.39), calls=%async_computation.3 | async-start | bytes 1507328 | tf_op jit(solution)/shard_map/all_to_all | solution.py:34
  126.6 3.6 %fusion.3 = (f32[4,8,128]{2,1,0:T(8,128)S(1)}, f32[4,256,128,8]{2,1,3,0:T(8,128)}) fusion(pred[128,256]{0,1:T(8,128)(4,1)} %fusion.48, bf16[128,4,8,64]{0,3,2,1:T(8,128)(2,1)S(1)} %bitcast.210, bf16[128,4,64]{0,2,1:T(8,128)(2,1)} %bitcast.220, bf16[128,4,64]{0,2,1:T(8,128)(2,1)} %bitcast.224), kind=kOutput, calls=%fused_computation.7 | convolution fusion | flops 137621504 | bytes 4898816 | tf_op jit(solution)/shard_map/baqj,eaj->aqbe/dot_general | solution.py:58
  132.3 3.2 %fusion.11 = f32[4,8,128]{2,1,0:T(8,128)S(1)} fusion(f32[4,256,128,8]{2,1,3,0:T(8,128)} %get-tuple-element.93, f32[4,8,128]{2,1,0:T(8,128)S(1)} %broadcast_maximum_fusion, pred[128,256]{0,1:T(8,128)(4,1)} %fusion.48), kind=kLoop, calls=%fused_computation.22 | loop fusion | flops 5238784 | bytes 4259840 | tf_op jit(solution)/shard_map/reduce_sum | solution.py:64
  137.5 18.9 %all-to-all-done.3 = bf16[16,8,2944]{2,1,0:T(8,128)(2,1)S(1)} async-done(((bf16[16,8,2944]{2,1,0:T(8,128)(2,1)}), bf16[16,8,2944]{2,1,0:T(8,128)(2,1)S(1)}, u32[]{:S(2)}, u32[]{:S(2)}) %all-to-all-start.3) | async-done | bytes 753696 | tf_op jit(solution)/shard_map/all_to_all | solution.py:34
  156.4 2.2 convolution_bitcast_fusion.4
  161.4 2.3 convolution_bitcast_fusion.3
  168.4 12.8 %all-to-all-start.4 = ((bf16[16,4,2944]{2,1,0:T(4,128)(2,1)}), bf16[16,4,2944]{2,1,0:T(4,128)(2,1)}, u32[]{:S(2)}, u32[]{:S(2)}) async-start(bf16[16,4,2944]{2,1,0:T(4,128)(2,1)} %pad_maximum_fusion), calls=%async_computation.4 | async-start | bytes 753664 | tf_op jit(solution)/shard_map/all_to_all | solution.py:34
  181.3 6.2 %fusion.12 = bf16[128,2048]{1,0:T(8,128)(2,1)S(1)} fusion(bf16[128,2880]{0,1:T(8,128)(2,1)S(1)} %broadcast_select_fusion, bf16[2048,2880]{0,1:T(8,128)(2,1)} %all-gather.2.cloned.1.call-done, pred[128]{0:T(512)(128)(4,1)} %get-tuple-element.56), kind=kOutput, calls=%fused_computation.24 | convolution fusion | flops 1510473728 | bytes 13058176 | tf_op jit(solution)/shard_map/dot_general | solution.py:30
  190.3 3.2 %collective-permute-start.2 = (f32[8,128]{1,0:T(8,128)}, f32[8,128]{1,0:T(8,128)}, u32[]{:S(2)}, u32[]{:S(2)}) collective-permute-start(f32[8,128]{1,0:T(8,128)} %broadcast_in_dim.297), channel_id=1, source_target_pairs={{0,16},{16,0},{1,17},{17,1},{2,18},{18,2},{3,19},{19,3},{4,20},{20... | collective-permute-start | bytes 12296 | tf_op jit(solution)/shard_map/ppermute | solution.py:43
  193.8 3.8 %fusion = (f32[4,8,128]{2,1,0:T(8,128)S(1)}, f32[4,256,128,8]{2,1,3,0:T(8,128)S(1)}) fusion(f32[4,8,128]{2,1,0:T(8,128)S(1)} %copy-done.52, f32[4,8,128]{2,1,0:T(8,128)S(1)} %copy-done.35, f32[4,256,128,8]{2,1,3,0:T(8,128)} %get-tuple-element.93, pred[128,256]{0,1:T(8,128)(4,1)S(1)} %copy-done.19, bf16[128,4,8,64]{0,3,2,1:T(8,128)(2,1)S(1)} %bitcast.227, ...), kind=kOutput, calls=%fused_computation.2 | convolution fusion | flops 141815808 | bytes 9125888 | tf_op jit(solution)/shard_map/baqj,eaj->aqbe/dot_general | solution.py:83
  214.1 6.1 %convolution_convert_fusion.6 = bf16[8,2048]{1,0:T(8,128)(2,1)S(1)} fusion(bf16[2048,2880]{0,1:T(8,128)(2,1)} %all-gather.2.cloned.1.call-done, f32[8,2880]{1,0:T(8,128)S(1)} %get-tuple-element.97, bf16[8,2880]{1,0:T(8,128)(2,1)S(1)} %fusion.9, bf16[8,2880]{1,0:T(8,128)(2,1)S(1)} %copy-done.27, f32[8]{0:T(128)S(1)} %broadcast_multiply_fusion.1, ...), kind=kOutput, calls=%fused_computation.29 | convolution fusion | flops 94618624 | bytes 12013672 | tf_op jit(solution)/shard_map/dot_general | solution.py:30
  222.3 5.2 %all-to-all-start.5 = ((f32[32,1,128]{2,1,0:T(1,128)}), f32[32,1,128]{2,1,0:T(1,128)S(1)}, u32[]{:S(2)}, u32[]{:S(2)}) async-start(f32[32,1,128]{2,1,0:T(1,128)} %broadcast_in_dim.317), calls=%async_computation.5 | async-start | bytes 32768 | tf_op jit(solution)/shard_map/all_to_all | solution.py:34
  230.7 3.6 %all-to-all-done.5 = f32[32,1,128]{2,1,0:T(1,128)S(1)} async-done(((f32[32,1,128]{2,1,0:T(1,128)}), f32[32,1,128]{2,1,0:T(1,128)S(1)}, u32[]{:S(2)}, u32[]{:S(2)}) %all-to-all-start.5) | async-done | bytes 16416 | tf_op jit(solution)/shard_map/all_to_all | solution.py:34
  234.9 11.7 %all-to-all-start.6 = ((f32[16,1,128]{2,1,0:T(1,128)}), f32[16,1,128]{2,1,0:T(1,128)S(1)}, u32[]{:S(2)}, u32[]{:S(2)}) async-start(f32[16,1,128]{2,1,0:T(1,128)} %broadcast_in_dim.318), calls=%async_computation.6 | async-start | bytes 16384 | tf_op jit(solution)/shard_map/all_to_all | solution.py:34
  247.8 10.0 %all-to-all-done.6 = f32[16,1,128]{2,1,0:T(1,128)S(1)} async-done(((f32[16,1,128]{2,1,0:T(1,128)}), f32[16,1,128]{2,1,0:T(1,128)S(1)}, u32[]{:S(2)}, u32[]{:S(2)}) %all-to-all-start.6) | async-done | bytes 8224 | tf_op jit(solution)/shard_map/all_to_all | solution.py:34
  (343 shorter events, 81.2 us)
Async XLA Ops:
  7.2 78.2 %copy-start = (bf16[1,128,2880]{1,2,0:T(8,128)(2,1)S(1)}, bf16[1,128,2880]{1,2,0:T(8,128)(2,1)}, u32[]{:S(2)}) copy-start(bf16[1,128,2880]{1,2,0:T(8,128)(2,1)} %param.20) | copy-start | bytes 2211844
  8.8 25.0 %collective-permute-start = (bf16[128,512]{1,0:T(8,128)(2,1)}, bf16[128,512]{1,0:T(8,128)(2,1)}, u32[]{:S(2)}, u32[]{:S(2)}) collective-permute-start(bf16[128,512]{1,0:T(8,128)(2,1)} %pad_maximum_fusion.2), channel_id=1, source_target_pairs={{0,16},{16,32},{32,48},{48,64},{64,80},{80,96},{96,112},{112,128},... | collective-permute-start | bytes 393224 | tf_op jit(solution)/shard_map/ppermute | solution.py:50
  16.3 37.7 %all-to-all-start = ((bf16[16,3,180,128]{3,2,1,0:T(8,128)(2,1)}), bf16[16,3,180,128]{3,2,1,0:T(8,128)(2,1)S(1)}, u32[]{:S(2)}, u32[]{:S(2)}) async-start(bf16[16,3,180,128]{3,2,1,0:T(8,128)(2,1)} %broadcast_in_dim.284), calls=%async_computation | async-start | bytes 4521984 | tf_op jit(solution)/shard_map/all_to_all | solution.py:34
  23.1 158.1 %all-gather.2.cloned.1.call-start = ((), (), s32[]{:S(2)}) async-start(), calls=%async_computation.7 | async-start | bytes 12533760 | tf_op jit(solution)/shard_map/all_gather | solution.py:178
  25.9 28.1 %copy-start.82 = (pred[256]{0:T(512)(128)(4,1)}, pred[256]{0:T(512)(128)(4,1)S(1)}, u32[]{:S(2)}) copy-start(pred[256]{0:T(512)(128)(4,1)S(1)} %compare_or_fusion) | copy-start | bytes 772
  27.5 26.5 %copy-start.67 = (pred[8,256]{1,0:T(8,128)(4,1)}, pred[8,256]{1,0:T(8,128)(4,1)S(1)}, u32[]{:S(2)}) copy-start(pred[8,256]{1,0:T(8,128)(4,1)S(1)} %fusion.83) | copy-start | bytes 6148
  31.0 27.6 %copy-start.81 = (f32[2,128]{1,0:T(2,128)S(1)}, f32[2,128]{1,0:T(2,128)}, u32[]{:S(2)}) copy-start(f32[2,128]{1,0:T(2,128)} %copy-done.80) | copy-start | bytes 3076
  31.0 27.6 %copy-start.84 = (pred[128,2]{0,1:T(4,128)(4,1)S(1)}, pred[128,2]{0,1:T(4,128)(4,1)}, u32[]{:S(2)}) copy-start(pred[128,2]{0,1:T(4,128)(4,1)} %copy-done.83) | copy-start | bytes 772
  58.6 38.7 %copy-start.46 = (bf16[8,128]{1,0:T(8,128)(2,1)}, bf16[8,128]{1,0:T(8,128)(2,1)S(1)}, u32[]{:S(2)}) copy-start(bf16[8,128]{1,0:T(8,128)(2,1)S(1)} %and_convert_fusion) | copy-start | bytes 6148
  61.5 19.6 %all-to-all-start.1 = ((bf16[16,16,128]{2,1,0:T(8,128)(2,1)}), bf16[16,16,128]{2,1,0:T(8,128)(2,1)}, u32[]{:S(2)}, u32[]{:S(2)}) async-start(bf16[16,16,128]{2,1,0:T(8,128)(2,1)} %copy.214), calls=%async_computation.1 | async-start | bytes 131072 | tf_op jit(solution)/shard_map/all_to_all | solution.py:34
  74.6 31.9 %copy-start.63 = (f32[2880]{0:T(1024)S(1)}, f32[2880]{0:T(1024)}, u32[]{:S(2)}) copy-start(f32[2880]{0:T(1024)} %param.22) | copy-start | bytes 34564
  76.6 84.7 %collective-permute-start.1 = (bf16[2880,384]{1,0:T(8,128)(2,1)}, bf16[2880,384]{1,0:T(8,128)(2,1)}, u32[]{:S(2)}, u32[]{:S(2)}) collective-permute-start(bf16[2880,384]{1,0:T(8,128)(2,1)} %constant_dynamic-update-slice_fusion), channel_id=1, source_target_pairs={{0,16},{16,0},{1,17},{17,1},{2,18},{18,2},{3,19},{19,3},{4,20},{20... | collective-permute-start | bytes 6635528 | tf_op jit(solution)/shard_map/ppermute | solution.py:43
  83.1 41.2 %copy-start.74 = (s32[1,128,4]{1,2,0:T(4,128)S(1)}, s32[1,128,4]{1,2,0:T(4,128)}, u32[]{:S(2)}) copy-start(s32[1,128,4]{1,2,0:T(4,128)} %param.27) | copy-start | bytes 6148
  83.1 41.3 %copy-start.3 = (bf16[2880,128]{1,0:T(8,128)(2,1)S(1)}, bf16[2880,128]{1,0:T(8,128)(2,1)}, u32[]{:S(2)}) copy-start(bf16[2880,128]{1,0:T(8,128)(2,1)} %param.23) | copy-start | bytes 2211844
  85.4 39.3 %copy-start.86 = (s32[8]{0:T(128)S(1)}, s32[8]{0:T(128)}, u32[]{:S(2)}) copy-start(s32[8]{0:T(128)} %iota_add_fusion.2) | copy-start | bytes 100
  85.4 19.8 %all-to-all-start.2 = ((bf16[16,8,2880]{2,1,0:T(8,128)(2,1)}), bf16[16,8,2880]{2,1,0:T(8,128)(2,1)S(1)}, u32[]{:S(2)}, u32[]{:S(2)}) async-start(bf16[16,8,2880]{2,1,0:T(8,128)(2,1)} %bitcast.24), calls=%async_computation.2 | async-start | bytes 1507328 | tf_op jit(solution)/shard_map/all_to_all | solution.py:34
  98.8 27.8 %copy-start.26 = (bf16[8,2880]{1,0:T(8,128)(2,1)}, bf16[8,2880]{1,0:T(8,128)(2,1)S(1)}, u32[]{:S(2)}) copy-start(bf16[8,2880]{1,0:T(8,128)(2,1)S(1)} %convolution_convert_fusion.3) | copy-start | bytes 138244
  108.4 48.0 %all-to-all-start.3 = ((bf16[16,8,2944]{2,1,0:T(8,128)(2,1)}), bf16[16,8,2944]{2,1,0:T(8,128)(2,1)S(1)}, u32[]{:S(2)}, u32[]{:S(2)}) async-start(bf16[16,8,2944]{2,1,0:T(8,128)(2,1)} %bitcast.39), calls=%async_computation.3 | async-start | bytes 1507328 | tf_op jit(solution)/shard_map/all_to_all | solution.py:34
  130.2 28.4 %copy-start.28 = (f32[4,8,128]{2,1,0:T(8,128)}, f32[4,8,128]{2,1,0:T(8,128)S(1)}, u32[]{:S(2)}) copy-start(f32[4,8,128]{2,1,0:T(8,128)S(1)} %get-tuple-element.92) | copy-start | bytes 49156
  168.4 41.6 %all-to-all-start.4 = ((bf16[16,4,2944]{2,1,0:T(4,128)(2,1)}), bf16[16,4,2944]{2,1,0:T(4,128)(2,1)}, u32[]{:S(2)}, u32[]{:S(2)}) async-start(bf16[16,4,2944]{2,1,0:T(4,128)(2,1)} %pad_maximum_fusion), calls=%async_computation.4 | async-start | bytes 753664 | tf_op jit(solution)/shard_map/all_to_all | solution.py:34
  190.3 9.9 %collective-permute-start.2 = (f32[8,128]{1,0:T(8,128)}, f32[8,128]{1,0:T(8,128)}, u32[]{:S(2)}, u32[]{:S(2)}) collective-permute-start(f32[8,128]{1,0:T(8,128)} %broadcast_in_dim.297), channel_id=1, source_target_pairs={{0,16},{16,0},{1,17},{17,1},{2,18},{18,2},{3,19},{19,3},{4,20},{20... | collective-permute-start | bytes 12296 | tf_op jit(solution)/shard_map/ppermute | solution.py:43
  222.3 12.0 %all-to-all-start.5 = ((f32[32,1,128]{2,1,0:T(1,128)}), f32[32,1,128]{2,1,0:T(1,128)S(1)}, u32[]{:S(2)}, u32[]{:S(2)}) async-start(f32[32,1,128]{2,1,0:T(1,128)} %broadcast_in_dim.317), calls=%async_computation.5 | async-start | bytes 32768 | tf_op jit(solution)/shard_map/all_to_all | solution.py:34
  228.2 30.2 %collective-permute-start.3 = (bf16[128,512]{1,0:T(8,128)(2,1)S(1)}, bf16[128,512]{1,0:T(8,128)(2,1)S(1)}, u32[]{:S(2)}, u32[]{:S(2)}) collective-permute-start(bf16[128,512]{1,0:T(8,128)(2,1)S(1)} %pad_maximum_fusion.3), channel_id=1, source_target_pairs={{16,0},{32,16},{48,32},{64,48},{80,64},{96,80},{112,96},{128,112},... | collective-permute-start | bytes 393224 | tf_op jit(solution)/shard_map/ppermute | solution.py:50
  234.9 22.9 %all-to-all-start.6 = ((f32[16,1,128]{2,1,0:T(1,128)}), f32[16,1,128]{2,1,0:T(1,128)S(1)}, u32[]{:S(2)}, u32[]{:S(2)}) async-start(f32[16,1,128]{2,1,0:T(1,128)} %broadcast_in_dim.318), calls=%async_computation.6 | async-start | bytes 16384 | tf_op jit(solution)/shard_map/all_to_all | solution.py:34
  (77 other events, 533.2 us)
Sparse Core Ops, SparseCore 0:
  54.3 119.0 all-gather.1

commit v4 on v3

--- a/solution.py
+++ b/solution.py
@@ -1,6 +1,8 @@
 import jax
 import jax.numpy as jnp
 from jax import lax
+from jax.experimental import pallas as pl
+from jax.experimental.pallas import tpu as pltpu
 from jax.sharding import Mesh, PartitionSpec as P
 
 D = 2880
@@ -71,29 +73,87 @@
     return mixed.reshape(mixed.shape[0], QUERY_HEADS * HEAD_SIZE).astype(BF16)
 
 
-def head_grads(
-    probs, probs_low, sink_probs, query_rows, key_rows, value_rows, grad_attended, scale
-):
+def head_spread(probs, value_rows, grad_attended):
+    tokens, keys = grad_attended.shape[0], value_rows.shape[0]
+    per_group = QUERY_HEADS // KEY_VALUE_HEADS
+    v = value_rows.reshape(keys, KEY_VALUE_HEADS, HEAD_SIZE)
+    g = grad_attended.reshape(tokens, KEY_VALUE_HEADS, per_group, HEAD_SIZE)
+    grad_prob = jnp.einsum("baqj,eaj->aqbe", g, v, preferred_element_type=F32)
+    return grad_prob, jnp.sum(probs * grad_prob, axis=3)
+
+
+def head_grads(probs, grad_prob, spread, query_rows, key_rows, grad_attended, scale):
     tokens, keys = query_rows.shape[0], key_rows.shape[0]
     per_group = QUERY_HEADS // KEY_VALUE_HEADS
     q = query_rows.reshape(tokens, KEY_VALUE_HEADS, per_group, HEAD_SIZE)
     k = key_rows.reshape(keys, KEY_VALUE_HEADS, HEAD_SIZE)
-    v = value_rows.reshape(keys, KEY_VALUE_HEADS, HEAD_SIZE)
     g = grad_attended.reshape(tokens, KEY_VALUE_HEADS, per_group, HEAD_SIZE)
-    grad_prob = jnp.einsum("baqj,eaj->aqbe", g, v, preferred_element_type=F32)
-    spread = jnp.sum(probs * grad_prob, axis=3)
     grad_score = (probs * (grad_prob - spread[..., None])).astype(BF16)
+    probs_low = probs.astype(BF16)
     scaling = HEAD_SIZE**-0.5 * scale
     grad_q = jnp.einsum("amlh,hai->lami", grad_score, k, preferred_element_type=F32) * scaling
     grad_k = jnp.einsum("ujko,kujm->oum", grad_score, q, preferred_element_type=F32) * scaling
     grad_v = jnp.einsum("ujko,kujm->oum", probs_low, g, preferred_element_type=F32) * scale
-    grad_sinks = -jnp.sum(sink_probs * spread, axis=2).reshape(QUERY_HEADS) * scale
     return (
         grad_q.reshape(tokens, QUERY_HEADS * HEAD_SIZE).astype(BF16),
         grad_k.reshape(keys, KEY_VALUE_HEADS * HEAD_SIZE),
         grad_v.reshape(keys, KEY_VALUE_HEADS * HEAD_SIZE),
-        grad_sinks,
-    )
+    )
+
+
+def experts_kernel(rows_ref, own_ref, other_ref, out_ref):
+    count = rows_ref.shape[0]
+    kept = count // 2
+    hid = own_ref.shape[1] // 3
+    at = lax.broadcasted_iota(jnp.int32, (kept, count), 0)
+    source = (at // CAP) * (2 * CAP) + at % CAP
+    column = lax.broadcasted_iota(jnp.int32, (kept, count), 1)
+    rows = rows_ref[:, :D]
+    normed = dot32((column == source).astype(BF16), rows).astype(BF16)
+    upstream = dot32((column == source + CAP).astype(BF16), rows).astype(BF16)
+    piece = jnp.zeros((kept, D), F32)
+    share = jnp.zeros((kept, 1), F32)
+    for block in (own_ref, other_ref):
+        pair = block[:, : 2 * hid]
+        pre = dot32(normed, pair)
+        up_down = dot32(upstream, block[:, 2 * hid :])
+        gate_pre, up_pre = pre[:, :hid], pre[:, hid:]
+        sigmoid_gate = jax.nn.sigmoid(GLU_SLOPE * gate_pre)
+        activation = ((up_pre + 1.0) * gate_pre * sigmoid_gate).astype(BF16)
+        share = share + jnp.sum(activation.astype(F32) * up_down, axis=1, keepdims=True)
+        grad_up = up_down * (gate_pre * sigmoid_gate)
+        grad_gate = (
+            up_down
+            * (up_pre + 1.0)
+            * (sigmoid_gate + GLU_SLOPE * gate_pre * sigmoid_gate * (1.0 - sigmoid_gate))
+        )
+        grads = jnp.concatenate([grad_gate, grad_up], axis=1).astype(BF16)
+        piece = piece + dot_last(grads, pair)
+    share_1 = share.astype(BF16).astype(F32)
+    share_2 = (share - share_1).astype(BF16).astype(F32)
+    share_3 = share - share_1 - share_2
+    lane = lax.broadcasted_iota(jnp.int32, (kept, PADDED - D), 1)
+    tail = jnp.where(lane == 0, share_1, jnp.where(lane == 1, share_2, 0.0))
+    tail = jnp.where(lane == 2, share_3, tail)
+    even = (D // 128) * 128
+    out_ref[:, :even] = piece[:, :even].astype(BF16)
+    out_ref[:, even:] = jnp.concatenate([piece[:, even:], tail], axis=1).astype(BF16)
+
+
+def experts_step(rows, own_block, other_block):
+    count, hid = rows.shape[0], own_block.shape[1] // 3
+    return pl.pallas_call(
+        experts_kernel,
+        out_shape=jax.ShapeDtypeStruct((count // 2, PADDED), BF16),
+        in_specs=[pl.BlockSpec(memory_space=pltpu.VMEM)] * 3,
+        out_specs=pl.BlockSpec(memory_space=pltpu.VMEM),
+        compiler_params=pltpu.CompilerParams(vmem_limit_bytes=24 << 20),
+        cost_estimate=pl.CostEstimate(
+            flops=2 * 2 * count // 2 * D * hid * 5,
+            bytes_accessed=2 * (2 * D * 3 * hid + 2 * count * PADDED),
+            transcendentals=count * hid,
+        ),
+    )(rows, own_block, other_block)
 
 
 def shards(
@@ -134,31 +194,33 @@
     pick_low = pick.astype(BF16)
     slot_expert = jnp.repeat(window, CAP)
 
-    shard = jnp.stack([expert_gate, expert_up, expert_down])
-    gathered = to_all(shard, "dp")
-    hid = expert_gate.shape[1]
-
-    halo = along_seq(jnp.concatenate([key_rows[0], value_matrix[0]], axis=1), 1)
+    shard = jnp.concatenate([expert_gate, expert_up, expert_down], axis=1)
+    spread_shard = jnp.broadcast_to(shard[None], (dp_count, *shard.shape))
+    spread_shard, own_keys, own_values = lax.optimization_barrier(
+        (spread_shard, key_rows[0], value_matrix[0])
+    )
+    gathered = exchange(spread_shard, "dp")
+
+    halo = along_seq(jnp.concatenate([own_keys, own_values], axis=1), 1)
     kv_width = key_rows.shape[2]
-    keys_here = jnp.concatenate([halo[:, :kv_width], key_rows[0]], axis=0)
-    values_here = jnp.concatenate([halo[:, kv_width:], value_matrix[0]], axis=0)
+    keys_here = jnp.concatenate([halo[:, :kv_width], own_keys], axis=0)
+    values_here = jnp.concatenate([halo[:, kv_width:], own_values], axis=0)
     row_index = jnp.arange(tokens, dtype=jnp.int32)[:, None]
     col_index = jnp.arange(WINDOW + tokens, dtype=jnp.int32)[None, :]
 
-    def visible(rows):
+    def visible(rows, columns):
         return (
-            (col_index >= rows + 1)
-            & (col_index <= rows + WINDOW)
-            & ((col_index >= WINDOW) | (seq_index > 0))
+            (columns >= rows + 1)
+            & (columns <= rows + WINDOW)
+            & ((columns >= WINDOW) | (seq_index > 0))
         )
 
     slot_rows = jnp.sum(jnp.where(pick, row_index[:, 0][None, :], 0), axis=1, keepdims=True)
     query_slots = dot32(pick_low, query_rows).astype(BF16)
     probs_slots, sink_slots = head_scores(
-        query_slots, keys_here, head_sink_logits, visible(slot_rows)
-    )
-    probs_slots_low = probs_slots.astype(BF16)
-    attended_slots = head_mix(probs_slots_low, values_here)
+        query_slots, keys_here, head_sink_logits, visible(slot_rows, col_index)
+    )
+    attended_slots = head_mix(probs_slots.astype(BF16), values_here)
 
     mask_wide = response_mask[0].astype(F32)
     facts = jnp.stack(
@@ -185,7 +247,7 @@
     partial = exchange(partial, "dp")
     pick = pick_low > 0
     projected = jnp.sum(partial.astype(F32), axis=0)
-    own_block = jnp.concatenate([gathered[:, i].reshape(D, -1) for i in range(3)], axis=1)
+    own_block = gathered.reshape(D, shard.shape[1])
     other_block = swap_cores(own_block)
 
     residual_slots = dot32(pick_low, residual_rows)
@@ -218,9 +280,18 @@
     source = (at // SLOTS) * CAP + at % CAP + jnp.where(at % SLOTS >= CAP, SLOTS, 0)
     arrange = (source[:, None] == at[None, :]).astype(BF16)
     by_expert = dot32(arrange, both).astype(BF16).reshape(EW, 1, 2 * CAP, PADDED)
-    query_late, normed_late, route_late, upstream_rows, pick_low, by_expert = (
+    query_late, normed_late, route_late, upstream_rows, pick_low, by_expert, row_late, col_late = (
         lax.optimization_barrier(
-            (query_rows, normed, route_rows, upstream_rows, pick_low, by_expert)
+            (
+                query_rows,
+                normed,
+                route_rows,
+                upstream_rows,
+                pick_low,
+                by_expert,
+                row_index,
+                col_index,
+            )
         )
     )
     pick = pick_low > 0
@@ -231,57 +302,29 @@
     outgoing = jnp.broadcast_to(by_expert, (EW, chips // EW, 2 * CAP, PADDED))
     came = exchange(outgoing.reshape(chips, 2 * CAP, PADDED), "z")
 
-    rows = came.reshape(chips * 2 * CAP, PADDED)[:, :D]
-    shares = 0.0
-    grads = []
-    for block in (own_block, other_block):
-        pre = dot32(rows, block).reshape(chips, 2 * CAP, 3 * hid)
-        up_down = pre[:, CAP:, 2 * hid :].reshape(chips * CAP, hid)
-        gate_pre = pre[:, :CAP, :hid].reshape(chips * CAP, hid)
-        up_pre = pre[:, :CAP, hid : 2 * hid].reshape(chips * CAP, hid)
-        sigmoid_gate = jax.nn.sigmoid(GLU_SLOPE * gate_pre)
-        activation = ((up_pre + 1.0) * gate_pre * sigmoid_gate).astype(BF16)
-        shares = shares + jnp.sum(activation.astype(F32) * up_down, axis=1)
-        grad_up = up_down * (gate_pre * sigmoid_gate)
-        grad_gate = (
-            up_down
-            * (up_pre + 1.0)
-            * (sigmoid_gate + GLU_SLOPE * gate_pre * sigmoid_gate * (1.0 - sigmoid_gate))
-        )
-        grads.append(jnp.concatenate([grad_gate, grad_up], axis=1).astype(BF16))
-    piece = dot_last(grads[0], own_block[:, : 2 * hid]) + dot_last(
-        grads[1], other_block[:, : 2 * hid]
-    )
-    share_1 = shares.astype(BF16).astype(F32)
-    share_2 = (shares - share_1).astype(BF16).astype(F32)
-    share_3 = shares - share_1 - share_2
-    tail = jnp.pad(jnp.stack([share_1, share_2, share_3], axis=1), ((0, 0), (0, PADDED - D - 3)))
-    back = jnp.concatenate([piece, tail], axis=1).astype(BF16)
-    masked = jnp.where(mask_wide[:, None] > 0.0, upstream_rows, jnp.zeros_like(upstream_rows))
-    back, masked = lax.optimization_barrier((back.reshape(chips, CAP, PADDED), masked))
+    back = experts_step(came.reshape(chips * 2 * CAP, PADDED), own_block, other_block)
+    back, mask_late = lax.optimization_barrier((back.reshape(chips, CAP, PADDED), mask_wide))
     back = exchange(back, "z")
 
+    masked = jnp.where(mask_late[:, None] > 0.0, upstream_rows, jnp.zeros_like(upstream_rows))
     grad_attended = jnp.where(taken[:, None], 0.0, dot_last(masked, out_full)).astype(BF16)
     came, grad_attended = lax.optimization_barrier((came, grad_attended))
     count_parts = jnp.sum(came[:, 0, D : D + 2].astype(F32), axis=0)
     core_count = count_parts[0] * 64.0 + count_parts[1]
     token_total = core_count + swap_cores(jnp.full((8, 128), core_count))[0, 0]
     token_scale = -advantage * all_tokens / token_total
-    loss_weight = token_scale * mask_wide
-    probs, sink_probs = head_scores(query_late, keys_here, head_sink_logits, visible(row_index))
-    grad_q, grad_k, grad_v, grad_sinks = head_grads(
-        probs,
-        probs.astype(BF16),
-        sink_probs,
-        query_late,
-        keys_here,
-        values_here,
-        grad_attended,
-        token_scale,
-    )
-    back, grad_q, grad_k, grad_v, grad_sinks = lax.optimization_barrier(
-        (back, grad_q, grad_k, grad_v, grad_sinks)
-    )
+    loss_weight = token_scale * mask_late
+    probs, sink_probs = head_scores(
+        query_late, keys_here, head_sink_logits, visible(row_late, col_late)
+    )
+    grad_prob, spread = head_spread(probs, values_here, grad_attended)
+    grad_q, grad_k, grad_v = head_grads(
+        probs, grad_prob, spread, query_late, keys_here, grad_attended, token_scale
+    )
+    back, grad_q, grad_k, grad_v, spread = lax.optimization_barrier(
+        (back, grad_q, grad_k, grad_v, spread)
+    )
+    dense_sinks = jnp.sum(sink_probs * spread, axis=2).reshape(QUERY_HEADS) * token_scale
     summed = jnp.sum(back.reshape(EW, chips // EW, CAP, PADDED).astype(F32), axis=1)
     summed = summed.reshape(SLOTS, PADDED)
     share_slots = jnp.sum(summed[:, D : D + 3], axis=1)
@@ -318,19 +361,19 @@
     grad_slots = jnp.where(primary[:, None], grad_slots, 0.0).astype(BF16)
 
     attended_grad_slots = dot_last(grad_slots, out_full).astype(BF16)
-    slot_q, slot_k, slot_v, slot_sinks = head_grads(
-        probs_slots,
-        probs_slots_low,
-        sink_slots,
-        query_slots,
-        keys_here,
-        values_here,
-        attended_grad_slots,
-        1.0,
-    )
-    sinks = jnp.pad(grad_sinks + slot_sinks, (0, 128 - QUERY_HEADS))[None]
-    sinks = jnp.sum(to_all(sinks, ("core", "dp")), axis=0)
-    sinks = jnp.sum(to_all(sinks, "z"), axis=0)
+    slot_prob, slot_spread = head_spread(probs_slots, values_here, attended_grad_slots)
+    slot_sinks = jnp.sum(sink_slots * slot_spread, axis=2).reshape(QUERY_HEADS)
+    sinks = jnp.pad(-(dense_sinks + slot_sinks), (0, 128 - QUERY_HEADS))[None]
+    sinks = to_all(sinks, ("core", "dp"))
+    sinks, slot_prob, upstream_rows = lax.optimization_barrier(
+        (jnp.sum(sinks, axis=0), slot_prob, upstream_rows)
+    )
+    sinks = to_all(sinks, "z")
+    sinks = jnp.sum(sinks, axis=0)
+
+    slot_q, slot_k, slot_v = head_grads(
+        probs_slots, slot_prob, slot_spread, query_slots, keys_here, attended_grad_slots, 1.0
+    )
     grad_k = grad_k + slot_k
     grad_v = grad_v + slot_v
     onward = jnp.concatenate([grad_k[:WINDOW], grad_v[:WINDOW]], axis=1).astype(BF16)
@@ -363,6 +406,7 @@
     seq, dp = mesh.shape["seq"], mesh.shape["dp"]
     split = Mesh(mesh.devices.reshape(seq // 2, 2, dp), ("z", "core", "dp"))
     whole = ("z", "core")
+
     return jax.shard_map(
         shards,
         mesh=split,

time: 268 us -> 253 us (0.944)
  local copies, waits for them, and re-layouts: 36.6 us -> 28.7 us
  waiting for transfers between devices: 55.1 us -> 48.1 us
  matrix products: 43.5 us -> 37.6 us
  starting transfers between devices: 78.2 us -> 82.9 us
  Pallas kernels: 0 us -> 3.95 us
    all_to_all x7, waiting for transfers between devices: 55.1 us -> 46.6 us  [exchange(): return lax.all_to_all(value, axis, split_axis=0, concat_axis=0, tiled=True)]
    another operation x3 -> x0, local copies, waits for them, and re-layouts: 5.1 us -> none  [shards(): gathered[:, i].reshape(D, -1)]
    pallas_call x0 -> x1, Pallas kernels: none -> 3.95 us  [experts_step(): pl.pallas_call(experts_kernel, out_shape=jax.ShapeDtypeStruct((count // 2...]
    dot_general x6 -> x4, matrix products: 16.7 us -> 13 us  [dot_last(): return lax.dot_general(a, b, CONTRACT_LAST, preferred_element_type=F32)]
    reshape x1 -> x3, local copies, waits for them, and re-layouts: 0.13 us -> 3.54 us  [the longest x1 2.54 us: shards(): own_block = gathered.reshape(D, shard.shape[1])]
    all_to_all x7, starting transfers between devices: 63.5 us -> 66.6 us  [exchange(): return lax.all_to_all(value, axis, split_axis=0, concat_axis=0, tiled=True)]
    dot_general x11 -> x9, matrix products: 11.4 us -> 8.64 us  [dot32(): return jnp.dot(a, b, preferred_element_type=F32, **kw)]
    unnamed x186 -> x159, local copies, waits for them, and re-layouts: 8.33 us -> 6.76 us
  transfers between devices with their start and end apart: 12 -> 12, of which waited for: 5 -> 6; matrix products, arithmetic and copies ran while one was open for 35% -> 29% of each run, Pallas kernels for 0% -> 2%
where the time goes in v4:
time: 253 us; the launch traced here: 251 us
  starting transfers between devices  82.9 us (33%)
  waiting for transfers between devices  48.1 us (19%)
  matrix products  37.6 us (15%)
  local copies, waits for them, and re-layouts  28.7 us (11%)
  other arithmetic  28.6 us (11%)
  between operations  21.4 us (8%)
  Pallas kernels  3.95 us (2%)
    all_to_all x7, starting transfers between devices, exchange(): return lax.all_to_all(value, axis, split_axis=0, concat_axis=0, tiled=True)  66.6 us
    all_to_all x7, waiting for transfers between devices, exchange(): return lax.all_to_all(value, axis, split_axis=0, concat_axis=0, tiled=True)  46.6 us
    dot_general x4, matrix products, dot_last(): return lax.dot_general(a, b, CONTRACT_LAST, preferred_element_type=F32)  13 us
    ppermute x2, starting transfers between devices, swap_cores(): return lax.ppermute(value, 'core', [(0, 1), (1, 0)])  8.87 us
    dot_general x9, matrix products, dot32(): return jnp.dot(a, b, preferred_element_type=F32, **kw)  8.64 us
    ppermute x2, starting transfers between devices, along_seq(): lax.ppermute(value, ('z', 'core'), [(i, i + steps) for i in range(first,...  7.42 us
    unnamed x159, local copies, waits for them, and re-layouts  6.76 us
  transfers between devices with their start and end apart: 12, of which 6 were waited for; matrix products, arithmetic and copies ran while one was open for 29% of the time, Pallas kernels for 2%

profile of v4, /device:TPU:1, one launch (start us, length us, event | category | flops | bytes accessed | tf_op | source)
XLA Modules:
  0.0 251.2 jit_solution(3815712199219711699)
XLA Ops:
  9.8 7.6 %all-to-all-start = ((bf16[16,180,384]{2,1,0:T(8,128)(2,1)}), bf16[16,180,384]{2,1,0:T(8,128)(2,1)S(1)}, u32[]{:S(2)}, u32[]{:S(2)}) async-start(bf16[16,180,384]{2,1,0:T(8,128)(2,1)} %broadcast_in_dim.278), calls=%async_computation | async-start | bytes 4521984 | tf_op jit(solution)/shard_map/all_to_all | solution.py:36
  18.9 4.4 %collective-permute-start = (bf16[128,512]{1,0:T(8,128)(2,1)}, bf16[128,512]{1,0:T(8,128)(2,1)}, u32[]{:S(2)}, u32[]{:S(2)}) collective-permute-start(bf16[128,512]{1,0:T(8,128)(2,1)} %pad_maximum_fusion.1), channel_id=1, source_target_pairs={{0,16},{16,32},{32,48},{48,64},{64,80},{80,96},{96,112},{112,128},... | collective-permute-start | bytes 393224 | tf_op jit(solution)/shard_map/ppermute | solution.py:52
  37.5 6.8 %all-to-all-done = bf16[16,180,384]{2,1,0:T(8,128)(2,1)S(1)} async-done(((bf16[16,180,384]{2,1,0:T(8,128)(2,1)}), bf16[16,180,384]{2,1,0:T(8,128)(2,1)S(1)}, u32[]{:S(2)}, u32[]{:S(2)}) %all-to-all-start) | async-done | bytes 2211872 | tf_op jit(solution)/shard_map/all_to_all | solution.py:36
  49.7 7.0 %all-to-all-start.1 = ((bf16[16,16,128]{2,1,0:T(8,128)(2,1)}), bf16[16,16,128]{2,1,0:T(8,128)(2,1)}, u32[]{:S(2)}, u32[]{:S(2)}) async-start(bf16[16,16,128]{2,1,0:T(8,128)(2,1)} %copy.191), calls=%async_computation.1 | async-start | bytes 131072 | tf_op jit(solution)/shard_map/all_to_all | solution.py:36
  57.2 2.5 %reshape.492.own_ref = bf16[2880,384]{1,0:T(8,128)(2,1)S(1)} reshape(bf16[16,180,384]{2,1,0:T(8,128)(2,1)} %copy-done.5) | data formatting | bytes 4423680 | tf_op jit(solution)/shard_map/reshape | solution.py:250
  59.7 4.7 %collective-permute-start.1 = (bf16[2880,384]{1,0:T(8,128)(2,1)S(1)}, bf16[2880,384]{1,0:T(8,128)(2,1)}, u32[]{:S(2)}, u32[]{:S(2)}) collective-permute-start(bf16[2880,384]{1,0:T(8,128)(2,1)S(1)} %reshape.492.own_ref), channel_id=1, source_target_pairs={{0,16},{16,0},{1,17},{17,1},{2,18},{18,2},{3,19},{19,3},{4,20},{20... | collective-permute-start | bytes 6635528 | tf_op jit(solution)/shard_map/ppermute | solution.py:45
  65.4 2.3 convolution_convert_fusion.1
  67.7 2.4 copy.192
  70.1 6.9 %all-to-all-start.2 = ((bf16[16,8,2880]{2,1,0:T(8,128)(2,1)}), bf16[16,8,2880]{2,1,0:T(8,128)(2,1)}, u32[]{:S(2)}, u32[]{:S(2)}) async-start(bf16[16,8,2880]{2,1,0:T(8,128)(2,1)} %bitcast.193), calls=%async_computation.2 | async-start | bytes 1507328 | tf_op jit(solution)/shard_map/all_to_all | solution.py:36
  81.3 2.1 convolution_convert_fusion.3
  83.3 11.0 %all-to-all-done.2 = bf16[16,8,2880]{2,1,0:T(8,128)(2,1)} async-done(((bf16[16,8,2880]{2,1,0:T(8,128)(2,1)}), bf16[16,8,2880]{2,1,0:T(8,128)(2,1)}, u32[]{:S(2)}, u32[]{:S(2)}) %all-to-all-start.2) | async-done | bytes 737312 | tf_op jit(solution)/shard_map/all_to_all | solution.py:36
  98.8 15.5 %all-to-all-start.3 = ((bf16[16,8,2944]{2,1,0:T(8,128)(2,1)}), bf16[16,8,2944]{2,1,0:T(8,128)(2,1)}, u32[]{:S(2)}, u32[]{:S(2)}) async-start(bf16[16,8,2944]{2,1,0:T(8,128)(2,1)} %bitcast.194), calls=%async_computation.3 | async-start | bytes 1507328 | tf_op jit(solution)/shard_map/all_to_all | solution.py:36
  125.4 21.9 %all-to-all-done.3 = bf16[16,8,2944]{2,1,0:T(8,128)(2,1)} async-done(((bf16[16,8,2944]{2,1,0:T(8,128)(2,1)}), bf16[16,8,2944]{2,1,0:T(8,128)(2,1)}, u32[]{:S(2)}, u32[]{:S(2)}) %all-to-all-start.3) | async-done | bytes 753696 | tf_op jit(solution)/shard_map/all_to_all | solution.py:36
  147.4 3.9 %shard_map.191 = bf16[64,2944]{1,0:T(8,128)(2,1)S(1)} custom-call(bf16[128,2944]{1,0:T(8,128)(2,1)} %bitcast.36.rows_ref, bf16[2880,384]{1,0:T(8,128)(2,1)S(1)} %reshape.492.own_ref, bf16[2880,384]{1,0:T(8,128)(2,1)} %collective-permute-done.1.other_ref), custom_call_target="tpu_custom_call" | custom-call | flops 471859200 | bytes 5931008 | tf_op jit(solution)/shard_map/pallas_call | solution.py:145
  152.2 12.4 %all-to-all-start.4 = ((bf16[16,4,2944]{2,1,0:T(4,128)(2,1)}), bf16[16,4,2944]{2,1,0:T(4,128)(2,1)}, u32[]{:S(2)}, u32[]{:S(2)}) async-start(bf16[16,4,2944]{2,1,0:T(4,128)(2,1)} %reshape.493), calls=%async_computation.4 | async-start | bytes 753664 | tf_op jit(solution)/shard_map/all_to_all | solution.py:36
  166.1 6.5 %fusion.11 = bf16[128,2048]{1,0:T(8,128)(2,1)S(1)} fusion(bf16[2048,2880]{0,1:T(8,128)(2,1)} %all-gather.2.cloned.1.call-done, bf16[128,2880]{0,1:T(8,128)(2,1)} %bitcast.189, pred[128]{0:T(512)(128)(4,1)S(1)} %broadcast_compare_fusion.1, pred[128]{0:T(512)(128)(4,1)S(1)} %copy-done.63), kind=kOutput, calls=%fused_computation.22 | convolution fusion | flops 1510842368 | bytes 13058304 | tf_op jit(solution)/shard_map/dot_general | solution.py:32
  175.7 4.1 %collective-permute-start.2 = (f32[8,128]{1,0:T(8,128)S(1)}, f32[8,128]{1,0:T(8,128)S(1)}, u32[]{:S(2)}, u32[]{:S(2)}) collective-permute-start(f32[8,128]{1,0:T(8,128)S(1)} %broadcast_in_dim.299), channel_id=1, source_target_pairs={{0,16},{16,0},{1,17},{17,1},{2,18},{18,2},{3,19},{19,3},{4,20},{20... | collective-permute-start | bytes 12296 | tf_op jit(solution)/shard_map/ppermute | solution.py:45
  179.8 3.8 %fusion = (f32[4,8,128]{2,1,0:T(8,128)S(1)}, f32[4,256,128,8]{2,1,3,0:T(8,128)S(1)}) fusion(f32[4,8,128]{2,1,0:T(8,128)S(1)} %fusion.65, f32[4,8,128]{2,1,0:T(8,128)S(1)} %broadcast_maximum_fusion, f32[4,256,128,8]{2,1,3,0:T(8,128)} %copy-done.1, pred[128,256]{0,1:T(8,128)(4,1)S(1)} %and_and_fusion, bf16[256,4,64,1]{0,2,3,1:T(8,128)(2,1)S(1)} %bitcast.206, ...), kind=kOutput, calls=%fused_computation.2 | convolution fusion | flops 141553664 | bytes 9125888 | tf_op jit(solution)/shard_map/baqj,eaj->aqbe/dot_general | solution.py:81
  195.7 6.1 %convolution_convert_fusion.6 = bf16[8,2048]{1,0:T(8,128)(2,1)S(1)} fusion(bf16[8,2880]{1,0:T(8,128)(2,1)S(1)} %fusion.51, bf16[2048,2880]{0,1:T(8,128)(2,1)} %all-gather.2.cloned.1.call-done), kind=kOutput, calls=%fused_computation.27 | convolution fusion | flops 94388224 | bytes 11875328 | tf_op jit(solution)/shard_map/dot_general | solution.py:32
  203.6 5.2 %all-to-all-start.5 = ((f32[32,1,128]{2,1,0:T(1,128)}), f32[32,1,128]{2,1,0:T(1,128)}, u32[]{:S(2)}, u32[]{:S(2)}) async-start(f32[32,1,128]{2,1,0:T(1,128)} %broadcast_in_dim.311), calls=%async_computation.5 | async-start | bytes 32768 | tf_op jit(solution)/shard_map/all_to_all | solution.py:36
  212.0 3.6 %all-to-all-done.5 = f32[32,1,128]{2,1,0:T(1,128)} async-done(((f32[32,1,128]{2,1,0:T(1,128)}), f32[32,1,128]{2,1,0:T(1,128)}, u32[]{:S(2)}, u32[]{:S(2)}) %all-to-all-start.5) | async-done | bytes 16416 | tf_op jit(solution)/shard_map/all_to_all | solution.py:36
  219.8 12.0 %all-to-all-start.6 = ((f32[16,1,128]{2,1,0:T(1,128)}), f32[16,1,128]{2,1,0:T(1,128)S(1)}, u32[]{:S(2)}, u32[]{:S(2)}) async-start(f32[16,1,128]{2,1,0:T(1,128)} %broadcast_in_dim.318), calls=%async_computation.6 | async-start | bytes 16384 | tf_op jit(solution)/shard_map/all_to_all | solution.py:36
  232.9 3.0 %collective-permute-start.3 = (bf16[128,512]{1,0:T(8,128)(2,1)S(1)}, bf16[128,512]{1,0:T(8,128)(2,1)S(1)}, u32[]{:S(2)}, u32[]{:S(2)}) collective-permute-start(bf16[128,512]{1,0:T(8,128)(2,1)S(1)} %pad_maximum_fusion.4), channel_id=1, source_target_pairs={{16,0},{32,16},{48,32},{64,48},{80,64},{96,80},{112,96},{128,112},... | collective-permute-start | bytes 393224 | tf_op jit(solution)/shard_map/ppermute | solution.py:52
  239.8 3.2 %all-to-all-done.6 = f32[16,1,128]{2,1,0:T(1,128)S(1)} async-done(((f32[16,1,128]{2,1,0:T(1,128)}), f32[16,1,128]{2,1,0:T(1,128)S(1)}, u32[]{:S(2)}, u32[]{:S(2)}) %all-to-all-start.6) | async-done | bytes 8224 | tf_op jit(solution)/shard_map/all_to_all | solution.py:36
  (299 shorter events, 70.7 us)
Async XLA Ops:
  7.2 63.0 %copy-start = (bf16[1,128,2880]{1,2,0:T(8,128)(2,1)S(1)}, bf16[1,128,2880]{1,2,0:T(8,128)(2,1)}, u32[]{:S(2)}) copy-start(bf16[1,128,2880]{1,2,0:T(8,128)(2,1)} %param.20) | copy-start | bytes 2211844
  9.8 34.5 %all-to-all-start = ((bf16[16,180,384]{2,1,0:T(8,128)(2,1)}), bf16[16,180,384]{2,1,0:T(8,128)(2,1)S(1)}, u32[]{:S(2)}, u32[]{:S(2)}) async-start(bf16[16,180,384]{2,1,0:T(8,128)(2,1)} %broadcast_in_dim.278), calls=%async_computation | async-start | bytes 4521984 | tf_op jit(solution)/shard_map/all_to_all | solution.py:36
  17.3 148.7 %all-gather.2.cloned.1.call-start = ((), (), s32[]{:S(2)}) async-start(), calls=%async_computation.7 | async-start | bytes 12533760 | tf_op jit(solution)/shard_map/all_gather | solution.py:240
  18.9 13.3 %collective-permute-start = (bf16[128,512]{1,0:T(8,128)(2,1)}, bf16[128,512]{1,0:T(8,128)(2,1)}, u32[]{:S(2)}, u32[]{:S(2)}) collective-permute-start(bf16[128,512]{1,0:T(8,128)(2,1)} %pad_maximum_fusion.1), channel_id=1, source_target_pairs={{0,16},{16,32},{32,48},{48,64},{64,80},{80,96},{96,112},{112,128},... | collective-permute-start | bytes 393224 | tf_op jit(solution)/shard_map/ppermute | solution.py:52
  46.0 74.5 %copy-start.6 = (bf16[1,128,2048]{1,2,0:T(8,128)(2,1)}, bf16[1,128,2048]{1,2,0:T(8,128)(2,1)S(1)}, u32[]{:S(2)}) copy-start(bf16[1,128,2048]{1,2,0:T(8,128)(2,1)S(1)} %copy.185) | copy-start | bytes 1572868
  49.7 14.8 %all-to-all-start.1 = ((bf16[16,16,128]{2,1,0:T(8,128)(2,1)}), bf16[16,16,128]{2,1,0:T(8,128)(2,1)}, u32[]{:S(2)}, u32[]{:S(2)}) async-start(bf16[16,16,128]{2,1,0:T(8,128)(2,1)} %copy.191), calls=%async_computation.1 | async-start | bytes 131072 | tf_op jit(solution)/shard_map/all_to_all | solution.py:36
  59.7 36.3 %copy-start.53 = (f32[2880]{0:T(1024)S(1)}, f32[2880]{0:T(1024)}, u32[]{:S(2)}) copy-start(f32[2880]{0:T(1024)} %param.22) | copy-start | bytes 34564
  59.7 65.7 %collective-permute-start.1 = (bf16[2880,384]{1,0:T(8,128)(2,1)S(1)}, bf16[2880,384]{1,0:T(8,128)(2,1)}, u32[]{:S(2)}, u32[]{:S(2)}) collective-permute-start(bf16[2880,384]{1,0:T(8,128)(2,1)S(1)} %reshape.492.own_ref), channel_id=1, source_target_pairs={{0,16},{16,0},{1,17},{17,1},{2,18},{18,2},{3,19},{19,3},{4,20},{20... | collective-permute-start | bytes 6635528 | tf_op jit(solution)/shard_map/ppermute | solution.py:45
  67.7 47.9 %copy-start.65 = (s32[1,128,4]{1,2,0:T(4,128)S(1)}, s32[1,128,4]{1,2,0:T(4,128)}, u32[]{:S(2)}) copy-start(s32[1,128,4]{1,2,0:T(4,128)} %param.27) | copy-start | bytes 6148
  70.1 24.2 %all-to-all-start.2 = ((bf16[16,8,2880]{2,1,0:T(8,128)(2,1)}), bf16[16,8,2880]{2,1,0:T(8,128)(2,1)}, u32[]{:S(2)}, u32[]{:S(2)}) async-start(bf16[16,8,2880]{2,1,0:T(8,128)(2,1)} %bitcast.193), calls=%async_computation.2 | async-start | bytes 1507328 | tf_op jit(solution)/shard_map/all_to_all | solution.py:36
  95.9 26.3 %copy-start.17 = (bf16[8,2880]{1,0:T(8,128)(2,1)}, bf16[8,2880]{1,0:T(8,128)(2,1)S(1)}, u32[]{:S(2)}) copy-start(bf16[8,2880]{1,0:T(8,128)(2,1)S(1)} %fusion.8) | copy-start | bytes 138244
  97.8 21.9 %copy-start.72 = (s32[1,256]{1,0:T(1,128)}, s32[1,256]{1,0:T(1,128)S(1)}, u32[]{:S(2)}) copy-start(s32[1,256]{1,0:T(1,128)S(1)} %iota.98) | copy-start | bytes 3076
  98.8 48.6 %all-to-all-start.3 = ((bf16[16,8,2944]{2,1,0:T(8,128)(2,1)}), bf16[16,8,2944]{2,1,0:T(8,128)(2,1)}, u32[]{:S(2)}, u32[]{:S(2)}) async-start(bf16[16,8,2944]{2,1,0:T(8,128)(2,1)} %bitcast.194), calls=%async_computation.3 | async-start | bytes 1507328 | tf_op jit(solution)/shard_map/all_to_all | solution.py:36
  125.3 22.1 %copy-start.35 = (f32[4,8,128]{2,1,0:T(8,128)}, f32[4,8,128]{2,1,0:T(8,128)S(1)}, u32[]{:S(2)}) copy-start(f32[4,8,128]{2,1,0:T(8,128)S(1)} %fusion.10) | copy-start | bytes 49156
  125.3 39.3 %copy-start.77 = (f32[128]{0:T(128)S(1)}, f32[128]{0:T(128)}, u32[]{:S(2)}) copy-start(f32[128]{0:T(128)} %convert_bitcast_fusion) | copy-start | bytes 1540
  125.3 40.8 %copy-start.63 = (pred[128]{0:T(512)(128)(4,1)S(1)}, pred[128]{0:T(512)(128)(4,1)}, u32[]{:S(2)}) copy-start(pred[128]{0:T(512)(128)(4,1)} %get-tuple-element.72) | copy-start | bytes 388
  125.4 58.2 %copy-start.46 = (f32[4,8,128]{2,1,0:T(8,128)}, f32[4,8,128]{2,1,0:T(8,128)S(1)}, u32[]{:S(2)}) copy-start(f32[4,8,128]{2,1,0:T(8,128)S(1)} %fusion.65) | copy-start | bytes 49156
  152.2 40.4 %all-to-all-start.4 = ((bf16[16,4,2944]{2,1,0:T(4,128)(2,1)}), bf16[16,4,2944]{2,1,0:T(4,128)(2,1)}, u32[]{:S(2)}, u32[]{:S(2)}) async-start(bf16[16,4,2944]{2,1,0:T(4,128)(2,1)} %reshape.493), calls=%async_computation.4 | async-start | bytes 753664 | tf_op jit(solution)/shard_map/all_to_all | solution.py:36
  175.7 9.7 %collective-permute-start.2 = (f32[8,128]{1,0:T(8,128)S(1)}, f32[8,128]{1,0:T(8,128)S(1)}, u32[]{:S(2)}, u32[]{:S(2)}) collective-permute-start(f32[8,128]{1,0:T(8,128)S(1)} %broadcast_in_dim.299), channel_id=1, source_target_pairs={{0,16},{16,0},{1,17},{17,1},{2,18},{18,2},{3,19},{19,3},{4,20},{20... | collective-permute-start | bytes 12296 | tf_op jit(solution)/shard_map/ppermute | solution.py:45
  201.9 34.0 %copy-start.4 = (bf16[1,128,2880]{1,2,0:T(8,128)(2,1)S(1)}, bf16[1,128,2880]{1,2,0:T(8,128)(2,1)}, u32[]{:S(2)}) copy-start(bf16[1,128,2880]{1,2,0:T(8,128)(2,1)} %param.31) | copy-start | bytes 2211844
  203.6 12.0 %all-to-all-start.5 = ((f32[32,1,128]{2,1,0:T(1,128)}), f32[32,1,128]{2,1,0:T(1,128)}, u32[]{:S(2)}, u32[]{:S(2)}) async-start(f32[32,1,128]{2,1,0:T(1,128)} %broadcast_in_dim.311), calls=%async_computation.5 | async-start | bytes 32768 | tf_op jit(solution)/shard_map/all_to_all | solution.py:36
  211.8 31.9 %copy-start.21 = (f32[256,256]{1,0:T(8,128)S(1)}, f32[256,256]{1,0:T(8,128)}, u32[]{:S(2)}) copy-start(f32[256,256]{1,0:T(8,128)} %copy-done.20) | copy-start | bytes 786436
  219.8 23.3 %all-to-all-start.6 = ((f32[16,1,128]{2,1,0:T(1,128)}), f32[16,1,128]{2,1,0:T(1,128)S(1)}, u32[]{:S(2)}, u32[]{:S(2)}) async-start(f32[16,1,128]{2,1,0:T(1,128)} %broadcast_in_dim.318), calls=%async_computation.6 | async-start | bytes 16384 | tf_op jit(solution)/shard_map/all_to_all | solution.py:36
  232.9 10.7 %collective-permute-start.3 = (bf16[128,512]{1,0:T(8,128)(2,1)S(1)}, bf16[128,512]{1,0:T(8,128)(2,1)S(1)}, u32[]{:S(2)}, u32[]{:S(2)}) collective-permute-start(bf16[128,512]{1,0:T(8,128)(2,1)S(1)} %pad_maximum_fusion.4), channel_id=1, source_target_pairs={{16,0},{32,16},{48,32},{64,48},{80,64},{96,80},{112,96},{128,112},... | collective-permute-start | bytes 393224 | tf_op jit(solution)/shard_map/ppermute | solution.py:52
  (66 other events, 396.7 us)
Sparse Core Ops, SparseCore 0:
  44.5 121.5 all-gather.1

commit v5 on v4

--- a/solution.py
+++ b/solution.py
@@ -19,6 +19,7 @@
 NORM_EPS = 1e-05
 GLU_SLOPE = 1.702
 HIGHEST = lax.Precision.HIGHEST
+SEQ = ("pair", "half", "core")
 CONTRACT_LAST = (((1,), (1,)), ((), ()))
 F32 = jnp.float32
 BF16 = jnp.bfloat16
@@ -41,15 +42,14 @@
     return exchange(jnp.broadcast_to(value[None], (count, *value.shape)), axis)
 
 
-def swap_cores(value):
-    return lax.ppermute(value, "core", [(0, 1), (1, 0)])
+def swap(value, axis):
+    return lax.ppermute(value, axis, [(0, 1), (1, 0)])
 
 
 def along_seq(value, steps):
-    chips, cores = lax.axis_size("z"), lax.axis_size("core")
-    count = chips * cores
+    count = lax.psum(1, SEQ)
     first, last = max(0, -steps), min(count, count - steps)
-    return lax.ppermute(value, ("z", "core"), [(i, i + steps) for i in range(first, last)])
+    return lax.ppermute(value, SEQ, [(i, i + steps) for i in range(first, last)])
 
 
 def head_scores(query_rows, key_rows, sinks, allowed):
@@ -101,10 +101,11 @@
     )
 
 
-def experts_kernel(rows_ref, own_ref, other_ref, out_ref):
+def experts_kernel(rows_ref, *refs):
+    blocks, out_ref = refs[:-1], refs[-1]
     count = rows_ref.shape[0]
     kept = count // 2
-    hid = own_ref.shape[1] // 3
+    hid = blocks[0].shape[1] // 3
     at = lax.broadcasted_iota(jnp.int32, (kept, count), 0)
     source = (at // CAP) * (2 * CAP) + at % CAP
     column = lax.broadcasted_iota(jnp.int32, (kept, count), 1)
@@ -113,7 +114,7 @@
     upstream = dot32((column == source + CAP).astype(BF16), rows).astype(BF16)
     piece = jnp.zeros((kept, D), F32)
     share = jnp.zeros((kept, 1), F32)
-    for block in (own_ref, other_ref):
+    for block in blocks:
         pair = block[:, : 2 * hid]
         pre = dot32(normed, pair)
         up_down = dot32(upstream, block[:, 2 * hid :])
@@ -140,20 +141,45 @@
     out_ref[:, even:] = jnp.concatenate([piece[:, even:], tail], axis=1).astype(BF16)
 
 
-def experts_step(rows, own_block, other_block):
-    count, hid = rows.shape[0], own_block.shape[1] // 3
+def experts_step(rows, *blocks):
+    count, hid = rows.shape[0], blocks[0].shape[1] // 3
     return pl.pallas_call(
         experts_kernel,
         out_shape=jax.ShapeDtypeStruct((count // 2, PADDED), BF16),
-        in_specs=[pl.BlockSpec(memory_space=pltpu.VMEM)] * 3,
+        in_specs=[pl.BlockSpec(memory_space=pltpu.VMEM)] * (1 + len(blocks)),
         out_specs=pl.BlockSpec(memory_space=pltpu.VMEM),
-        compiler_params=pltpu.CompilerParams(vmem_limit_bytes=24 << 20),
+        compiler_params=pltpu.CompilerParams(vmem_limit_bytes=32 << 20),
         cost_estimate=pl.CostEstimate(
-            flops=2 * 2 * count // 2 * D * hid * 5,
-            bytes_accessed=2 * (2 * D * 3 * hid + 2 * count * PADDED),
+            flops=len(blocks) * count * D * hid * 5,
+            bytes_accessed=2 * (len(blocks) * D * 3 * hid + 2 * count * PADDED),
             transcendentals=count * hid,
         ),
-    )(rows, own_block, other_block)
+    )(rows, *blocks)
+
+
+def project_kernel(columns_ref, weight_ref, out_ref):
+    count = columns_ref.shape[0]
+    at = lax.broadcasted_iota(jnp.int32, (count // 2, count), 0)
+    source = (at // SLOTS) * (2 * SLOTS) + at % SLOTS
+    kept = lax.broadcasted_iota(jnp.int32, (count // 2, count), 1) == source
+    rows = dot32(kept.astype(BF16), columns_ref[...]).astype(BF16)
+    out_ref[...] = dot_last(rows, weight_ref[...]).astype(BF16)
+
+
+def project_slots(columns, weight):
+    count, lanes = columns.shape
+    return pl.pallas_call(
+        project_kernel,
+        out_shape=jax.ShapeDtypeStruct((count // 2, D), BF16),
+        in_specs=[pl.BlockSpec(memory_space=pltpu.VMEM)] * 2,
+        out_specs=pl.BlockSpec(memory_space=pltpu.VMEM),
+        compiler_params=pltpu.CompilerParams(vmem_limit_bytes=16 << 20),
+        cost_estimate=pl.CostEstimate(
+            flops=count * D * lanes,
+            bytes_accessed=2 * (count * lanes + D * lanes + count * D // 2),
+            transcendentals=0,
+        ),
+    )(columns, weight)
 
 
 def shards(
@@ -174,12 +200,12 @@
     response_mask,
     upstream,
 ):
-    chips, cores, dp_count = lax.axis_size("z"), lax.axis_size("core"), lax.axis_size("dp")
-    seq_index = lax.axis_index("z") * cores + lax.axis_index("core")
+    pairs, dp_count = lax.axis_size("pair"), lax.axis_size("dp")
+    seq_index = lax.axis_index(SEQ)
     query_rows = queries[0]
     tokens = query_rows.shape[0]
     group_count = max(dp_count // 4, 1)
-    all_tokens = dp_count * chips * cores * tokens
+    all_tokens = dp_count * lax.psum(1, SEQ) * tokens
     lanes = out_weight.shape[0]
 
     route_rows = routes[0]
@@ -196,8 +222,8 @@
 
     shard = jnp.concatenate([expert_gate, expert_up, expert_down], axis=1)
     spread_shard = jnp.broadcast_to(shard[None], (dp_count, *shard.shape))
-    spread_shard, own_keys, own_values = lax.optimization_barrier(
-        (spread_shard, key_rows[0], value_matrix[0])
+    spread_shard, own_keys, own_values, mask_row = lax.optimization_barrier(
+        (spread_shard, key_rows[0], value_matrix[0], response_mask[0])
     )
     gathered = exchange(spread_shard, "dp")
 
@@ -222,15 +248,19 @@
     )
     attended_slots = head_mix(probs_slots.astype(BF16), values_here)
 
-    mask_wide = response_mask[0].astype(F32)
+    pair_count = jnp.full((8, 128), jnp.sum(mask_row.astype(F32)))
+    pair_count = pair_count + swap(pair_count, "core")
+    pair_count = pair_count[0, 0] + swap(pair_count, "half")[0, 0]
+    pair_high = jnp.floor(pair_count / 64.0)
     facts = jnp.stack(
         [
-            jnp.sum(mask_wide),
+            pair_high,
+            pair_count - 64.0 * pair_high,
             rewards[0].astype(F32),
             group_ids[0].astype(F32),
         ]
     )
-    facts_row = jnp.pad(facts, (0, lanes - 3))[None].astype(BF16)
+    facts_row = jnp.pad(facts, (0, lanes - 4))[None].astype(BF16)
     columns = attended_slots.reshape(SLOTS, dp_count, lanes).transpose(1, 0, 2)
     sent = jnp.concatenate(
         [columns, jnp.broadcast_to(facts_row[None], (dp_count, 1, lanes))], axis=1
@@ -239,16 +269,17 @@
     sent, gathered, late_weight = lax.optimization_barrier((sent, gathered, out_weight))
     out_full = lax.all_gather(late_weight, "dp", axis=0, tiled=True)
     arrived = exchange(sent, "dp")
-    facts_all = arrived[:, SLOTS, :3].astype(F32)
-    partial = dot32(arrived[:, :SLOTS].reshape(dp_count * SLOTS, lanes), out_weight)
+    facts_all = arrived[:, SLOTS, :4].astype(F32)
+    partial = project_slots(arrived.reshape(dp_count * 2 * SLOTS, lanes), out_weight.T)
     partial, residual_rows, upstream_rows, pick_low = lax.optimization_barrier(
-        (partial.astype(BF16).reshape(dp_count, SLOTS, D), residual[0], upstream[0], pick_low)
+        (partial.reshape(dp_count, SLOTS, D), residual[0], upstream[0], pick_low)
     )
     partial = exchange(partial, "dp")
     pick = pick_low > 0
     projected = jnp.sum(partial.astype(F32), axis=0)
     own_block = gathered.reshape(D, shard.shape[1])
-    other_block = swap_cores(own_block)
+    half_block = swap(own_block, "half")
+    blocks = (own_block, half_block, swap(own_block, "core"), swap(half_block, "core"))
 
     residual_slots = dot32(pick_low, residual_rows)
     upstream_slots = dot32(pick_low, upstream_rows).astype(BF16)
@@ -258,9 +289,9 @@
     unit_rows = mid_wide * inv_rms
     normed = (unit_rows * norm_gain[None, :]).astype(BF16)
 
-    counts_here = jnp.sum(facts_all[:, 0])
-    group_hot = (facts_all[:, 2][:, None] == jnp.arange(group_count, dtype=F32)).astype(F32)
-    reward_all = facts_all[:, 1]
+    counts_here = jnp.sum(64.0 * facts_all[:, 0] + facts_all[:, 1])
+    group_hot = (facts_all[:, 3][:, None] == jnp.arange(group_count, dtype=F32)).astype(F32)
+    reward_all = facts_all[:, 2]
     group_sizes = jnp.sum(group_hot, axis=0)
     group_sums = jnp.sum(group_hot * reward_all[:, None], axis=0)
     group_squares = jnp.sum(group_hot * (reward_all * reward_all)[:, None], axis=0)
@@ -299,19 +330,21 @@
     primary = jnp.sum(jnp.tril(same, -1), axis=1) == 0
     place = jnp.where(primary[:, None], pick, False)
     taken = jnp.any(pick, axis=0)
-    outgoing = jnp.broadcast_to(by_expert, (EW, chips // EW, 2 * CAP, PADDED))
-    came = exchange(outgoing.reshape(chips, 2 * CAP, PADDED), "z")
-
-    back = experts_step(came.reshape(chips * 2 * CAP, PADDED), own_block, other_block)
-    back, mask_late = lax.optimization_barrier((back.reshape(chips, CAP, PADDED), mask_wide))
-    back = exchange(back, "z")
+    outgoing = jnp.broadcast_to(by_expert, (EW, pairs // EW, 2 * CAP, PADDED))
+    came = exchange(outgoing.reshape(pairs, 2 * CAP, PADDED), "pair")
+
+    back = experts_step(came.reshape(pairs * 2 * CAP, PADDED), *blocks)
+    back, mask_late = lax.optimization_barrier(
+        (back.reshape(pairs, CAP, PADDED), mask_row)
+    )
+    mask_late = mask_late.astype(F32)
+    back = exchange(back, "pair")
 
     masked = jnp.where(mask_late[:, None] > 0.0, upstream_rows, jnp.zeros_like(upstream_rows))
     grad_attended = jnp.where(taken[:, None], 0.0, dot_last(masked, out_full)).astype(BF16)
     came, grad_attended = lax.optimization_barrier((came, grad_attended))
     count_parts = jnp.sum(came[:, 0, D : D + 2].astype(F32), axis=0)
-    core_count = count_parts[0] * 64.0 + count_parts[1]
-    token_total = core_count + swap_cores(jnp.full((8, 128), core_count))[0, 0]
+    token_total = count_parts[0] * 64.0 + count_parts[1]
     token_scale = -advantage * all_tokens / token_total
     loss_weight = token_scale * mask_late
     probs, sink_probs = head_scores(
@@ -325,7 +358,7 @@
         (back, grad_q, grad_k, grad_v, spread)
     )
     dense_sinks = jnp.sum(sink_probs * spread, axis=2).reshape(QUERY_HEADS) * token_scale
-    summed = jnp.sum(back.reshape(EW, chips // EW, CAP, PADDED).astype(F32), axis=1)
+    summed = jnp.sum(back.reshape(EW, pairs // EW, CAP, PADDED).astype(F32), axis=1)
     summed = summed.reshape(SLOTS, PADDED)
     share_slots = jnp.sum(summed[:, D : D + 3], axis=1)
 
@@ -368,7 +401,7 @@
     sinks, slot_prob, upstream_rows = lax.optimization_barrier(
         (jnp.sum(sinks, axis=0), slot_prob, upstream_rows)
     )
-    sinks = to_all(sinks, "z")
+    sinks = to_all(sinks, ("pair", "half"))
     sinks = jnp.sum(sinks, axis=0)
 
     slot_q, slot_k, slot_v = head_grads(
@@ -404,8 +437,8 @@
 
 def solution(mesh):
     seq, dp = mesh.shape["seq"], mesh.shape["dp"]
-    split = Mesh(mesh.devices.reshape(seq // 2, 2, dp), ("z", "core", "dp"))
-    whole = ("z", "core")
+    split = Mesh(mesh.devices.reshape(seq // 4, 2, 2, dp), (*SEQ, "dp"))
+    whole = SEQ
 
     return jax.shard_map(
         shards,

time: 253 us -> 249 us (0.984)
  matrix products: 37.6 us -> 32.9 us
  waiting for transfers between devices: 48.1 us -> 44 us
  Pallas kernels: 3.95 us -> 6.97 us
    all_to_all x7, waiting for transfers between devices: 46.6 us -> 23.7 us  [exchange(): return lax.all_to_all(value, axis, split_axis=0, concat_axis=0, tiled=True)]
    ppermute x4 -> x7, waiting for transfers between devices: 0.01 us -> 10.8 us  [the longest x5 10.8 us: swap(): return lax.ppermute(value, axis, [(0, 1), (1, 0)])]
    all_gather x1, waiting for transfers between devices: 1.44 us -> 9.52 us  [shards(): out_full = lax.all_gather(late_weight, 'dp', axis=0, tiled=True)]
    ppermute x4 -> x7, starting transfers between devices: 16.3 us -> 21.9 us  [the longest x5 16.9 us: swap(): return lax.ppermute(value, axis, [(0, 1), (1, 0)])]
    all_to_all x7, starting transfers between devices: 66.6 us -> 62 us  [exchange(): return lax.all_to_all(value, axis, split_axis=0, concat_axis=0, tiled=True)]
    dot_general x9 -> x8, matrix products: 8.64 us -> 4.82 us  [dot32(): return jnp.dot(a, b, preferred_element_type=F32, **kw)]
    pallas_call x1, Pallas kernels: 3.95 us -> 6.51 us  [experts_step(): pl.pallas_call(experts_kernel, out_shape=jax.ShapeDtypeStruct((count // 2...]
    unnamed x159 -> x136, local copies, waits for them, and re-layouts: 6.76 us -> 6.96 us
  transfers between devices with their start and end apart: 12 -> 15, of which waited for: 6 -> 6; matrix products, arithmetic and copies ran while one was open for 29% -> 28% of each run, Pallas kernels for 2% -> 3%
where the time goes in v5:
time: 249 us; the launch traced here: 247 us
  starting transfers between devices  83.9 us (34%)
  waiting for transfers between devices  44 us (18%)
  matrix products  32.9 us (13%)
  local copies, waits for them, and re-layouts  30 us (12%)
  other arithmetic  27.8 us (11%)
  between operations  21.7 us (9%)
  Pallas kernels  6.97 us (3%)
    all_to_all x7, starting transfers between devices, exchange(): return lax.all_to_all(value, axis, split_axis=0, concat_axis=0, tiled=True)  62 us
    all_to_all x7, waiting for transfers between devices, exchange(): return lax.all_to_all(value, axis, split_axis=0, concat_axis=0, tiled=True)  23.7 us
    ppermute x5, starting transfers between devices, swap(): return lax.ppermute(value, axis, [(0, 1), (1, 0)])  16.9 us
    dot_general x4, matrix products, dot_last(): return lax.dot_general(a, b, CONTRACT_LAST, preferred_element_type=F32)  12.8 us
    ppermute x5, waiting for transfers between devices, swap(): return lax.ppermute(value, axis, [(0, 1), (1, 0)])  10.8 us
    all_gather x1, waiting for transfers between devices, shards(): out_full = lax.all_gather(late_weight, 'dp', axis=0, tiled=True)  9.52 us
    unnamed x136, local copies, waits for them, and re-layouts  6.96 us
    pallas_call x1, Pallas kernels, experts_step(): pl.pallas_call(experts_kernel, out_shape=jax.ShapeDtypeStruct((count // 2...  6.51 us
  transfers between devices with their start and end apart: 15, of which 6 were waited for; matrix products, arithmetic and copies ran while one was open for 28% of the time, Pallas kernels for 3%

profile of v5, /device:TPU:1, one launch (start us, length us, event | category | flops | bytes accessed | tf_op | source)
XLA Modules:
  0.0 247.2 jit_solution(17287272998295176211)
XLA Ops:
  9.7 7.6 %all-to-all-start = ((bf16[16,180,384]{2,1,0:T(8,128)(2,1)}), bf16[16,180,384]{2,1,0:T(8,128)(2,1)S(1)}, u32[]{:S(2)}, u32[]{:S(2)}) async-start(bf16[16,180,384]{2,1,0:T(8,128)(2,1)} %broadcast_in_dim.278), calls=%async_computation | async-start | bytes 4521984 | tf_op jit(solution)/shard_map/all_to_all | solution.py:37
  19.2 4.9 %collective-permute-start.1 = (f32[8,128]{1,0:T(8,128)}, f32[8,128]{1,0:T(8,128)}, u32[]{:S(2)}, u32[]{:S(2)}) collective-permute-start(f32[8,128]{1,0:T(8,128)} %broadcast_in_dim.284), channel_id=1, source_target_pairs={{0,16},{16,0},{1,17},{17,1},{2,18},{18,2},{3,19},{19,3},{4,20},{20... | collective-permute-start | bytes 12296 | tf_op jit(solution)/shard_map/ppermute | solution.py:46
  33.2 3.0 %collective-permute-start.2 = (f32[8,128]{1,0:T(8,128)S(1)}, f32[8,128]{1,0:T(8,128)S(1)}, u32[]{:S(2)}, u32[]{:S(2)}) collective-permute-start(f32[8,128]{1,0:T(8,128)S(1)} %broadcast_add_fusion), channel_id=1, source_target_pairs={{0,32},{32,0},{1,33},{33,1},{2,34},{34,2},{3,35},{35,3},{4,36},{36... | collective-permute-start | bytes 12296 | tf_op jit(solution)/shard_map/ppermute | solution.py:46
  51.2 2.4 copy.181
  56.5 6.9 %all-to-all-start.1 = ((bf16[16,16,128]{2,1,0:T(8,128)(2,1)}), bf16[16,16,128]{2,1,0:T(8,128)(2,1)S(1)}, u32[]{:S(2)}, u32[]{:S(2)}) async-start(bf16[16,16,128]{2,1,0:T(8,128)(2,1)} %copy.187), calls=%async_computation.1 | async-start | bytes 131072 | tf_op jit(solution)/shard_map/all_to_all | solution.py:37
  63.4 2.5 %reshape.495.refs_0_ = bf16[2880,384]{1,0:T(8,128)(2,1)S(1)} reshape(bf16[16,180,384]{2,1,0:T(8,128)(2,1)} %copy-done.6) | data formatting | bytes 4423680 | tf_op jit(solution)/shard_map/reshape | solution.py:280
  68.2 3.6 %collective-permute-start.3 = (bf16[2880,384]{1,0:T(8,128)(2,1)S(1)}, bf16[2880,384]{1,0:T(8,128)(2,1)}, u32[]{:S(2)}, u32[]{:S(2)}) collective-permute-start(bf16[2880,384]{1,0:T(8,128)(2,1)S(1)} %reshape.495.refs_0_), channel_id=1, source_target_pairs={{0,32},{32,0},{1,33},{33,1},{2,34},{34,2},{3,35},{35,3},{4,36},{36... | collective-permute-start | bytes 6635528 | tf_op jit(solution)/shard_map/ppermute | solution.py:46
  74.5 7.0 %all-to-all-start.2 = ((bf16[16,8,2880]{2,1,0:T(8,128)(2,1)}), bf16[16,8,2880]{2,1,0:T(8,128)(2,1)}, u32[]{:S(2)}, u32[]{:S(2)}) async-start(bf16[16,8,2880]{2,1,0:T(8,128)(2,1)} %bitcast.184), calls=%async_computation.2 | async-start | bytes 1507328 | tf_op jit(solution)/shard_map/all_to_all | solution.py:37
  87.1 10.1 %all-to-all-done.2 = bf16[16,8,2880]{2,1,0:T(8,128)(2,1)} async-done(((bf16[16,8,2880]{2,1,0:T(8,128)(2,1)}), bf16[16,8,2880]{2,1,0:T(8,128)(2,1)}, u32[]{:S(2)}, u32[]{:S(2)}) %all-to-all-start.2) | async-done | bytes 737312 | tf_op jit(solution)/shard_map/all_to_all | solution.py:37
  100.8 12.4 %all-to-all-start.3 = ((bf16[8,8,2944]{2,1,0:T(8,128)(2,1)}), bf16[8,8,2944]{2,1,0:T(8,128)(2,1)S(1)}, u32[]{:S(2)}, u32[]{:S(2)}) async-start(bf16[8,8,2944]{2,1,0:T(8,128)(2,1)} %bitcast.198), calls=%async_computation.3 | async-start | bytes 753664 | tf_op jit(solution)/shard_map/all_to_all | solution.py:37
  114.8 10.8 %collective-permute-done.3.refs_1_ = bf16[2880,384]{1,0:T(8,128)(2,1)} collective-permute-done((bf16[2880,384]{1,0:T(8,128)(2,1)S(1)}, bf16[2880,384]{1,0:T(8,128)(2,1)}, u32[]{:S(2)}, u32[]{:S(2)}) %collective-permute-start.3) | collective-permute-done | bytes 2211872 | tf_op jit(solution)/shard_map/ppermute | solution.py:46
  125.6 3.2 %collective-permute-start.5 = (bf16[2880,384]{1,0:T(8,128)(2,1)}, bf16[2880,384]{1,0:T(8,128)(2,1)}, u32[]{:S(2)}, u32[]{:S(2)}) collective-permute-start(bf16[2880,384]{1,0:T(8,128)(2,1)} %collective-permute-done.3.refs_1_), channel_id=1, source_target_pairs={{0,16},{16,0},{1,17},{17,1},{2,18},{18,2},{3,19},{19,3},{4,20},{20... | collective-permute-start | bytes 6635528 | tf_op jit(solution)/shard_map/ppermute | solution.py:46
  136.4 6.7 %all-to-all-done.3 = bf16[8,8,2944]{2,1,0:T(8,128)(2,1)S(1)} async-done(((bf16[8,8,2944]{2,1,0:T(8,128)(2,1)}), bf16[8,8,2944]{2,1,0:T(8,128)(2,1)S(1)}, u32[]{:S(2)}, u32[]{:S(2)}) %all-to-all-start.3) | async-done | bytes 376864 | tf_op jit(solution)/shard_map/all_to_all | solution.py:37
  143.1 6.5 %shard_map.192 = bf16[32,2944]{1,0:T(8,128)(2,1)S(1)} custom-call(bf16[64,2944]{1,0:T(8,128)(2,1)S(1)} %bitcast.186, bf16[2880,384]{1,0:T(8,128)(2,1)S(1)} %reshape.495.refs_0_, bf16[2880,384]{1,0:T(8,128)(2,1)} %collective-permute-done.3.refs_1_, bf16[2880,384]{1,0:T(8,128)(2,1)} %collective-permute-done.4.refs_2_, ...), custom_call_target="tpu_custom_call" | custom-call | flops 471859200 | bytes 9601024 | tf_op jit(solution)/shard_map/pallas_call | solution.py:146
  150.4 9.1 %all-to-all-start.4 = ((bf16[8,4,2944]{2,1,0:T(4,128)(2,1)}), bf16[8,4,2944]{2,1,0:T(4,128)(2,1)S(1)}, u32[]{:S(2)}, u32[]{:S(2)}) async-start(bf16[8,4,2944]{2,1,0:T(4,128)(2,1)} %reshape.496), calls=%async_computation.4 | async-start | bytes 376832 | tf_op jit(solution)/shard_map/all_to_all | solution.py:37
  160.1 9.5 %all-gather.2.cloned.1.call-done = bf16[2048,2880]{0,1:T(8,128)(2,1)} async-done(((bf16[128,2880]{0,1:T(8,128)(2,1)}), bf16[2048,2880]{0,1:T(8,128)(2,1)}) %all-gather.2.cloned.1.call-update) | async-done | bytes 11796496 | tf_op jit(solution)/shard_map/all_gather | solution.py:270
  169.6 6.3 %fusion.11 = bf16[128,2048]{1,0:T(8,128)(2,1)S(1)} fusion(bf16[2048,2880]{0,1:T(8,128)(2,1)} %all-gather.2.cloned.1.call-done, bf16[128,2880]{0,1:T(8,128)(2,1)} %bitcast.189, pred[128]{0:T(512)(128)(4,1)S(1)} %convert_compare_fusion, pred[128]{0:T(512)(128)(4,1)} %get-tuple-element.74), kind=kOutput, calls=%fused_computation.21 | convolution fusion | flops 1510842368 | bytes 13058304 | tf_op jit(solution)/shard_map/dot_general | solution.py:33
  178.7 3.8 %fusion = (f32[4,8,128]{2,1,0:T(8,128)S(1)}, f32[4,256,128,8]{2,1,3,0:T(8,128)S(1)}) fusion(f32[4,8,128]{2,1,0:T(8,128)S(1)} %copy-done.43, f32[4,8,128]{2,1,0:T(8,128)S(1)} %copy-done.32, f32[4,256,128,8]{2,1,3,0:T(8,128)} %copy-done.3, pred[128,256]{0,1:T(8,128)(4,1)S(1)} %and_and_fusion, bf16[256,4,64,1]{0,2,3,1:T(8,128)(2,1)S(1)} %bitcast.205, ...), kind=kOutput, calls=%fused_computation.2 | convolution fusion | flops 141553664 | bytes 9125888 | tf_op jit(solution)/shard_map/baqj,eaj->aqbe/dot_general | solution.py:81
  191.0 6.1 %convolution_convert_fusion.5 = bf16[8,2048]{1,0:T(8,128)(2,1)S(1)} fusion(bf16[8,2880]{1,0:T(8,128)(2,1)S(1)} %fusion.54, bf16[2048,2880]{0,1:T(8,128)(2,1)} %all-gather.2.cloned.1.call-done), kind=kOutput, calls=%fused_computation.26 | convolution fusion | flops 94388224 | bytes 11875328 | tf_op jit(solution)/shard_map/dot_general | solution.py:33
  198.9 7.1 %all-to-all-start.5 = ((f32[32,1,128]{2,1,0:T(1,128)}), f32[32,1,128]{2,1,0:T(1,128)}, u32[]{:S(2)}, u32[]{:S(2)}) async-start(f32[32,1,128]{2,1,0:T(1,128)} %broadcast_in_dim.311), calls=%async_computation.5 | async-start | bytes 32768 | tf_op jit(solution)/shard_map/all_to_all | solution.py:37
  209.2 3.6 %all-to-all-done.5 = f32[32,1,128]{2,1,0:T(1,128)} async-done(((f32[32,1,128]{2,1,0:T(1,128)}), f32[32,1,128]{2,1,0:T(1,128)}, u32[]{:S(2)}, u32[]{:S(2)}) %all-to-all-start.5) | async-done | bytes 16416 | tf_op jit(solution)/shard_map/all_to_all | solution.py:37
  215.9 12.0 %all-to-all-start.6 = ((f32[16,1,128]{2,1,0:T(1,128)}), f32[16,1,128]{2,1,0:T(1,128)S(1)}, u32[]{:S(2)}, u32[]{:S(2)}) async-start(f32[16,1,128]{2,1,0:T(1,128)} %broadcast_in_dim.318), calls=%async_computation.6 | async-start | bytes 16384 | tf_op jit(solution)/shard_map/all_to_all | solution.py:37
  228.9 3.0 %collective-permute-start.6 = (bf16[128,512]{1,0:T(8,128)(2,1)S(1)}, bf16[128,512]{1,0:T(8,128)(2,1)S(1)}, u32[]{:S(2)}, u32[]{:S(2)}) collective-permute-start(bf16[128,512]{1,0:T(8,128)(2,1)S(1)} %pad_maximum_fusion.4), channel_id=1, source_target_pairs={{16,0},{32,16},{48,32},{64,48},{80,64},{96,80},{112,96},{128,112},... | collective-permute-start | bytes 393224 | tf_op jit(solution)/shard_map/ppermute | solution.py:52
  235.9 3.3 %all-to-all-done.6 = f32[16,1,128]{2,1,0:T(1,128)S(1)} async-done(((f32[16,1,128]{2,1,0:T(1,128)}), f32[16,1,128]{2,1,0:T(1,128)S(1)}, u32[]{:S(2)}, u32[]{:S(2)}) %all-to-all-start.6) | async-done | bytes 8224 | tf_op jit(solution)/shard_map/all_to_all | solution.py:37
  (283 shorter events, 74.0 us)
Async XLA Ops:
  7.2 67.3 %copy-start = (bf16[1,128,2880]{1,2,0:T(8,128)(2,1)S(1)}, bf16[1,128,2880]{1,2,0:T(8,128)(2,1)}, u32[]{:S(2)}) copy-start(bf16[1,128,2880]{1,2,0:T(8,128)(2,1)} %param.20) | copy-start | bytes 2211844
  9.7 41.4 %all-to-all-start = ((bf16[16,180,384]{2,1,0:T(8,128)(2,1)}), bf16[16,180,384]{2,1,0:T(8,128)(2,1)S(1)}, u32[]{:S(2)}, u32[]{:S(2)}) async-start(bf16[16,180,384]{2,1,0:T(8,128)(2,1)} %broadcast_in_dim.278), calls=%async_computation | async-start | bytes 4521984 | tf_op jit(solution)/shard_map/all_to_all | solution.py:37
  17.3 152.3 %all-gather.2.cloned.1.call-start = ((), (), s32[]{:S(2)}) async-start(), calls=%async_computation.7 | async-start | bytes 12533760 | tf_op jit(solution)/shard_map/all_gather | solution.py:270
  19.2 12.6 %collective-permute-start.1 = (f32[8,128]{1,0:T(8,128)}, f32[8,128]{1,0:T(8,128)}, u32[]{:S(2)}, u32[]{:S(2)}) collective-permute-start(f32[8,128]{1,0:T(8,128)} %broadcast_in_dim.284), channel_id=1, source_target_pairs={{0,16},{16,0},{1,17},{17,1},{2,18},{18,2},{3,19},{19,3},{4,20},{20... | collective-permute-start | bytes 12296 | tf_op jit(solution)/shard_map/ppermute | solution.py:46
  25.6 17.0 %collective-permute-start = (bf16[128,512]{1,0:T(8,128)(2,1)}, bf16[128,512]{1,0:T(8,128)(2,1)}, u32[]{:S(2)}, u32[]{:S(2)}) collective-permute-start(bf16[128,512]{1,0:T(8,128)(2,1)} %pad_maximum_fusion.1), channel_id=1, source_target_pairs={{0,16},{16,32},{32,48},{48,64},{64,80},{80,96},{96,112},{112,128},... | collective-permute-start | bytes 393224 | tf_op jit(solution)/shard_map/ppermute | solution.py:52
  33.2 7.0 %collective-permute-start.2 = (f32[8,128]{1,0:T(8,128)S(1)}, f32[8,128]{1,0:T(8,128)S(1)}, u32[]{:S(2)}, u32[]{:S(2)}) collective-permute-start(f32[8,128]{1,0:T(8,128)S(1)} %broadcast_add_fusion), channel_id=1, source_target_pairs={{0,32},{32,0},{1,33},{33,1},{2,34},{34,2},{3,35},{35,3},{4,36},{36... | collective-permute-start | bytes 12296 | tf_op jit(solution)/shard_map/ppermute | solution.py:46
  44.6 87.3 %copy-start.11 = (bf16[256,256]{0,1:T(8,128)(2,1)}, bf16[256,256]{0,1:T(8,128)(2,1)S(1)}, u32[]{:S(2)}) copy-start(bf16[256,256]{0,1:T(8,128)(2,1)S(1)} %copy.183) | copy-start | bytes 393220
  56.5 15.4 %all-to-all-start.1 = ((bf16[16,16,128]{2,1,0:T(8,128)(2,1)}), bf16[16,16,128]{2,1,0:T(8,128)(2,1)S(1)}, u32[]{:S(2)}, u32[]{:S(2)}) async-start(bf16[16,16,128]{2,1,0:T(8,128)(2,1)} %copy.187), calls=%async_computation.1 | async-start | bytes 131072 | tf_op jit(solution)/shard_map/all_to_all | solution.py:37
  63.4 35.5 %copy-start.45 = (f32[2880]{0:T(1024)S(1)}, f32[2880]{0:T(1024)}, u32[]{:S(2)}) copy-start(f32[2880]{0:T(1024)} %param.22) | copy-start | bytes 34564
  66.0 47.2 %copy-start.55 = (s32[1,128,4]{1,2,0:T(4,128)S(1)}, s32[1,128,4]{1,2,0:T(4,128)}, u32[]{:S(2)}) copy-start(s32[1,128,4]{1,2,0:T(4,128)} %param.27) | copy-start | bytes 6148
  66.0 77.0 %collective-permute-start.4 = (bf16[2880,384]{1,0:T(8,128)(2,1)S(1)}, bf16[2880,384]{1,0:T(8,128)(2,1)}, u32[]{:S(2)}, u32[]{:S(2)}) collective-permute-start(bf16[2880,384]{1,0:T(8,128)(2,1)S(1)} %reshape.495.refs_0_), channel_id=1, source_target_pairs={{0,16},{16,0},{1,17},{17,1},{2,18},{18,2},{3,19},{19,3},{4,20},{20... | collective-permute-start | bytes 6635528 | tf_op jit(solution)/shard_map/ppermute | solution.py:46
  68.2 57.5 %collective-permute-start.3 = (bf16[2880,384]{1,0:T(8,128)(2,1)S(1)}, bf16[2880,384]{1,0:T(8,128)(2,1)}, u32[]{:S(2)}, u32[]{:S(2)}) collective-permute-start(bf16[2880,384]{1,0:T(8,128)(2,1)S(1)} %reshape.495.refs_0_), channel_id=1, source_target_pairs={{0,32},{32,0},{1,33},{33,1},{2,34},{34,2},{3,35},{35,3},{4,36},{36... | collective-permute-start | bytes 6635528 | tf_op jit(solution)/shard_map/ppermute | solution.py:46
  74.5 22.7 %all-to-all-start.2 = ((bf16[16,8,2880]{2,1,0:T(8,128)(2,1)}), bf16[16,8,2880]{2,1,0:T(8,128)(2,1)}, u32[]{:S(2)}, u32[]{:S(2)}) async-start(bf16[16,8,2880]{2,1,0:T(8,128)(2,1)} %bitcast.184), calls=%async_computation.2 | async-start | bytes 1507328 | tf_op jit(solution)/shard_map/all_to_all | solution.py:37
  98.4 35.3 %copy-start.41 = (f32[4,8]{1,0:T(4,128)S(1)}, f32[4,8]{1,0:T(4,128)}, u32[]{:S(2)}) copy-start(f32[4,8]{1,0:T(4,128)} %max.33) | copy-start | bytes 388
  98.9 31.5 %copy-start.57 = (f32[8]{0:T(128)}, f32[8]{0:T(128)S(1)}, u32[]{:S(2)}) copy-start(f32[8]{0:T(128)S(1)} %add_rsqrt_fusion) | copy-start | bytes 100
  99.3 31.2 %copy-start.61 = (s32[1,256]{1,0:T(1,128)}, s32[1,256]{1,0:T(1,128)S(1)}, u32[]{:S(2)}) copy-start(s32[1,256]{1,0:T(1,128)S(1)} %iota.98) | copy-start | bytes 3076
  99.4 35.5 %copy-start.47 = (f32[8,8]{0,1:T(8,128)}, f32[8,8]{0,1:T(8,128)S(1)}, u32[]{:S(2)}) copy-start(f32[8,8]{0,1:T(8,128)S(1)} %get-tuple-element.101) | copy-start | bytes 772
  100.8 42.2 %all-to-all-start.3 = ((bf16[8,8,2944]{2,1,0:T(8,128)(2,1)}), bf16[8,8,2944]{2,1,0:T(8,128)(2,1)S(1)}, u32[]{:S(2)}, u32[]{:S(2)}) async-start(bf16[8,8,2944]{2,1,0:T(8,128)(2,1)} %bitcast.198), calls=%async_computation.3 | async-start | bytes 753664 | tf_op jit(solution)/shard_map/all_to_all | solution.py:37
  125.6 17.4 %collective-permute-start.5 = (bf16[2880,384]{1,0:T(8,128)(2,1)}, bf16[2880,384]{1,0:T(8,128)(2,1)}, u32[]{:S(2)}, u32[]{:S(2)}) collective-permute-start(bf16[2880,384]{1,0:T(8,128)(2,1)} %collective-permute-done.3.refs_1_), channel_id=1, source_target_pairs={{0,16},{16,0},{1,17},{17,1},{2,18},{18,2},{3,19},{19,3},{4,20},{20... | collective-permute-start | bytes 6635528 | tf_op jit(solution)/shard_map/ppermute | solution.py:46
  150.4 37.3 %all-to-all-start.4 = ((bf16[8,4,2944]{2,1,0:T(4,128)(2,1)}), bf16[8,4,2944]{2,1,0:T(4,128)(2,1)S(1)}, u32[]{:S(2)}, u32[]{:S(2)}) async-start(bf16[8,4,2944]{2,1,0:T(4,128)(2,1)} %reshape.496), calls=%async_computation.4 | async-start | bytes 376832 | tf_op jit(solution)/shard_map/all_to_all | solution.py:37
  197.3 34.7 %copy-start.5 = (bf16[1,128,2880]{1,2,0:T(8,128)(2,1)S(1)}, bf16[1,128,2880]{1,2,0:T(8,128)(2,1)}, u32[]{:S(2)}) copy-start(bf16[1,128,2880]{1,2,0:T(8,128)(2,1)} %param.31) | copy-start | bytes 2211844
  198.9 13.9 %all-to-all-start.5 = ((f32[32,1,128]{2,1,0:T(1,128)}), f32[32,1,128]{2,1,0:T(1,128)}, u32[]{:S(2)}, u32[]{:S(2)}) async-start(f32[32,1,128]{2,1,0:T(1,128)} %broadcast_in_dim.311), calls=%async_computation.5 | async-start | bytes 32768 | tf_op jit(solution)/shard_map/all_to_all | solution.py:37
  215.9 23.2 %all-to-all-start.6 = ((f32[16,1,128]{2,1,0:T(1,128)}), f32[16,1,128]{2,1,0:T(1,128)S(1)}, u32[]{:S(2)}, u32[]{:S(2)}) async-start(f32[16,1,128]{2,1,0:T(1,128)} %broadcast_in_dim.318), calls=%async_computation.6 | async-start | bytes 16384 | tf_op jit(solution)/shard_map/all_to_all | solution.py:37
  228.9 10.7 %collective-permute-start.6 = (bf16[128,512]{1,0:T(8,128)(2,1)S(1)}, bf16[128,512]{1,0:T(8,128)(2,1)S(1)}, u32[]{:S(2)}, u32[]{:S(2)}) collective-permute-start(bf16[128,512]{1,0:T(8,128)(2,1)S(1)} %pad_maximum_fusion.4), channel_id=1, source_target_pairs={{16,0},{32,16},{48,32},{64,48},{80,64},{96,80},{112,96},{128,112},... | collective-permute-start | bytes 393224 | tf_op jit(solution)/shard_map/ppermute | solution.py:52
  (58 other events, 406.6 us)
Sparse Core Ops, SparseCore 0:
  51.3 118.2 all-gather.1

commit v6 on v5

--- a/solution.py
+++ b/solution.py
@@ -222,8 +222,8 @@
 
     shard = jnp.concatenate([expert_gate, expert_up, expert_down], axis=1)
     spread_shard = jnp.broadcast_to(shard[None], (dp_count, *shard.shape))
-    spread_shard, own_keys, own_values, mask_row = lax.optimization_barrier(
-        (spread_shard, key_rows[0], value_matrix[0], response_mask[0])
+    spread_shard, own_keys, own_values, mask_row, query_rows = lax.optimization_barrier(
+        (spread_shard, key_rows[0], value_matrix[0], response_mask[0], query_rows)
     )
     gathered = exchange(spread_shard, "dp")
 
@@ -243,33 +243,29 @@
 
     slot_rows = jnp.sum(jnp.where(pick, row_index[:, 0][None, :], 0), axis=1, keepdims=True)
     query_slots = dot32(pick_low, query_rows).astype(BF16)
+    query_slots, late_weight = lax.optimization_barrier((query_slots, out_weight))
+    out_full = lax.all_gather(late_weight, "dp", axis=0, tiled=True)
     probs_slots, sink_slots = head_scores(
         query_slots, keys_here, head_sink_logits, visible(slot_rows, col_index)
     )
     attended_slots = head_mix(probs_slots.astype(BF16), values_here)
 
-    pair_count = jnp.full((8, 128), jnp.sum(mask_row.astype(F32)))
-    pair_count = pair_count + swap(pair_count, "core")
-    pair_count = pair_count[0, 0] + swap(pair_count, "half")[0, 0]
-    pair_high = jnp.floor(pair_count / 64.0)
     facts = jnp.stack(
         [
-            pair_high,
-            pair_count - 64.0 * pair_high,
+            jnp.sum(mask_row.astype(F32)),
             rewards[0].astype(F32),
             group_ids[0].astype(F32),
         ]
     )
-    facts_row = jnp.pad(facts, (0, lanes - 4))[None].astype(BF16)
+    facts_row = jnp.pad(facts, (0, lanes - 3))[None].astype(BF16)
     columns = attended_slots.reshape(SLOTS, dp_count, lanes).transpose(1, 0, 2)
     sent = jnp.concatenate(
         [columns, jnp.broadcast_to(facts_row[None], (dp_count, 1, lanes))], axis=1
     )
     sent = jnp.pad(sent, ((0, 0), (0, 2 * SLOTS - SLOTS - 1), (0, 0)))
-    sent, gathered, late_weight = lax.optimization_barrier((sent, gathered, out_weight))
-    out_full = lax.all_gather(late_weight, "dp", axis=0, tiled=True)
+    sent, gathered = lax.optimization_barrier((sent, gathered))
     arrived = exchange(sent, "dp")
-    facts_all = arrived[:, SLOTS, :4].astype(F32)
+    facts_all = arrived[:, SLOTS, :3].astype(F32)
     partial = project_slots(arrived.reshape(dp_count * 2 * SLOTS, lanes), out_weight.T)
     partial, residual_rows, upstream_rows, pick_low = lax.optimization_barrier(
         (partial.reshape(dp_count, SLOTS, D), residual[0], upstream[0], pick_low)
@@ -279,7 +275,8 @@
     projected = jnp.sum(partial.astype(F32), axis=0)
     own_block = gathered.reshape(D, shard.shape[1])
     half_block = swap(own_block, "half")
-    blocks = (own_block, half_block, swap(own_block, "core"), swap(half_block, "core"))
+    core_block = swap(own_block, "core")
+    blocks = (own_block, half_block, core_block, swap(half_block, "core"))
 
     residual_slots = dot32(pick_low, residual_rows)
     upstream_slots = dot32(pick_low, upstream_rows).astype(BF16)
@@ -289,9 +286,11 @@
     unit_rows = mid_wide * inv_rms
     normed = (unit_rows * norm_gain[None, :]).astype(BF16)
 
-    counts_here = jnp.sum(64.0 * facts_all[:, 0] + facts_all[:, 1])
-    group_hot = (facts_all[:, 3][:, None] == jnp.arange(group_count, dtype=F32)).astype(F32)
-    reward_all = facts_all[:, 2]
+    pair_count = jnp.full((8, 128), jnp.sum(facts_all[:, 0]))
+    pair_count = pair_count + swap(pair_count, "core")
+    counts_here = pair_count[0, 0] + swap(pair_count, "half")[0, 0]
+    group_hot = (facts_all[:, 2][:, None] == jnp.arange(group_count, dtype=F32)).astype(F32)
+    reward_all = facts_all[:, 1]
     group_sizes = jnp.sum(group_hot, axis=0)
     group_sums = jnp.sum(group_hot * reward_all[:, None], axis=0)
     group_squares = jnp.sum(group_hot * (reward_all * reward_all)[:, None], axis=0)
@@ -397,11 +396,11 @@
     slot_prob, slot_spread = head_spread(probs_slots, values_here, attended_grad_slots)
     slot_sinks = jnp.sum(sink_slots * slot_spread, axis=2).reshape(QUERY_HEADS)
     sinks = jnp.pad(-(dense_sinks + slot_sinks), (0, 128 - QUERY_HEADS))[None]
-    sinks = to_all(sinks, ("core", "dp"))
+    sinks = to_all(sinks, ("half", "core", "dp"))
     sinks, slot_prob, upstream_rows = lax.optimization_barrier(
         (jnp.sum(sinks, axis=0), slot_prob, upstream_rows)
     )
-    sinks = to_all(sinks, ("pair", "half"))
+    sinks = to_all(sinks, "pair")
     sinks = jnp.sum(sinks, axis=0)
 
     slot_q, slot_k, slot_v = head_grads(

time: 249 us -> 260 us (1.044)
  waiting for transfers between devices: 44 us -> 57.5 us
  starting transfers between devices: 83.9 us -> 93.2 us
  local copies, waits for them, and re-layouts: 30 us -> 24.6 us
  other arithmetic: 27.8 us -> 23.7 us
    ppermute x5, waiting for transfers between devices: 10.8 us -> 28.8 us  [swap(): return lax.ppermute(value, axis, [(0, 1), (1, 0)])]
    all_gather x1, waiting for transfers between devices: 9.52 us -> 0.01 us  [shards(): out_full = lax.all_gather(late_weight, 'dp', axis=0, tiled=True)]
    all_to_all x7, starting transfers between devices: 62 us -> 68.4 us  [exchange(): return lax.all_to_all(value, axis, split_axis=0, concat_axis=0, tiled=True)]
    all_to_all x7, waiting for transfers between devices: 23.7 us -> 28.6 us  [exchange(): return lax.all_to_all(value, axis, split_axis=0, concat_axis=0, tiled=True)]
    unnamed x136 -> x145, local copies, waits for them, and re-layouts: 6.96 us -> 6.9 us
  transfers between devices with their start and end apart: 15 -> 15, of which waited for: 6 -> 5; matrix products, arithmetic and copies ran while one was open for 28% -> 21% of each run, Pallas kernels for 3% -> 3%
where the time goes in v6:
time: 260 us; the launch traced here: 258 us
  starting transfers between devices  93.2 us (36%)
  waiting for transfers between devices  57.5 us (22%)
  matrix products  31.6 us (12%)
  local copies, waits for them, and re-layouts  24.6 us (9%)
  other arithmetic  23.7 us (9%)
  between operations  20.6 us (8%)
  Pallas kernels  6.97 us (3%)
    all_to_all x7, starting transfers between devices, exchange(): return lax.all_to_all(value, axis, split_axis=0, concat_axis=0, tiled=True)  68.4 us
    ppermute x5, waiting for transfers between devices, swap(): return lax.ppermute(value, axis, [(0, 1), (1, 0)])  28.8 us
    all_to_all x7, waiting for transfers between devices, exchange(): return lax.all_to_all(value, axis, split_axis=0, concat_axis=0, tiled=True)  28.6 us
    ppermute x5, starting transfers between devices, swap(): return lax.ppermute(value, axis, [(0, 1), (1, 0)])  17.4 us
    dot_general x4, matrix products, dot_last(): return lax.dot_general(a, b, CONTRACT_LAST, preferred_element_type=F32)  12.9 us
    ppermute x2, starting transfers between devices, along_seq(): lax.ppermute(value, SEQ, [(i, i + steps) for i in range(first, last)])  7.3 us
    unnamed x145, local copies, waits for them, and re-layouts  6.9 us
    pallas_call x1, Pallas kernels, experts_step(): pl.pallas_call(experts_kernel, out_shape=jax.ShapeDtypeStruct((count // 2...  6.51 us
  transfers between devices with their start and end apart: 15, of which 5 were waited for; matrix products, arithmetic and copies ran while one was open for 21% of the time, Pallas kernels for 3%

profile of v6, /device:TPU:1, one launch (start us, length us, event | category | flops | bytes accessed | tf_op | source)
XLA Modules:
  0.0 258.2 jit_solution(12041472369926120155)
XLA Ops:
  13.2 7.6 %all-to-all-start = ((bf16[16,180,384]{2,1,0:T(8,128)(2,1)}), bf16[16,180,384]{2,1,0:T(8,128)(2,1)S(1)}, u32[]{:S(2)}, u32[]{:S(2)}) async-start(bf16[16,180,384]{2,1,0:T(8,128)(2,1)} %broadcast_in_dim.278), calls=%async_computation | async-start | bytes 4521984 | tf_op jit(solution)/shard_map/all_to_all | solution.py:37
  21.5 4.4 %collective-permute-start = (bf16[128,512]{1,0:T(8,128)(2,1)}, bf16[128,512]{1,0:T(8,128)(2,1)S(1)}, u32[]{:S(2)}, u32[]{:S(2)}) collective-permute-start(bf16[128,512]{1,0:T(8,128)(2,1)} %pad_maximum_fusion.1), channel_id=1, source_target_pairs={{0,16},{16,32},{32,48},{48,64},{64,80},{80,96},{96,112},{112,128},... | collective-permute-start | bytes 393224 | tf_op jit(solution)/shard_map/ppermute | solution.py:52
  35.2 13.8 %all-to-all-done = bf16[16,180,384]{2,1,0:T(8,128)(2,1)S(1)} async-done(((bf16[16,180,384]{2,1,0:T(8,128)(2,1)}), bf16[16,180,384]{2,1,0:T(8,128)(2,1)S(1)}, u32[]{:S(2)}, u32[]{:S(2)}) %all-to-all-start) | async-done | bytes 2211872 | tf_op jit(solution)/shard_map/all_to_all | solution.py:37
  50.6 8.6 %all-to-all-start.1 = ((bf16[16,16,128]{2,1,0:T(8,128)(2,1)}), bf16[16,16,128]{2,1,0:T(8,128)(2,1)S(1)}, u32[]{:S(2)}, u32[]{:S(2)}) async-start(bf16[16,16,128]{2,1,0:T(8,128)(2,1)} %copy.187), calls=%async_computation.1 | async-start | bytes 131072 | tf_op jit(solution)/shard_map/all_to_all | solution.py:37
  59.2 2.6 reshape.459.refs_0_
  61.8 6.6 %collective-permute-start.4 = (bf16[2880,384]{1,0:T(8,128)(2,1)S(1)}, bf16[2880,384]{1,0:T(8,128)(2,1)}, u32[]{:S(2)}, u32[]{:S(2)}) collective-permute-start(bf16[2880,384]{1,0:T(8,128)(2,1)S(1)} %reshape.459.refs_0_), channel_id=1, source_target_pairs={{0,16},{16,0},{1,17},{17,1},{2,18},{18,2},{3,19},{19,3},{4,20},{20... | collective-permute-start | bytes 6635528 | tf_op jit(solution)/shard_map/ppermute | solution.py:46
  68.4 3.7 %collective-permute-start.3 = (bf16[2880,384]{1,0:T(8,128)(2,1)S(1)}, bf16[2880,384]{1,0:T(8,128)(2,1)}, u32[]{:S(2)}, u32[]{:S(2)}) collective-permute-start(bf16[2880,384]{1,0:T(8,128)(2,1)S(1)} %reshape.459.refs_0_), channel_id=1, source_target_pairs={{0,32},{32,0},{1,33},{33,1},{2,34},{34,2},{3,35},{35,3},{4,36},{36... | collective-permute-start | bytes 6635528 | tf_op jit(solution)/shard_map/ppermute | solution.py:46
  73.5 2.2 collective-permute-start.1
  78.2 7.0 %all-to-all-start.2 = ((bf16[16,8,2880]{2,1,0:T(8,128)(2,1)}), bf16[16,8,2880]{2,1,0:T(8,128)(2,1)}, u32[]{:S(2)}, u32[]{:S(2)}) async-start(bf16[16,8,2880]{2,1,0:T(8,128)(2,1)} %bitcast.180), calls=%async_computation.2 | async-start | bytes 1507328 | tf_op jit(solution)/shard_map/all_to_all | solution.py:37
  91.9 28.8 %collective-permute-done.2 = f32[8,128]{1,0:T(8,128)S(1)} collective-permute-done((f32[8,128]{1,0:T(8,128)S(1)}, f32[8,128]{1,0:T(8,128)S(1)}, u32[]{:S(2)}, u32[]{:S(2)}) %collective-permute-start.2) | collective-permute-done | bytes 4128 | tf_op jit(solution)/shard_map/ppermute | solution.py:46
  126.4 14.0 %all-to-all-start.3 = ((bf16[8,8,2944]{2,1,0:T(8,128)(2,1)}), bf16[8,8,2944]{2,1,0:T(8,128)(2,1)S(1)}, u32[]{:S(2)}, u32[]{:S(2)}) async-start(bf16[8,8,2944]{2,1,0:T(8,128)(2,1)} %bitcast.195), calls=%async_computation.3 | async-start | bytes 753664 | tf_op jit(solution)/shard_map/all_to_all | solution.py:37
  142.0 3.0 %collective-permute-start.5 = (bf16[2880,384]{1,0:T(8,128)(2,1)}, bf16[2880,384]{1,0:T(8,128)(2,1)}, u32[]{:S(2)}, u32[]{:S(2)}) collective-permute-start(bf16[2880,384]{1,0:T(8,128)(2,1)} %collective-permute-done.3.refs_1_), channel_id=1, source_target_pairs={{0,16},{16,0},{1,17},{17,1},{2,18},{18,2},{3,19},{19,3},{4,20},{20... | collective-permute-start | bytes 6635528 | tf_op jit(solution)/shard_map/ppermute | solution.py:46
  152.5 6.8 %all-to-all-done.3 = bf16[8,8,2944]{2,1,0:T(8,128)(2,1)S(1)} async-done(((bf16[8,8,2944]{2,1,0:T(8,128)(2,1)}), bf16[8,8,2944]{2,1,0:T(8,128)(2,1)S(1)}, u32[]{:S(2)}, u32[]{:S(2)}) %all-to-all-start.3) | async-done | bytes 376864 | tf_op jit(solution)/shard_map/all_to_all | solution.py:37
  159.4 6.5 %shard_map.192 = bf16[32,2944]{1,0:T(8,128)(2,1)S(1)} custom-call(bf16[64,2944]{1,0:T(8,128)(2,1)S(1)} %bitcast.182, bf16[2880,384]{1,0:T(8,128)(2,1)S(1)} %reshape.459.refs_0_, bf16[2880,384]{1,0:T(8,128)(2,1)} %collective-permute-done.3.refs_1_, bf16[2880,384]{1,0:T(8,128)(2,1)} %collective-permute-done.4.refs_2_, ...), custom_call_target="tpu_custom_call" | custom-call | flops 471859200 | bytes 9601024 | tf_op jit(solution)/shard_map/pallas_call | solution.py:146
  166.6 9.5 %all-to-all-start.4 = ((bf16[8,4,2944]{2,1,0:T(4,128)(2,1)}), bf16[8,4,2944]{2,1,0:T(4,128)(2,1)S(1)}, u32[]{:S(2)}, u32[]{:S(2)}) async-start(bf16[8,4,2944]{2,1,0:T(4,128)(2,1)} %reshape.460), calls=%async_computation.4 | async-start | bytes 376832 | tf_op jit(solution)/shard_map/all_to_all | solution.py:37
  176.8 6.4 %fusion.11 = bf16[128,2048]{1,0:T(8,128)(2,1)S(1)} fusion(bf16[2048,2880]{0,1:T(8,128)(2,1)} %all-gather.2.cloned.1.call-done, bf16[128,2880]{0,1:T(8,128)(2,1)} %bitcast.185, pred[128]{0:T(512)(128)(4,1)S(1)} %convert_compare_fusion, pred[128]{0:T(512)(128)(4,1)} %get-tuple-element.78), kind=kOutput, calls=%fused_computation.21 | convolution fusion | flops 1510842368 | bytes 13058304 | tf_op jit(solution)/shard_map/dot_general | solution.py:33
  186.0 3.8 %fusion = (f32[4,8,128]{2,1,0:T(8,128)S(1)}, f32[4,256,128,8]{2,1,3,0:T(8,128)S(1)}) fusion(f32[4,8,128]{2,1,0:T(8,128)S(1)} %copy-done.47, f32[4,8,128]{2,1,0:T(8,128)S(1)} %copy-done.34, f32[4,256,128,8]{2,1,3,0:T(8,128)} %copy-done.3, pred[128,256]{0,1:T(8,128)(4,1)S(1)} %and_and_fusion, bf16[256,4,64,1]{0,2,3,1:T(8,128)(2,1)S(1)} %bitcast.202, ...), kind=kOutput, calls=%fused_computation.2 | convolution fusion | flops 141553664 | bytes 9125888 | tf_op jit(solution)/shard_map/baqj,eaj->aqbe/dot_general | solution.py:81
  198.2 6.1 %convolution_convert_fusion.5 = bf16[8,2048]{1,0:T(8,128)(2,1)S(1)} fusion(bf16[8,2880]{1,0:T(8,128)(2,1)S(1)} %fusion.53, bf16[2048,2880]{0,1:T(8,128)(2,1)} %all-gather.2.cloned.1.call-done), kind=kOutput, calls=%fused_computation.26 | convolution fusion | flops 94388224 | bytes 11875328 | tf_op jit(solution)/shard_map/dot_general | solution.py:33
  206.1 10.0 %all-to-all-start.5 = ((f32[64,1,128]{2,1,0:T(1,128)}), f32[64,1,128]{2,1,0:T(1,128)}, u32[]{:S(2)}, u32[]{:S(2)}) async-start(f32[64,1,128]{2,1,0:T(1,128)} %broadcast_in_dim.311), calls=%async_computation.5 | async-start | bytes 65536 | tf_op jit(solution)/shard_map/all_to_all | solution.py:37
  219.4 4.5 %all-to-all-done.5 = f32[64,1,128]{2,1,0:T(1,128)} async-done(((f32[64,1,128]{2,1,0:T(1,128)}), f32[64,1,128]{2,1,0:T(1,128)}, u32[]{:S(2)}, u32[]{:S(2)}) %all-to-all-start.5) | async-done | bytes 32800 | tf_op jit(solution)/shard_map/all_to_all | solution.py:37
  227.0 11.8 %all-to-all-start.6 = ((f32[8,1,128]{2,1,0:T(1,128)}), f32[8,1,128]{2,1,0:T(1,128)S(1)}, u32[]{:S(2)}, u32[]{:S(2)}) async-start(f32[8,1,128]{2,1,0:T(1,128)} %broadcast_in_dim.318), calls=%async_computation.6 | async-start | bytes 8192 | tf_op jit(solution)/shard_map/all_to_all | solution.py:37
  239.8 2.9 %collective-permute-start.6 = (bf16[128,512]{1,0:T(8,128)(2,1)S(1)}, bf16[128,512]{1,0:T(8,128)(2,1)S(1)}, u32[]{:S(2)}, u32[]{:S(2)}) collective-permute-start(bf16[128,512]{1,0:T(8,128)(2,1)S(1)} %pad_maximum_fusion.4), channel_id=1, source_target_pairs={{16,0},{32,16},{48,32},{64,48},{80,64},{96,80},{112,96},{128,112},... | collective-permute-start | bytes 393224 | tf_op jit(solution)/shard_map/ppermute | solution.py:52
  242.8 2.0 fusion.5
  246.6 3.4 %all-to-all-done.6 = f32[8,1,128]{2,1,0:T(1,128)S(1)} async-done(((f32[8,1,128]{2,1,0:T(1,128)}), f32[8,1,128]{2,1,0:T(1,128)S(1)}, u32[]{:S(2)}, u32[]{:S(2)}) %all-to-all-start.6) | async-done | bytes 4128 | tf_op jit(solution)/shard_map/all_to_all | solution.py:37
  (291 shorter events, 61.6 us)
Async XLA Ops:
  7.2 71.0 %copy-start = (bf16[1,128,2880]{1,2,0:T(8,128)(2,1)S(1)}, bf16[1,128,2880]{1,2,0:T(8,128)(2,1)}, u32[]{:S(2)}) copy-start(bf16[1,128,2880]{1,2,0:T(8,128)(2,1)} %param.20) | copy-start | bytes 2211844
  7.2 169.6 %all-gather.2.cloned.1.call-start = ((), (), s32[]{:S(2)}) async-start(), calls=%async_computation.7 | async-start | bytes 12533760 | tf_op jit(solution)/shard_map/all_gather | solution.py:247
  13.2 35.8 %all-to-all-start = ((bf16[16,180,384]{2,1,0:T(8,128)(2,1)}), bf16[16,180,384]{2,1,0:T(8,128)(2,1)S(1)}, u32[]{:S(2)}, u32[]{:S(2)}) async-start(bf16[16,180,384]{2,1,0:T(8,128)(2,1)} %broadcast_in_dim.278), calls=%async_computation | async-start | bytes 4521984 | tf_op jit(solution)/shard_map/all_to_all | solution.py:37
  21.5 9.4 %collective-permute-start = (bf16[128,512]{1,0:T(8,128)(2,1)}, bf16[128,512]{1,0:T(8,128)(2,1)S(1)}, u32[]{:S(2)}, u32[]{:S(2)}) collective-permute-start(bf16[128,512]{1,0:T(8,128)(2,1)} %pad_maximum_fusion.1), channel_id=1, source_target_pairs={{0,16},{16,32},{32,48},{48,64},{64,80},{80,96},{96,112},{112,128},... | collective-permute-start | bytes 393224 | tf_op jit(solution)/shard_map/ppermute | solution.py:52
  29.6 47.6 %copy-start.26 = (bf16[8,4,8,64]{3,2,1,0:T(8,128)(2,1)}, bf16[8,4,8,64]{3,2,1,0:T(8,128)(2,1)S(1)}, u32[]{:S(2)}) copy-start(bf16[8,4,8,64]{3,2,1,0:T(8,128)(2,1)S(1)} %reshape.452) | copy-start | bytes 98308
  31.1 46.2 %copy-start.22 = (bf16[256,256]{0,1:T(8,128)(2,1)}, bf16[256,256]{0,1:T(8,128)(2,1)S(1)}, u32[]{:S(2)}) copy-start(bf16[256,256]{0,1:T(8,128)(2,1)S(1)} %copy.182) | copy-start | bytes 393220
  31.2 116.8 %copy-start.12 = (bf16[256,256]{0,1:T(8,128)(2,1)}, bf16[256,256]{0,1:T(8,128)(2,1)S(1)}, u32[]{:S(2)}) copy-start(bf16[256,256]{0,1:T(8,128)(2,1)S(1)} %copy.183) | copy-start | bytes 393220
  50.6 21.5 %all-to-all-start.1 = ((bf16[16,16,128]{2,1,0:T(8,128)(2,1)}), bf16[16,16,128]{2,1,0:T(8,128)(2,1)S(1)}, u32[]{:S(2)}, u32[]{:S(2)}) async-start(bf16[16,16,128]{2,1,0:T(8,128)(2,1)} %copy.187), calls=%async_computation.1 | async-start | bytes 131072 | tf_op jit(solution)/shard_map/all_to_all | solution.py:37
  59.1 64.8 %copy-start.43 = (bf16[8,128]{1,0:T(8,128)(2,1)S(1)}, bf16[8,128]{1,0:T(8,128)(2,1)}, u32[]{:S(2)}) copy-start(bf16[8,128]{1,0:T(8,128)(2,1)} %get-tuple-element.49) | copy-start | bytes 6148
  59.2 65.3 %copy-start.49 = (f32[2880]{0:T(1024)S(1)}, f32[2880]{0:T(1024)}, u32[]{:S(2)}) copy-start(f32[2880]{0:T(1024)} %param.22) | copy-start | bytes 34564
  59.2 65.6 %copy-start.68 = (s32[8]{0:T(128)S(1)}, s32[8]{0:T(128)}, u32[]{:S(2)}) copy-start(s32[8]{0:T(128)} %iota_add_fusion) | copy-start | bytes 100
  61.8 78.6 %copy-start.59 = (s32[1,128,4]{1,2,0:T(4,128)S(1)}, s32[1,128,4]{1,2,0:T(4,128)}, u32[]{:S(2)}) copy-start(s32[1,128,4]{1,2,0:T(4,128)} %param.27) | copy-start | bytes 6148
  61.8 97.6 %collective-permute-start.4 = (bf16[2880,384]{1,0:T(8,128)(2,1)S(1)}, bf16[2880,384]{1,0:T(8,128)(2,1)}, u32[]{:S(2)}, u32[]{:S(2)}) collective-permute-start(bf16[2880,384]{1,0:T(8,128)(2,1)S(1)} %reshape.459.refs_0_), channel_id=1, source_target_pairs={{0,16},{16,0},{1,17},{17,1},{2,18},{18,2},{3,19},{19,3},{4,20},{20... | collective-permute-start | bytes 6635528 | tf_op jit(solution)/shard_map/ppermute | solution.py:46
  68.4 73.6 %collective-permute-start.3 = (bf16[2880,384]{1,0:T(8,128)(2,1)S(1)}, bf16[2880,384]{1,0:T(8,128)(2,1)}, u32[]{:S(2)}, u32[]{:S(2)}) collective-permute-start(bf16[2880,384]{1,0:T(8,128)(2,1)S(1)} %reshape.459.refs_0_), channel_id=1, source_target_pairs={{0,32},{32,0},{1,33},{33,1},{2,34},{34,2},{3,35},{35,3},{4,36},{36... | collective-permute-start | bytes 6635528 | tf_op jit(solution)/shard_map/ppermute | solution.py:46
  73.5 13.3 %collective-permute-start.1 = (f32[8,128]{1,0:T(8,128)S(1)}, f32[8,128]{1,0:T(8,128)S(1)}, u32[]{:S(2)}, u32[]{:S(2)}) collective-permute-start(f32[8,128]{1,0:T(8,128)S(1)} %broadcast_in_dim.285), channel_id=1, source_target_pairs={{0,16},{16,0},{1,17},{17,1},{2,18},{18,2},{3,19},{19,3},{4,20},{20... | collective-permute-start | bytes 12296 | tf_op jit(solution)/shard_map/ppermute | solution.py:46
  78.2 44.5 %all-to-all-start.2 = ((bf16[16,8,2880]{2,1,0:T(8,128)(2,1)}), bf16[16,8,2880]{2,1,0:T(8,128)(2,1)}, u32[]{:S(2)}, u32[]{:S(2)}) async-start(bf16[16,8,2880]{2,1,0:T(8,128)(2,1)} %bitcast.180), calls=%async_computation.2 | async-start | bytes 1507328 | tf_op jit(solution)/shard_map/all_to_all | solution.py:37
  86.6 39.7 %copy-start.32 = (bf16[8,2880]{1,0:T(8,128)(2,1)}, bf16[8,2880]{1,0:T(8,128)(2,1)S(1)}, u32[]{:S(2)}) copy-start(bf16[8,2880]{1,0:T(8,128)(2,1)S(1)} %convolution_convert_fusion.2) | copy-start | bytes 138244
  87.5 33.2 %collective-permute-start.2 = (f32[8,128]{1,0:T(8,128)S(1)}, f32[8,128]{1,0:T(8,128)S(1)}, u32[]{:S(2)}, u32[]{:S(2)}) collective-permute-start(f32[8,128]{1,0:T(8,128)S(1)} %broadcast_add_fusion), channel_id=1, source_target_pairs={{0,32},{32,0},{1,33},{33,1},{2,34},{34,2},{3,35},{35,3},{4,36},{36... | collective-permute-start | bytes 12296 | tf_op jit(solution)/shard_map/ppermute | solution.py:46
  126.4 33.0 %all-to-all-start.3 = ((bf16[8,8,2944]{2,1,0:T(8,128)(2,1)}), bf16[8,8,2944]{2,1,0:T(8,128)(2,1)S(1)}, u32[]{:S(2)}, u32[]{:S(2)}) async-start(bf16[8,8,2944]{2,1,0:T(8,128)(2,1)} %bitcast.195), calls=%async_computation.3 | async-start | bytes 753664 | tf_op jit(solution)/shard_map/all_to_all | solution.py:37
  142.0 17.4 %collective-permute-start.5 = (bf16[2880,384]{1,0:T(8,128)(2,1)}, bf16[2880,384]{1,0:T(8,128)(2,1)}, u32[]{:S(2)}, u32[]{:S(2)}) collective-permute-start(bf16[2880,384]{1,0:T(8,128)(2,1)} %collective-permute-done.3.refs_1_), channel_id=1, source_target_pairs={{0,16},{16,0},{1,17},{17,1},{2,18},{18,2},{3,19},{19,3},{4,20},{20... | collective-permute-start | bytes 6635528 | tf_op jit(solution)/shard_map/ppermute | solution.py:46
  166.6 28.3 %all-to-all-start.4 = ((bf16[8,4,2944]{2,1,0:T(4,128)(2,1)}), bf16[8,4,2944]{2,1,0:T(4,128)(2,1)S(1)}, u32[]{:S(2)}, u32[]{:S(2)}) async-start(bf16[8,4,2944]{2,1,0:T(4,128)(2,1)} %reshape.460), calls=%async_computation.4 | async-start | bytes 376832 | tf_op jit(solution)/shard_map/all_to_all | solution.py:37
  206.1 17.8 %all-to-all-start.5 = ((f32[64,1,128]{2,1,0:T(1,128)}), f32[64,1,128]{2,1,0:T(1,128)}, u32[]{:S(2)}, u32[]{:S(2)}) async-start(f32[64,1,128]{2,1,0:T(1,128)} %broadcast_in_dim.311), calls=%async_computation.5 | async-start | bytes 65536 | tf_op jit(solution)/shard_map/all_to_all | solution.py:37
  227.0 23.0 %all-to-all-start.6 = ((f32[8,1,128]{2,1,0:T(1,128)}), f32[8,1,128]{2,1,0:T(1,128)S(1)}, u32[]{:S(2)}, u32[]{:S(2)}) async-start(f32[8,1,128]{2,1,0:T(1,128)} %broadcast_in_dim.318), calls=%async_computation.6 | async-start | bytes 8192 | tf_op jit(solution)/shard_map/all_to_all | solution.py:37
  239.8 10.8 %collective-permute-start.6 = (bf16[128,512]{1,0:T(8,128)(2,1)S(1)}, bf16[128,512]{1,0:T(8,128)(2,1)S(1)}, u32[]{:S(2)}, u32[]{:S(2)}) collective-permute-start(bf16[128,512]{1,0:T(8,128)(2,1)S(1)} %pad_maximum_fusion.4), channel_id=1, source_target_pairs={{16,0},{32,16},{48,32},{64,48},{80,64},{96,80},{112,96},{128,112},... | collective-permute-start | bytes 393224 | tf_op jit(solution)/shard_map/ppermute | solution.py:52
  (62 other events, 491.1 us)
Sparse Core Ops, SparseCore 0:
  13.4 132.9 all-gather.1

commit v7 on v5

--- a/solution.py
+++ b/solution.py
@@ -222,8 +222,8 @@
 
     shard = jnp.concatenate([expert_gate, expert_up, expert_down], axis=1)
     spread_shard = jnp.broadcast_to(shard[None], (dp_count, *shard.shape))
-    spread_shard, own_keys, own_values, mask_row = lax.optimization_barrier(
-        (spread_shard, key_rows[0], value_matrix[0], response_mask[0])
+    spread_shard, own_keys, own_values, mask_row, query_rows = lax.optimization_barrier(
+        (spread_shard, key_rows[0], value_matrix[0], response_mask[0], query_rows)
     )
     gathered = exchange(spread_shard, "dp")
 
@@ -243,6 +243,8 @@
 
     slot_rows = jnp.sum(jnp.where(pick, row_index[:, 0][None, :], 0), axis=1, keepdims=True)
     query_slots = dot32(pick_low, query_rows).astype(BF16)
+    query_slots, late_weight = lax.optimization_barrier((query_slots, out_weight))
+    out_full = lax.all_gather(late_weight, "dp", axis=0, tiled=True)
     probs_slots, sink_slots = head_scores(
         query_slots, keys_here, head_sink_logits, visible(slot_rows, col_index)
     )
@@ -266,8 +268,7 @@
         [columns, jnp.broadcast_to(facts_row[None], (dp_count, 1, lanes))], axis=1
     )
     sent = jnp.pad(sent, ((0, 0), (0, 2 * SLOTS - SLOTS - 1), (0, 0)))
-    sent, gathered, late_weight = lax.optimization_barrier((sent, gathered, out_weight))
-    out_full = lax.all_gather(late_weight, "dp", axis=0, tiled=True)
+    sent, gathered = lax.optimization_barrier((sent, gathered))
     arrived = exchange(sent, "dp")
     facts_all = arrived[:, SLOTS, :4].astype(F32)
     partial = project_slots(arrived.reshape(dp_count * 2 * SLOTS, lanes), out_weight.T)
@@ -279,7 +280,8 @@
     projected = jnp.sum(partial.astype(F32), axis=0)
     own_block = gathered.reshape(D, shard.shape[1])
     half_block = swap(own_block, "half")
-    blocks = (own_block, half_block, swap(own_block, "core"), swap(half_block, "core"))
+    core_block = swap(own_block, "core")
+    blocks = (own_block, half_block, core_block, swap(half_block, "core"))
 
     residual_slots = dot32(pick_low, residual_rows)
     upstream_slots = dot32(pick_low, upstream_rows).astype(BF16)

time: 249 us -> 242 us (0.972)
  starting transfers between devices: 83.9 us -> 92.8 us
  local copies, waits for them, and re-layouts: 30 us -> 24.6 us
  other arithmetic: 27.8 us -> 22.9 us
  waiting for transfers between devices: 44 us -> 40.1 us
    all_to_all x7, waiting for transfers between devices: 23.7 us -> 39.1 us  [exchange(): return lax.all_to_all(value, axis, split_axis=0, concat_axis=0, tiled=True)]
    ppermute x5, waiting for transfers between devices: 10.8 us -> 0.96 us  [swap(): return lax.ppermute(value, axis, [(0, 1), (1, 0)])]
    all_gather x1, waiting for transfers between devices: 9.52 us -> 0.01 us  [shards(): out_full = lax.all_gather(late_weight, 'dp', axis=0, tiled=True)]
    all_to_all x7, starting transfers between devices: 62 us -> 66.7 us  [exchange(): return lax.all_to_all(value, axis, split_axis=0, concat_axis=0, tiled=True)]
    ppermute x5, starting transfers between devices: 16.9 us -> 21.3 us  [swap(): return lax.ppermute(value, axis, [(0, 1), (1, 0)])]
    unnamed x136 -> x144, local copies, waits for them, and re-layouts: 6.96 us -> 6.89 us
  transfers between devices with their start and end apart: 15 -> 15, of which waited for: 6 -> 6; matrix products, arithmetic and copies ran while one was open for 28% -> 22% of each run, Pallas kernels for 3% -> 3%
where the time goes in v7:
time: 242 us; the launch traced here: 241 us
  starting transfers between devices  92.8 us (38%)
  waiting for transfers between devices  40.1 us (17%)
  matrix products  31.6 us (13%)
  local copies, waits for them, and re-layouts  24.6 us (10%)
  other arithmetic  22.9 us (9%)
  between operations  21.8 us (9%)
  Pallas kernels  6.97 us (3%)
    all_to_all x7, starting transfers between devices, exchange(): return lax.all_to_all(value, axis, split_axis=0, concat_axis=0, tiled=True)  66.7 us
    all_to_all x7, waiting for transfers between devices, exchange(): return lax.all_to_all(value, axis, split_axis=0, concat_axis=0, tiled=True)  39.1 us
    ppermute x5, starting transfers between devices, swap(): return lax.ppermute(value, axis, [(0, 1), (1, 0)])  21.3 us
    dot_general x4, matrix products, dot_last(): return lax.dot_general(a, b, CONTRACT_LAST, preferred_element_type=F32)  12.9 us
    unnamed x144, local copies, waits for them, and re-layouts  6.89 us
    pallas_call x1, Pallas kernels, experts_step(): pl.pallas_call(experts_kernel, out_shape=jax.ShapeDtypeStruct((count // 2...  6.51 us
  transfers between devices with their start and end apart: 15, of which 6 were waited for; matrix products, arithmetic and copies ran while one was open for 22% of the time, Pallas kernels for 3%

profile of v7, /device:TPU:1, one launch (start us, length us, event | category | flops | bytes accessed | tf_op | source)
XLA Modules:
  0.0 240.8 jit_solution(13715730267103483869)
XLA Ops:
  13.2 7.6 %all-to-all-start = ((bf16[16,180,384]{2,1,0:T(8,128)(2,1)}), bf16[16,180,384]{2,1,0:T(8,128)(2,1)S(1)}, u32[]{:S(2)}, u32[]{:S(2)}) async-start(bf16[16,180,384]{2,1,0:T(8,128)(2,1)} %broadcast_in_dim.278), calls=%async_computation | async-start | bytes 4521984 | tf_op jit(solution)/shard_map/all_to_all | solution.py:37
  22.1 4.9 %collective-permute-start.1 = (f32[8,128]{1,0:T(8,128)S(1)}, f32[8,128]{1,0:T(8,128)S(1)}, u32[]{:S(2)}, u32[]{:S(2)}) collective-permute-start(f32[8,128]{1,0:T(8,128)S(1)} %broadcast_in_dim.284), channel_id=1, source_target_pairs={{0,16},{16,0},{1,17},{17,1},{2,18},{18,2},{3,19},{19,3},{4,20},{20... | collective-permute-start | bytes 12296 | tf_op jit(solution)/shard_map/ppermute | solution.py:46
  30.7 3.0 %collective-permute-start.2 = (f32[8,128]{1,0:T(8,128)S(1)}, f32[8,128]{1,0:T(8,128)S(1)}, u32[]{:S(2)}, u32[]{:S(2)}) collective-permute-start(f32[8,128]{1,0:T(8,128)S(1)} %broadcast_add_fusion), channel_id=1, source_target_pairs={{0,32},{32,0},{1,33},{33,1},{2,34},{34,2},{3,35},{35,3},{4,36},{36... | collective-permute-start | bytes 12296 | tf_op jit(solution)/shard_map/ppermute | solution.py:46
  43.6 5.5 %all-to-all-done = bf16[16,180,384]{2,1,0:T(8,128)(2,1)S(1)} async-done(((bf16[16,180,384]{2,1,0:T(8,128)(2,1)}), bf16[16,180,384]{2,1,0:T(8,128)(2,1)S(1)}, u32[]{:S(2)}, u32[]{:S(2)}) %all-to-all-start) | async-done | bytes 2211872 | tf_op jit(solution)/shard_map/all_to_all | solution.py:37
  50.5 8.6 %all-to-all-start.1 = ((bf16[16,16,128]{2,1,0:T(8,128)(2,1)}), bf16[16,16,128]{2,1,0:T(8,128)(2,1)S(1)}, u32[]{:S(2)}, u32[]{:S(2)}) async-start(bf16[16,16,128]{2,1,0:T(8,128)(2,1)} %copy.187), calls=%async_computation.1 | async-start | bytes 131072 | tf_op jit(solution)/shard_map/all_to_all | solution.py:37
  59.2 2.6 %reshape.462.refs_0_ = bf16[2880,384]{1,0:T(8,128)(2,1)S(1)} reshape(bf16[16,180,384]{2,1,0:T(8,128)(2,1)} %copy-done.6) | data formatting | bytes 4423680 | tf_op jit(solution)/shard_map/reshape | solution.py:281
  61.8 6.6 %collective-permute-start.4 = (bf16[2880,384]{1,0:T(8,128)(2,1)S(1)}, bf16[2880,384]{1,0:T(8,128)(2,1)}, u32[]{:S(2)}, u32[]{:S(2)}) collective-permute-start(bf16[2880,384]{1,0:T(8,128)(2,1)S(1)} %reshape.462.refs_0_), channel_id=1, source_target_pairs={{0,16},{16,0},{1,17},{17,1},{2,18},{18,2},{3,19},{19,3},{4,20},{20... | collective-permute-start | bytes 6635528 | tf_op jit(solution)/shard_map/ppermute | solution.py:46
  68.4 3.7 %collective-permute-start.3 = (bf16[2880,384]{1,0:T(8,128)(2,1)S(1)}, bf16[2880,384]{1,0:T(8,128)(2,1)}, u32[]{:S(2)}, u32[]{:S(2)}) collective-permute-start(bf16[2880,384]{1,0:T(8,128)(2,1)S(1)} %reshape.462.refs_0_), channel_id=1, source_target_pairs={{0,32},{32,0},{1,33},{33,1},{2,34},{34,2},{3,35},{35,3},{4,36},{36... | collective-permute-start | bytes 6635528 | tf_op jit(solution)/shard_map/ppermute | solution.py:46
  74.7 7.0 %all-to-all-start.2 = ((bf16[16,8,2880]{2,1,0:T(8,128)(2,1)}), bf16[16,8,2880]{2,1,0:T(8,128)(2,1)}, u32[]{:S(2)}, u32[]{:S(2)}) async-start(bf16[16,8,2880]{2,1,0:T(8,128)(2,1)} %bitcast.181), calls=%async_computation.2 | async-start | bytes 1507328 | tf_op jit(solution)/shard_map/all_to_all | solution.py:37
  87.4 9.6 %all-to-all-done.2 = bf16[16,8,2880]{2,1,0:T(8,128)(2,1)} async-done(((bf16[16,8,2880]{2,1,0:T(8,128)(2,1)}), bf16[16,8,2880]{2,1,0:T(8,128)(2,1)}, u32[]{:S(2)}, u32[]{:S(2)}) %all-to-all-start.2) | async-done | bytes 737312 | tf_op jit(solution)/shard_map/all_to_all | solution.py:37
  100.6 17.5 %all-to-all-start.3 = ((bf16[8,8,2944]{2,1,0:T(8,128)(2,1)}), bf16[8,8,2944]{2,1,0:T(8,128)(2,1)S(1)}, u32[]{:S(2)}, u32[]{:S(2)}) async-start(bf16[8,8,2944]{2,1,0:T(8,128)(2,1)} %bitcast.196), calls=%async_computation.3 | async-start | bytes 753664 | tf_op jit(solution)/shard_map/all_to_all | solution.py:37
  120.6 3.0 %collective-permute-start.5 = (bf16[2880,384]{1,0:T(8,128)(2,1)}, bf16[2880,384]{1,0:T(8,128)(2,1)}, u32[]{:S(2)}, u32[]{:S(2)}) collective-permute-start(bf16[2880,384]{1,0:T(8,128)(2,1)} %collective-permute-done.3.refs_1_), channel_id=1, source_target_pairs={{0,16},{16,0},{1,17},{17,1},{2,18},{18,2},{3,19},{19,3},{4,20},{20... | collective-permute-start | bytes 6635528 | tf_op jit(solution)/shard_map/ppermute | solution.py:46
  131.2 17.0 %all-to-all-done.3 = bf16[8,8,2944]{2,1,0:T(8,128)(2,1)S(1)} async-done(((bf16[8,8,2944]{2,1,0:T(8,128)(2,1)}), bf16[8,8,2944]{2,1,0:T(8,128)(2,1)S(1)}, u32[]{:S(2)}, u32[]{:S(2)}) %all-to-all-start.3) | async-done | bytes 376864 | tf_op jit(solution)/shard_map/all_to_all | solution.py:37
  148.2 6.5 %shard_map.192 = bf16[32,2944]{1,0:T(8,128)(2,1)S(1)} custom-call(bf16[64,2944]{1,0:T(8,128)(2,1)S(1)} %bitcast.183, bf16[2880,384]{1,0:T(8,128)(2,1)S(1)} %reshape.462.refs_0_, bf16[2880,384]{1,0:T(8,128)(2,1)} %collective-permute-done.3.refs_1_, bf16[2880,384]{1,0:T(8,128)(2,1)} %collective-permute-done.4.refs_2_, ...), custom_call_target="tpu_custom_call" | custom-call | flops 471859200 | bytes 9601024 | tf_op jit(solution)/shard_map/pallas_call | solution.py:146
  155.5 6.7 %all-to-all-start.4 = ((bf16[8,4,2944]{2,1,0:T(4,128)(2,1)}), bf16[8,4,2944]{2,1,0:T(4,128)(2,1)S(1)}, u32[]{:S(2)}, u32[]{:S(2)}) async-start(bf16[8,4,2944]{2,1,0:T(4,128)(2,1)} %reshape.463), calls=%async_computation.4 | async-start | bytes 376832 | tf_op jit(solution)/shard_map/all_to_all | solution.py:37
  162.9 6.4 %fusion.11 = bf16[128,2048]{1,0:T(8,128)(2,1)S(1)} fusion(bf16[2048,2880]{0,1:T(8,128)(2,1)} %all-gather.2.cloned.1.call-done, bf16[128,2880]{0,1:T(8,128)(2,1)} %bitcast.186, pred[128]{0:T(512)(128)(4,1)S(1)} %convert_compare_fusion, pred[128]{0:T(512)(128)(4,1)} %get-tuple-element.78), kind=kOutput, calls=%fused_computation.21 | convolution fusion | flops 1510842368 | bytes 13058304 | tf_op jit(solution)/shard_map/dot_general | solution.py:33
  172.1 3.8 %fusion = (f32[4,8,128]{2,1,0:T(8,128)S(1)}, f32[4,256,128,8]{2,1,3,0:T(8,128)S(1)}) fusion(f32[4,8,128]{2,1,0:T(8,128)S(1)} %copy-done.47, f32[4,8,128]{2,1,0:T(8,128)S(1)} %copy-done.34, f32[4,256,128,8]{2,1,3,0:T(8,128)} %copy-done.3, pred[128,256]{0,1:T(8,128)(4,1)S(1)} %and_and_fusion, bf16[256,4,64,1]{0,2,3,1:T(8,128)(2,1)S(1)} %bitcast.203, ...), kind=kOutput, calls=%fused_computation.2 | convolution fusion | flops 141553664 | bytes 9125888 | tf_op jit(solution)/shard_map/baqj,eaj->aqbe/dot_general | solution.py:81
  184.3 6.1 %convolution_convert_fusion.5 = bf16[8,2048]{1,0:T(8,128)(2,1)S(1)} fusion(bf16[8,2880]{1,0:T(8,128)(2,1)S(1)} %fusion.53, bf16[2048,2880]{0,1:T(8,128)(2,1)} %all-gather.2.cloned.1.call-done), kind=kOutput, calls=%fused_computation.26 | convolution fusion | flops 94388224 | bytes 11875328 | tf_op jit(solution)/shard_map/dot_general | solution.py:33
  192.2 7.5 %all-to-all-start.5 = ((f32[32,1,128]{2,1,0:T(1,128)}), f32[32,1,128]{2,1,0:T(1,128)}, u32[]{:S(2)}, u32[]{:S(2)}) async-start(f32[32,1,128]{2,1,0:T(1,128)} %broadcast_in_dim.311), calls=%async_computation.5 | async-start | bytes 32768 | tf_op jit(solution)/shard_map/all_to_all | solution.py:37
  203.0 3.6 %all-to-all-done.5 = f32[32,1,128]{2,1,0:T(1,128)} async-done(((f32[32,1,128]{2,1,0:T(1,128)}), f32[32,1,128]{2,1,0:T(1,128)}, u32[]{:S(2)}, u32[]{:S(2)}) %all-to-all-start.5) | async-done | bytes 16416 | tf_op jit(solution)/shard_map/all_to_all | solution.py:37
  209.6 11.8 %all-to-all-start.6 = ((f32[16,1,128]{2,1,0:T(1,128)}), f32[16,1,128]{2,1,0:T(1,128)S(1)}, u32[]{:S(2)}, u32[]{:S(2)}) async-start(f32[16,1,128]{2,1,0:T(1,128)} %broadcast_in_dim.318), calls=%async_computation.6 | async-start | bytes 16384 | tf_op jit(solution)/shard_map/all_to_all | solution.py:37
  222.5 2.9 %collective-permute-start.6 = (bf16[128,512]{1,0:T(8,128)(2,1)S(1)}, bf16[128,512]{1,0:T(8,128)(2,1)S(1)}, u32[]{:S(2)}, u32[]{:S(2)}) collective-permute-start(bf16[128,512]{1,0:T(8,128)(2,1)S(1)} %pad_maximum_fusion.4), channel_id=1, source_target_pairs={{16,0},{32,16},{48,32},{64,48},{80,64},{96,80},{112,96},{128,112},... | collective-permute-start | bytes 393224 | tf_op jit(solution)/shard_map/ppermute | solution.py:52
  225.4 2.0 fusion.5
  229.3 3.4 %all-to-all-done.6 = f32[16,1,128]{2,1,0:T(1,128)S(1)} async-done(((f32[16,1,128]{2,1,0:T(1,128)}), f32[16,1,128]{2,1,0:T(1,128)S(1)}, u32[]{:S(2)}, u32[]{:S(2)}) %all-to-all-start.6) | async-done | bytes 8224 | tf_op jit(solution)/shard_map/all_to_all | solution.py:37
  (291 shorter events, 61.7 us)
Async XLA Ops:
  7.2 67.6 %copy-start = (bf16[1,128,2880]{1,2,0:T(8,128)(2,1)S(1)}, bf16[1,128,2880]{1,2,0:T(8,128)(2,1)}, u32[]{:S(2)}) copy-start(bf16[1,128,2880]{1,2,0:T(8,128)(2,1)} %param.20) | copy-start | bytes 2211844
  7.2 155.7 %all-gather.2.cloned.1.call-start = ((), (), s32[]{:S(2)}) async-start(), calls=%async_computation.7 | async-start | bytes 12533760 | tf_op jit(solution)/shard_map/all_gather | solution.py:247
  13.2 35.8 %all-to-all-start = ((bf16[16,180,384]{2,1,0:T(8,128)(2,1)}), bf16[16,180,384]{2,1,0:T(8,128)(2,1)S(1)}, u32[]{:S(2)}, u32[]{:S(2)}) async-start(bf16[16,180,384]{2,1,0:T(8,128)(2,1)} %broadcast_in_dim.278), calls=%async_computation | async-start | bytes 4521984 | tf_op jit(solution)/shard_map/all_to_all | solution.py:37
  22.1 7.9 %collective-permute-start.1 = (f32[8,128]{1,0:T(8,128)S(1)}, f32[8,128]{1,0:T(8,128)S(1)}, u32[]{:S(2)}, u32[]{:S(2)}) collective-permute-start(f32[8,128]{1,0:T(8,128)S(1)} %broadcast_in_dim.284), channel_id=1, source_target_pairs={{0,16},{16,0},{1,17},{17,1},{2,18},{18,2},{3,19},{19,3},{4,20},{20... | collective-permute-start | bytes 12296 | tf_op jit(solution)/shard_map/ppermute | solution.py:46
  27.7 11.6 %collective-permute-start = (bf16[128,512]{1,0:T(8,128)(2,1)}, bf16[128,512]{1,0:T(8,128)(2,1)S(1)}, u32[]{:S(2)}, u32[]{:S(2)}) collective-permute-start(bf16[128,512]{1,0:T(8,128)(2,1)} %pad_maximum_fusion.1), channel_id=1, source_target_pairs={{0,16},{16,32},{32,48},{48,64},{64,80},{80,96},{96,112},{112,128},... | collective-permute-start | bytes 393224 | tf_op jit(solution)/shard_map/ppermute | solution.py:52
  30.7 6.3 %collective-permute-start.2 = (f32[8,128]{1,0:T(8,128)S(1)}, f32[8,128]{1,0:T(8,128)S(1)}, u32[]{:S(2)}, u32[]{:S(2)}) collective-permute-start(f32[8,128]{1,0:T(8,128)S(1)} %broadcast_add_fusion), channel_id=1, source_target_pairs={{0,32},{32,0},{1,33},{33,1},{2,34},{34,2},{3,35},{35,3},{4,36},{36... | collective-permute-start | bytes 12296 | tf_op jit(solution)/shard_map/ppermute | solution.py:46
  36.4 37.4 %copy-start.26 = (bf16[8,4,8,64]{3,2,1,0:T(8,128)(2,1)}, bf16[8,4,8,64]{3,2,1,0:T(8,128)(2,1)S(1)}, u32[]{:S(2)}) copy-start(bf16[8,4,8,64]{3,2,1,0:T(8,128)(2,1)S(1)} %reshape.455) | copy-start | bytes 98308
  39.5 34.3 %copy-start.22 = (bf16[256,256]{0,1:T(8,128)(2,1)}, bf16[256,256]{0,1:T(8,128)(2,1)S(1)}, u32[]{:S(2)}) copy-start(bf16[256,256]{0,1:T(8,128)(2,1)S(1)} %copy.182) | copy-start | bytes 393220
  39.6 87.1 %copy-start.12 = (bf16[256,256]{0,1:T(8,128)(2,1)}, bf16[256,256]{0,1:T(8,128)(2,1)S(1)}, u32[]{:S(2)}) copy-start(bf16[256,256]{0,1:T(8,128)(2,1)S(1)} %copy.183) | copy-start | bytes 393220
  50.5 21.5 %all-to-all-start.1 = ((bf16[16,16,128]{2,1,0:T(8,128)(2,1)}), bf16[16,16,128]{2,1,0:T(8,128)(2,1)S(1)}, u32[]{:S(2)}, u32[]{:S(2)}) async-start(bf16[16,16,128]{2,1,0:T(8,128)(2,1)} %copy.187), calls=%async_computation.1 | async-start | bytes 131072 | tf_op jit(solution)/shard_map/all_to_all | solution.py:37
  59.1 39.0 %copy-start.43 = (bf16[8,128]{1,0:T(8,128)(2,1)S(1)}, bf16[8,128]{1,0:T(8,128)(2,1)}, u32[]{:S(2)}) copy-start(bf16[8,128]{1,0:T(8,128)(2,1)} %get-tuple-element.49) | copy-start | bytes 6148
  59.2 39.5 %copy-start.49 = (f32[2880]{0:T(1024)S(1)}, f32[2880]{0:T(1024)}, u32[]{:S(2)}) copy-start(f32[2880]{0:T(1024)} %param.22) | copy-start | bytes 34564
  59.2 39.9 %copy-start.68 = (s32[8]{0:T(128)S(1)}, s32[8]{0:T(128)}, u32[]{:S(2)}) copy-start(s32[8]{0:T(128)} %iota_add_fusion) | copy-start | bytes 100
  61.7 56.3 %copy-start.59 = (s32[1,128,4]{1,2,0:T(4,128)S(1)}, s32[1,128,4]{1,2,0:T(4,128)}, u32[]{:S(2)}) copy-start(s32[1,128,4]{1,2,0:T(4,128)} %param.27) | copy-start | bytes 6148
  61.8 86.5 %collective-permute-start.4 = (bf16[2880,384]{1,0:T(8,128)(2,1)S(1)}, bf16[2880,384]{1,0:T(8,128)(2,1)}, u32[]{:S(2)}, u32[]{:S(2)}) collective-permute-start(bf16[2880,384]{1,0:T(8,128)(2,1)S(1)} %reshape.462.refs_0_), channel_id=1, source_target_pairs={{0,16},{16,0},{1,17},{17,1},{2,18},{18,2},{3,19},{19,3},{4,20},{20... | collective-permute-start | bytes 6635528 | tf_op jit(solution)/shard_map/ppermute | solution.py:46
  68.4 52.2 %collective-permute-start.3 = (bf16[2880,384]{1,0:T(8,128)(2,1)S(1)}, bf16[2880,384]{1,0:T(8,128)(2,1)}, u32[]{:S(2)}, u32[]{:S(2)}) collective-permute-start(bf16[2880,384]{1,0:T(8,128)(2,1)S(1)} %reshape.462.refs_0_), channel_id=1, source_target_pairs={{0,32},{32,0},{1,33},{33,1},{2,34},{34,2},{3,35},{35,3},{4,36},{36... | collective-permute-start | bytes 6635528 | tf_op jit(solution)/shard_map/ppermute | solution.py:46
  74.7 22.2 %all-to-all-start.2 = ((bf16[16,8,2880]{2,1,0:T(8,128)(2,1)}), bf16[16,8,2880]{2,1,0:T(8,128)(2,1)}, u32[]{:S(2)}, u32[]{:S(2)}) async-start(bf16[16,8,2880]{2,1,0:T(8,128)(2,1)} %bitcast.181), calls=%async_computation.2 | async-start | bytes 1507328 | tf_op jit(solution)/shard_map/all_to_all | solution.py:37
  100.6 47.6 %all-to-all-start.3 = ((bf16[8,8,2944]{2,1,0:T(8,128)(2,1)}), bf16[8,8,2944]{2,1,0:T(8,128)(2,1)S(1)}, u32[]{:S(2)}, u32[]{:S(2)}) async-start(bf16[8,8,2944]{2,1,0:T(8,128)(2,1)} %bitcast.196), calls=%async_computation.3 | async-start | bytes 753664 | tf_op jit(solution)/shard_map/all_to_all | solution.py:37
  120.6 27.6 %collective-permute-start.5 = (bf16[2880,384]{1,0:T(8,128)(2,1)}, bf16[2880,384]{1,0:T(8,128)(2,1)}, u32[]{:S(2)}, u32[]{:S(2)}) collective-permute-start(bf16[2880,384]{1,0:T(8,128)(2,1)} %collective-permute-done.3.refs_1_), channel_id=1, source_target_pairs={{0,16},{16,0},{1,17},{17,1},{2,18},{18,2},{3,19},{19,3},{4,20},{20... | collective-permute-start | bytes 6635528 | tf_op jit(solution)/shard_map/ppermute | solution.py:46
  155.5 25.5 %all-to-all-start.4 = ((bf16[8,4,2944]{2,1,0:T(4,128)(2,1)}), bf16[8,4,2944]{2,1,0:T(4,128)(2,1)S(1)}, u32[]{:S(2)}, u32[]{:S(2)}) async-start(bf16[8,4,2944]{2,1,0:T(4,128)(2,1)} %reshape.463), calls=%async_computation.4 | async-start | bytes 376832 | tf_op jit(solution)/shard_map/all_to_all | solution.py:37
  190.5 34.8 %copy-start.5 = (bf16[1,128,2880]{1,2,0:T(8,128)(2,1)S(1)}, bf16[1,128,2880]{1,2,0:T(8,128)(2,1)}, u32[]{:S(2)}) copy-start(bf16[1,128,2880]{1,2,0:T(8,128)(2,1)} %param.31) | copy-start | bytes 2211844
  192.2 14.3 %all-to-all-start.5 = ((f32[32,1,128]{2,1,0:T(1,128)}), f32[32,1,128]{2,1,0:T(1,128)}, u32[]{:S(2)}, u32[]{:S(2)}) async-start(f32[32,1,128]{2,1,0:T(1,128)} %broadcast_in_dim.311), calls=%async_computation.5 | async-start | bytes 32768 | tf_op jit(solution)/shard_map/all_to_all | solution.py:37
  209.6 23.1 %all-to-all-start.6 = ((f32[16,1,128]{2,1,0:T(1,128)}), f32[16,1,128]{2,1,0:T(1,128)S(1)}, u32[]{:S(2)}, u32[]{:S(2)}) async-start(f32[16,1,128]{2,1,0:T(1,128)} %broadcast_in_dim.318), calls=%async_computation.6 | async-start | bytes 16384 | tf_op jit(solution)/shard_map/all_to_all | solution.py:37
  222.5 10.7 %collective-permute-start.6 = (bf16[128,512]{1,0:T(8,128)(2,1)S(1)}, bf16[128,512]{1,0:T(8,128)(2,1)S(1)}, u32[]{:S(2)}, u32[]{:S(2)}) collective-permute-start(bf16[128,512]{1,0:T(8,128)(2,1)S(1)} %pad_maximum_fusion.4), channel_id=1, source_target_pairs={{16,0},{32,16},{48,32},{64,48},{80,64},{96,80},{112,96},{128,112},... | collective-permute-start | bytes 393224 | tf_op jit(solution)/shard_map/ppermute | solution.py:52
  (62 other events, 518.3 us)
Sparse Core Ops, SparseCore 0:
  13.4 132.3 all-gather.1

commit v8 on v7

--- a/solution.py
+++ b/solution.py
@@ -353,12 +353,7 @@
         query_late, keys_here, head_sink_logits, visible(row_late, col_late)
     )
     grad_prob, spread = head_spread(probs, values_here, grad_attended)
-    grad_q, grad_k, grad_v = head_grads(
-        probs, grad_prob, spread, query_late, keys_here, grad_attended, token_scale
-    )
-    back, grad_q, grad_k, grad_v, spread = lax.optimization_barrier(
-        (back, grad_q, grad_k, grad_v, spread)
-    )
+    back, grad_prob, spread = lax.optimization_barrier((back, grad_prob, spread))
     dense_sinks = jnp.sum(sink_probs * spread, axis=2).reshape(QUERY_HEADS) * token_scale
     summed = jnp.sum(back.reshape(EW, pairs // EW, CAP, PADDED).astype(F32), axis=1)
     summed = summed.reshape(SLOTS, PADDED)
@@ -400,12 +395,15 @@
     slot_sinks = jnp.sum(sink_slots * slot_spread, axis=2).reshape(QUERY_HEADS)
     sinks = jnp.pad(-(dense_sinks + slot_sinks), (0, 128 - QUERY_HEADS))[None]
     sinks = to_all(sinks, ("core", "dp"))
-    sinks, slot_prob, upstream_rows = lax.optimization_barrier(
-        (jnp.sum(sinks, axis=0), slot_prob, upstream_rows)
+    sinks, slot_prob, grad_prob, upstream_rows = lax.optimization_barrier(
+        (jnp.sum(sinks, axis=0), slot_prob, grad_prob, upstream_rows)
     )
     sinks = to_all(sinks, ("pair", "half"))
     sinks = jnp.sum(sinks, axis=0)
 
+    grad_q, grad_k, grad_v = head_grads(
+        probs, grad_prob, spread, query_late, keys_here, grad_attended, token_scale
+    )
     slot_q, slot_k, slot_v = head_grads(
         probs_slots, slot_prob, slot_spread, query_slots, keys_here, attended_grad_slots, 1.0
     )

time: 242 us -> 268 us (1.11)
  waiting for transfers between devices: 40.1 us -> 58.9 us
  local copies, waits for them, and re-layouts: 24.6 us -> 29.5 us
  matrix products: 31.6 us -> 36.1 us
    all_to_all x7, waiting for transfers between devices: 39.1 us -> 58.8 us  [exchange(): return lax.all_to_all(value, axis, split_axis=0, concat_axis=0, tiled=True)]
    convert_element_type x2 -> x3, local copies, waits for them, and re-layouts: 0.14 us -> 5.15 us  [head_grads(): grad_q.reshape(tokens, QUERY_HEADS * HEAD_SIZE).astype(BF16)]
    all_to_all x7, starting transfers between devices: 66.7 us -> 62.1 us  [exchange(): return lax.all_to_all(value, axis, split_axis=0, concat_axis=0, tiled=True)]
    ppermute x2, starting transfers between devices: 4.79 us -> 7.53 us  [along_seq(): lax.ppermute(value, SEQ, [(i, i + steps) for i in range(first, last)])]
    unnamed x144 -> x150, local copies, waits for them, and re-layouts: 6.89 us -> 7.28 us
  transfers between devices with their start and end apart: 15 -> 15, of which waited for: 6 -> 5; matrix products, arithmetic and copies ran while one was open for 22% -> 19% of each run, Pallas kernels for 3% -> 3%
where the time goes in v8:
time: 268 us; the launch traced here: 267 us
  starting transfers between devices  90.3 us (34%)
  waiting for transfers between devices  58.9 us (22%)
  matrix products  36.1 us (13%)
  local copies, waits for them, and re-layouts  29.5 us (11%)
  other arithmetic  23 us (9%)
  between operations  21.9 us (8%)
  Pallas kernels  6.97 us (3%)
    all_to_all x7, starting transfers between devices, exchange(): return lax.all_to_all(value, axis, split_axis=0, concat_axis=0, tiled=True)  62.1 us
    all_to_all x7, waiting for transfers between devices, exchange(): return lax.all_to_all(value, axis, split_axis=0, concat_axis=0, tiled=True)  58.8 us
    ppermute x5, starting transfers between devices, swap(): return lax.ppermute(value, axis, [(0, 1), (1, 0)])  20.6 us
    dot_general x4, matrix products, dot_last(): return lax.dot_general(a, b, CONTRACT_LAST, preferred_element_type=F32)  12.9 us
    ppermute x2, starting transfers between devices, along_seq(): lax.ppermute(value, SEQ, [(i, i + steps) for i in range(first, last)])  7.53 us
    unnamed x150, local copies, waits for them, and re-layouts  7.28 us
    pallas_call x1, Pallas kernels, experts_step(): pl.pallas_call(experts_kernel, out_shape=jax.ShapeDtypeStruct((count // 2...  6.5 us
    dot_general x2, matrix products, head_spread(): grad_prob = jnp.einsum('baqj,eaj->aqbe', g, v, preferred_element_type=F32)  5.92 us
  transfers between devices with their start and end apart: 15, of which 5 were waited for; matrix products, arithmetic and copies ran while one was open for 19% of the time, Pallas kernels for 3%

profile of v8, /device:TPU:1, one launch (start us, length us, event | category | flops | bytes accessed | tf_op | source)
XLA Modules:
  0.0 266.7 jit_solution(9585363055147847656)
XLA Ops:
  13.9 4.9 %collective-permute-start = (bf16[128,512]{1,0:T(8,128)(2,1)}, bf16[128,512]{1,0:T(8,128)(2,1)S(1)}, u32[]{:S(2)}, u32[]{:S(2)}) collective-permute-start(bf16[128,512]{1,0:T(8,128)(2,1)} %pad_maximum_fusion.1), channel_id=1, source_target_pairs={{0,16},{16,32},{32,48},{48,64},{64,80},{80,96},{96,112},{112,128},... | collective-permute-start | bytes 393224 | tf_op jit(solution)/shard_map/ppermute | solution.py:52
  20.1 5.1 %collective-permute-start.1 = (f32[8,128]{1,0:T(8,128)S(1)}, f32[8,128]{1,0:T(8,128)S(1)}, u32[]{:S(2)}, u32[]{:S(2)}) collective-permute-start(f32[8,128]{1,0:T(8,128)S(1)} %broadcast_in_dim.284), channel_id=1, source_target_pairs={{0,16},{16,0},{1,17},{17,1},{2,18},{18,2},{3,19},{19,3},{4,20},{20... | collective-permute-start | bytes 12296 | tf_op jit(solution)/shard_map/ppermute | solution.py:46
  25.2 3.7 %all-to-all-start = ((bf16[16,180,384]{2,1,0:T(8,128)(2,1)}), bf16[16,180,384]{2,1,0:T(8,128)(2,1)S(1)}, u32[]{:S(2)}, u32[]{:S(2)}) async-start(bf16[16,180,384]{2,1,0:T(8,128)(2,1)} %broadcast_in_dim.278), calls=%async_computation | async-start | bytes 4521984 | tf_op jit(solution)/shard_map/all_to_all | solution.py:37
  30.1 3.4 %collective-permute-start.2 = (f32[8,128]{1,0:T(8,128)S(1)}, f32[8,128]{1,0:T(8,128)S(1)}, u32[]{:S(2)}, u32[]{:S(2)}) collective-permute-start(f32[8,128]{1,0:T(8,128)S(1)} %broadcast_add_fusion), channel_id=1, source_target_pairs={{0,32},{32,0},{1,33},{33,1},{2,34},{34,2},{3,35},{35,3},{4,36},{36... | collective-permute-start | bytes 12296 | tf_op jit(solution)/shard_map/ppermute | solution.py:46
  42.3 23.9 %all-to-all-done = bf16[16,180,384]{2,1,0:T(8,128)(2,1)S(1)} async-done(((bf16[16,180,384]{2,1,0:T(8,128)(2,1)}), bf16[16,180,384]{2,1,0:T(8,128)(2,1)S(1)}, u32[]{:S(2)}, u32[]{:S(2)}) %all-to-all-start) | async-done | bytes 2211872 | tf_op jit(solution)/shard_map/all_to_all | solution.py:37
  67.6 4.0 %all-to-all-start.1 = ((bf16[16,16,128]{2,1,0:T(8,128)(2,1)}), bf16[16,16,128]{2,1,0:T(8,128)(2,1)S(1)}, u32[]{:S(2)}, u32[]{:S(2)}) async-start(bf16[16,16,128]{2,1,0:T(8,128)(2,1)} %copy.187), calls=%async_computation.1 | async-start | bytes 131072 | tf_op jit(solution)/shard_map/all_to_all | solution.py:37
  74.2 3.2 %collective-permute-start.3 = (bf16[2880,384]{1,0:T(8,128)(2,1)S(1)}, bf16[2880,384]{1,0:T(8,128)(2,1)}, u32[]{:S(2)}, u32[]{:S(2)}) collective-permute-start(bf16[2880,384]{1,0:T(8,128)(2,1)S(1)} %reshape.462.refs_0_), channel_id=1, source_target_pairs={{0,32},{32,0},{1,33},{33,1},{2,34},{34,2},{3,35},{35,3},{4,36},{36... | collective-permute-start | bytes 6635528 | tf_op jit(solution)/shard_map/ppermute | solution.py:46
  77.4 5.5 %collective-permute-start.4 = (bf16[2880,384]{1,0:T(8,128)(2,1)S(1)}, bf16[2880,384]{1,0:T(8,128)(2,1)}, u32[]{:S(2)}, u32[]{:S(2)}) collective-permute-start(bf16[2880,384]{1,0:T(8,128)(2,1)S(1)} %reshape.462.refs_0_), channel_id=1, source_target_pairs={{0,16},{16,0},{1,17},{17,1},{2,18},{18,2},{3,19},{19,3},{4,20},{20... | collective-permute-start | bytes 6635528 | tf_op jit(solution)/shard_map/ppermute | solution.py:46
  85.5 6.9 %all-to-all-start.2 = ((bf16[16,8,2880]{2,1,0:T(8,128)(2,1)}), bf16[16,8,2880]{2,1,0:T(8,128)(2,1)}, u32[]{:S(2)}, u32[]{:S(2)}) async-start(bf16[16,8,2880]{2,1,0:T(8,128)(2,1)} %bitcast.178), calls=%async_computation.2 | async-start | bytes 1507328 | tf_op jit(solution)/shard_map/all_to_all | solution.py:37
  98.2 13.6 %all-to-all-done.2 = bf16[16,8,2880]{2,1,0:T(8,128)(2,1)} async-done(((bf16[16,8,2880]{2,1,0:T(8,128)(2,1)}), bf16[16,8,2880]{2,1,0:T(8,128)(2,1)}, u32[]{:S(2)}, u32[]{:S(2)}) %all-to-all-start.2) | async-done | bytes 737312 | tf_op jit(solution)/shard_map/all_to_all | solution.py:37
  114.6 14.6 %all-to-all-start.3 = ((bf16[8,8,2944]{2,1,0:T(8,128)(2,1)}), bf16[8,8,2944]{2,1,0:T(8,128)(2,1)S(1)}, u32[]{:S(2)}, u32[]{:S(2)}) async-start(bf16[8,8,2944]{2,1,0:T(8,128)(2,1)} %bitcast.193), calls=%async_computation.3 | async-start | bytes 753664 | tf_op jit(solution)/shard_map/all_to_all | solution.py:37
  131.6 3.4 %collective-permute-start.5 = (bf16[2880,384]{1,0:T(8,128)(2,1)}, bf16[2880,384]{1,0:T(8,128)(2,1)}, u32[]{:S(2)}, u32[]{:S(2)}) collective-permute-start(bf16[2880,384]{1,0:T(8,128)(2,1)} %collective-permute-done.3.refs_1_), channel_id=1, source_target_pairs={{0,16},{16,0},{1,17},{17,1},{2,18},{18,2},{3,19},{19,3},{4,20},{20... | collective-permute-start | bytes 6635528 | tf_op jit(solution)/shard_map/ppermute | solution.py:46
  142.5 8.4 %all-to-all-done.3 = bf16[8,8,2944]{2,1,0:T(8,128)(2,1)S(1)} async-done(((bf16[8,8,2944]{2,1,0:T(8,128)(2,1)}), bf16[8,8,2944]{2,1,0:T(8,128)(2,1)S(1)}, u32[]{:S(2)}, u32[]{:S(2)}) %all-to-all-start.3) | async-done | bytes 376864 | tf_op jit(solution)/shard_map/all_to_all | solution.py:37
  150.9 6.5 %shard_map.192 = bf16[32,2944]{1,0:T(8,128)(2,1)S(1)} custom-call(bf16[64,2944]{1,0:T(8,128)(2,1)S(1)} %bitcast.180, bf16[2880,384]{1,0:T(8,128)(2,1)S(1)} %reshape.462.refs_0_, bf16[2880,384]{1,0:T(8,128)(2,1)} %collective-permute-done.3.refs_1_, bf16[2880,384]{1,0:T(8,128)(2,1)} %collective-permute-done.4.refs_2_, ...), custom_call_target="tpu_custom_call" | custom-call | flops 471859200 | bytes 9601024 | tf_op jit(solution)/shard_map/pallas_call | solution.py:146
  158.2 12.7 %all-to-all-start.4 = ((bf16[8,4,2944]{2,1,0:T(4,128)(2,1)}), bf16[8,4,2944]{2,1,0:T(4,128)(2,1)S(1)}, u32[]{:S(2)}, u32[]{:S(2)}) async-start(bf16[8,4,2944]{2,1,0:T(4,128)(2,1)} %reshape.463), calls=%async_computation.4 | async-start | bytes 376832 | tf_op jit(solution)/shard_map/all_to_all | solution.py:37
  171.5 6.3 %fusion.8 = bf16[128,2048]{1,0:T(8,128)(2,1)S(1)} fusion(bf16[2048,2880]{0,1:T(8,128)(2,1)} %all-gather.2.cloned.1.call-done, bf16[128,2880]{0,1:T(8,128)(2,1)} %bitcast.183, pred[128]{0:T(512)(128)(4,1)S(1)} %convert_compare_fusion, pred[128]{0:T(512)(128)(4,1)} %get-tuple-element.76), kind=kOutput, calls=%fused_computation.18 | convolution fusion | flops 1510842368 | bytes 13058304 | tf_op jit(solution)/shard_map/dot_general | solution.py:33
  180.2 5.7 %multiply_reduce_fusion = (f32[4,8,128]{2,1,0:T(8,128)S(1)}, f32[4,8,128,256]{2,3,1,0:T(8,128)}) fusion(f32[4,8,128]{2,1,0:T(8,128)S(1)} %copy-done.46, f32[4,8,128]{2,1,0:T(8,128)S(1)} %copy-done.34, f32[4,256,128,8]{2,1,3,0:T(8,128)} %copy-done.3, pred[128,256]{0,1:T(8,128)(4,1)S(1)} %and_and_fusion, bf16[256,4,64,1]{0,2,3,1:T(8,128)(2,1)S(1)} %bitcast.197, ...), kind=kOutput, calls=%fused_computation.2 | convolution fusion | flops 141553664 | bytes 9125888 | tf_op jit(solution)/shard_map/baqj,eaj->aqbe/dot_general | solution.py:81
  189.0 6.1 %convolution_convert_fusion.5 = bf16[8,2048]{1,0:T(8,128)(2,1)S(1)} fusion(bf16[8,2880]{1,0:T(8,128)(2,1)S(1)} %fusion.53, bf16[2048,2880]{0,1:T(8,128)(2,1)} %all-gather.2.cloned.1.call-done), kind=kOutput, calls=%fused_computation.23 | convolution fusion | flops 94388224 | bytes 11875328 | tf_op jit(solution)/shard_map/dot_general | solution.py:33
  196.6 8.6 %all-to-all-start.5 = ((f32[32,1,128]{2,1,0:T(1,128)}), f32[32,1,128]{2,1,0:T(1,128)S(1)}, u32[]{:S(2)}, u32[]{:S(2)}) async-start(f32[32,1,128]{2,1,0:T(1,128)} %broadcast_in_dim.311), calls=%async_computation.5 | async-start | bytes 32768 | tf_op jit(solution)/shard_map/all_to_all | solution.py:37
  207.0 5.0 %all-to-all-done.5 = f32[32,1,128]{2,1,0:T(1,128)S(1)} async-done(((f32[32,1,128]{2,1,0:T(1,128)}), f32[32,1,128]{2,1,0:T(1,128)S(1)}, u32[]{:S(2)}, u32[]{:S(2)}) %all-to-all-start.5) | async-done | bytes 16416 | tf_op jit(solution)/shard_map/all_to_all | solution.py:37
  214.5 5.0 %multiply_convert_fusion = bf16[4,8,128,256]{2,3,1,0:T(8,128)(2,1)S(1)} fusion(f32[4,8,128,256]{2,3,1,0:T(8,128)} %get-tuple-element.66, f32[4,8,128]{2,1,0:T(8,128)S(1)} %get-tuple-element.59, f32[4,8,128]{2,1,0:T(8,128)S(1)} %copy-done.47, f32[4,8,128]{2,1,0:T(8,128)S(1)} %copy-done.34, f32[4,256,128,8]{2,1,3,0:T(8,128)} %copy-done.3, ...), kind=kLoop, calls=%fused_computation.1 | loop fusion | flops 8388608 | bytes 10567680 | tf_op jit(solution)/shard_map/convert_element_type | solution.py:91
  229.4 2.6 collective-permute-start.6
  235.7 11.6 %all-to-all-start.6 = ((f32[16,1,128]{2,1,0:T(1,128)}), f32[16,1,128]{2,1,0:T(1,128)S(1)}, u32[]{:S(2)}, u32[]{:S(2)}) async-start(f32[16,1,128]{2,1,0:T(1,128)} %broadcast_in_dim.318), calls=%async_computation.6 | async-start | bytes 16384 | tf_op jit(solution)/shard_map/all_to_all | solution.py:37
  250.7 8.0 %all-to-all-done.6 = f32[16,1,128]{2,1,0:T(1,128)S(1)} async-done(((f32[16,1,128]{2,1,0:T(1,128)}), f32[16,1,128]{2,1,0:T(1,128)S(1)}, u32[]{:S(2)}, u32[]{:S(2)}) %all-to-all-start.6) | async-done | bytes 8224 | tf_op jit(solution)/shard_map/all_to_all | solution.py:37
  (297 shorter events, 66.2 us)
Async XLA Ops:
  7.2 78.3 %copy-start = (bf16[1,128,2880]{1,2,0:T(8,128)(2,1)S(1)}, bf16[1,128,2880]{1,2,0:T(8,128)(2,1)}, u32[]{:S(2)}) copy-start(bf16[1,128,2880]{1,2,0:T(8,128)(2,1)} %param.20) | copy-start | bytes 2211844
  7.2 164.3 %all-gather.2.cloned.1.call-start = ((), (), s32[]{:S(2)}) async-start(), calls=%async_computation.7 | async-start | bytes 12533760 | tf_op jit(solution)/shard_map/all_gather | solution.py:247
  13.9 25.3 %collective-permute-start = (bf16[128,512]{1,0:T(8,128)(2,1)}, bf16[128,512]{1,0:T(8,128)(2,1)S(1)}, u32[]{:S(2)}, u32[]{:S(2)}) collective-permute-start(bf16[128,512]{1,0:T(8,128)(2,1)} %pad_maximum_fusion.1), channel_id=1, source_target_pairs={{0,16},{16,32},{32,48},{48,64},{64,80},{80,96},{96,112},{112,128},... | collective-permute-start | bytes 393224 | tf_op jit(solution)/shard_map/ppermute | solution.py:52
  20.1 9.3 %collective-permute-start.1 = (f32[8,128]{1,0:T(8,128)S(1)}, f32[8,128]{1,0:T(8,128)S(1)}, u32[]{:S(2)}, u32[]{:S(2)}) collective-permute-start(f32[8,128]{1,0:T(8,128)S(1)} %broadcast_in_dim.284), channel_id=1, source_target_pairs={{0,16},{16,0},{1,17},{17,1},{2,18},{18,2},{3,19},{19,3},{4,20},{20... | collective-permute-start | bytes 12296 | tf_op jit(solution)/shard_map/ppermute | solution.py:46
  25.2 40.9 %all-to-all-start = ((bf16[16,180,384]{2,1,0:T(8,128)(2,1)}), bf16[16,180,384]{2,1,0:T(8,128)(2,1)S(1)}, u32[]{:S(2)}, u32[]{:S(2)}) async-start(bf16[16,180,384]{2,1,0:T(8,128)(2,1)} %broadcast_in_dim.278), calls=%async_computation | async-start | bytes 4521984 | tf_op jit(solution)/shard_map/all_to_all | solution.py:37
  30.1 6.8 %collective-permute-start.2 = (f32[8,128]{1,0:T(8,128)S(1)}, f32[8,128]{1,0:T(8,128)S(1)}, u32[]{:S(2)}, u32[]{:S(2)}) collective-permute-start(f32[8,128]{1,0:T(8,128)S(1)} %broadcast_add_fusion), channel_id=1, source_target_pairs={{0,32},{32,0},{1,33},{33,1},{2,34},{34,2},{3,35},{35,3},{4,36},{36... | collective-permute-start | bytes 12296 | tf_op jit(solution)/shard_map/ppermute | solution.py:46
  34.2 50.4 %copy-start.25 = (bf16[8,4,8,64]{3,2,1,0:T(8,128)(2,1)}, bf16[8,4,8,64]{3,2,1,0:T(8,128)(2,1)S(1)}, u32[]{:S(2)}) copy-start(bf16[8,4,8,64]{3,2,1,0:T(8,128)(2,1)S(1)} %reshape.455) | copy-start | bytes 98308
  39.3 98.7 %copy-start.11 = (bf16[256,256]{0,1:T(8,128)(2,1)}, bf16[256,256]{0,1:T(8,128)(2,1)S(1)}, u32[]{:S(2)}) copy-start(bf16[256,256]{0,1:T(8,128)(2,1)S(1)} %copy.183) | copy-start | bytes 393220
  39.4 46.0 %copy-start.21 = (bf16[256,256]{0,1:T(8,128)(2,1)}, bf16[256,256]{0,1:T(8,128)(2,1)S(1)}, u32[]{:S(2)}) copy-start(bf16[256,256]{0,1:T(8,128)(2,1)S(1)} %copy.182) | copy-start | bytes 393220
  42.2 54.5 %copy-start.43 = (bf16[8,128]{1,0:T(8,128)(2,1)S(1)}, bf16[8,128]{1,0:T(8,128)(2,1)}, u32[]{:S(2)}) copy-start(bf16[8,128]{1,0:T(8,128)(2,1)} %get-tuple-element.48) | copy-start | bytes 6148
  67.6 15.3 %all-to-all-start.1 = ((bf16[16,16,128]{2,1,0:T(8,128)(2,1)}), bf16[16,16,128]{2,1,0:T(8,128)(2,1)S(1)}, u32[]{:S(2)}, u32[]{:S(2)}) async-start(bf16[16,16,128]{2,1,0:T(8,128)(2,1)} %copy.187), calls=%async_computation.1 | async-start | bytes 131072 | tf_op jit(solution)/shard_map/all_to_all | solution.py:37
  71.7 41.8 %copy-start.48 = (f32[2880]{0:T(1024)S(1)}, f32[2880]{0:T(1024)}, u32[]{:S(2)}) copy-start(f32[2880]{0:T(1024)} %param.22) | copy-start | bytes 34564
  71.7 41.9 %copy-start.73 = (s32[16]{0:T(128)S(1)}, s32[16]{0:T(128)}, u32[]{:S(2)}) copy-start(s32[16]{0:T(128)} %fusion.83) | copy-start | bytes 196
  74.2 55.7 %copy-start.60 = (s32[1,128,4]{1,2,0:T(4,128)S(1)}, s32[1,128,4]{1,2,0:T(4,128)}, u32[]{:S(2)}) copy-start(s32[1,128,4]{1,2,0:T(4,128)} %param.27) | copy-start | bytes 6148
  74.2 57.3 %collective-permute-start.3 = (bf16[2880,384]{1,0:T(8,128)(2,1)S(1)}, bf16[2880,384]{1,0:T(8,128)(2,1)}, u32[]{:S(2)}, u32[]{:S(2)}) collective-permute-start(bf16[2880,384]{1,0:T(8,128)(2,1)S(1)} %reshape.462.refs_0_), channel_id=1, source_target_pairs={{0,32},{32,0},{1,33},{33,1},{2,34},{34,2},{3,35},{35,3},{4,36},{36... | collective-permute-start | bytes 6635528 | tf_op jit(solution)/shard_map/ppermute | solution.py:46
  77.4 73.5 %collective-permute-start.4 = (bf16[2880,384]{1,0:T(8,128)(2,1)S(1)}, bf16[2880,384]{1,0:T(8,128)(2,1)}, u32[]{:S(2)}, u32[]{:S(2)}) collective-permute-start(bf16[2880,384]{1,0:T(8,128)(2,1)S(1)} %reshape.462.refs_0_), channel_id=1, source_target_pairs={{0,16},{16,0},{1,17},{17,1},{2,18},{18,2},{3,19},{19,3},{4,20},{20... | collective-permute-start | bytes 6635528 | tf_op jit(solution)/shard_map/ppermute | solution.py:46
  85.5 26.2 %all-to-all-start.2 = ((bf16[16,8,2880]{2,1,0:T(8,128)(2,1)}), bf16[16,8,2880]{2,1,0:T(8,128)(2,1)}, u32[]{:S(2)}, u32[]{:S(2)}) async-start(bf16[16,8,2880]{2,1,0:T(8,128)(2,1)} %bitcast.178), calls=%async_computation.2 | async-start | bytes 1507328 | tf_op jit(solution)/shard_map/all_to_all | solution.py:37
  114.6 36.3 %all-to-all-start.3 = ((bf16[8,8,2944]{2,1,0:T(8,128)(2,1)}), bf16[8,8,2944]{2,1,0:T(8,128)(2,1)S(1)}, u32[]{:S(2)}, u32[]{:S(2)}) async-start(bf16[8,8,2944]{2,1,0:T(8,128)(2,1)} %bitcast.193), calls=%async_computation.3 | async-start | bytes 753664 | tf_op jit(solution)/shard_map/all_to_all | solution.py:37
  131.6 19.3 %collective-permute-start.5 = (bf16[2880,384]{1,0:T(8,128)(2,1)}, bf16[2880,384]{1,0:T(8,128)(2,1)}, u32[]{:S(2)}, u32[]{:S(2)}) collective-permute-start(bf16[2880,384]{1,0:T(8,128)(2,1)} %collective-permute-done.3.refs_1_), channel_id=1, source_target_pairs={{0,16},{16,0},{1,17},{17,1},{2,18},{18,2},{3,19},{19,3},{4,20},{20... | collective-permute-start | bytes 6635528 | tf_op jit(solution)/shard_map/ppermute | solution.py:46
  137.4 48.5 %copy-start.18 = (pred[128,256]{0,1:T(8,128)(4,1)}, pred[128,256]{0,1:T(8,128)(4,1)S(1)}, u32[]{:S(2)}) copy-start(pred[128,256]{0,1:T(8,128)(4,1)S(1)} %and_and_fusion) | copy-start | bytes 98308
  158.2 29.1 %all-to-all-start.4 = ((bf16[8,4,2944]{2,1,0:T(4,128)(2,1)}), bf16[8,4,2944]{2,1,0:T(4,128)(2,1)S(1)}, u32[]{:S(2)}, u32[]{:S(2)}) async-start(bf16[8,4,2944]{2,1,0:T(4,128)(2,1)} %reshape.463), calls=%async_computation.4 | async-start | bytes 376832 | tf_op jit(solution)/shard_map/all_to_all | solution.py:37
  196.6 15.4 %all-to-all-start.5 = ((f32[32,1,128]{2,1,0:T(1,128)}), f32[32,1,128]{2,1,0:T(1,128)S(1)}, u32[]{:S(2)}, u32[]{:S(2)}) async-start(f32[32,1,128]{2,1,0:T(1,128)} %broadcast_in_dim.311), calls=%async_computation.5 | async-start | bytes 32768 | tf_op jit(solution)/shard_map/all_to_all | solution.py:37
  229.4 29.8 %collective-permute-start.6 = (bf16[128,512]{1,0:T(8,128)(2,1)S(1)}, bf16[128,512]{1,0:T(8,128)(2,1)S(1)}, u32[]{:S(2)}, u32[]{:S(2)}) collective-permute-start(bf16[128,512]{1,0:T(8,128)(2,1)S(1)} %pad_maximum_fusion.4), channel_id=1, source_target_pairs={{16,0},{32,16},{48,32},{64,48},{80,64},{96,80},{112,96},{128,112},... | collective-permute-start | bytes 393224 | tf_op jit(solution)/shard_map/ppermute | solution.py:52
  235.7 22.9 %all-to-all-start.6 = ((f32[16,1,128]{2,1,0:T(1,128)}), f32[16,1,128]{2,1,0:T(1,128)S(1)}, u32[]{:S(2)}, u32[]{:S(2)}) async-start(f32[16,1,128]{2,1,0:T(1,128)} %broadcast_in_dim.318), calls=%async_computation.6 | async-start | bytes 16384 | tf_op jit(solution)/shard_map/all_to_all | solution.py:37
  (65 other events, 580.9 us)
Sparse Core Ops, SparseCore 0:
  13.4 139.8 all-gather.1
